TPU v7x, 32 devices: a whole 2x2x4 slice. The times are simulated.
32 devices in a mesh: batch: 16 (over z, y, core), head: 2 (over x).
Axes of the slice: x: 2, y: 2, z: 4, core: 2. Of those that a mesh axis runs over, the one named last changes fastest.
Arguments:
- layer_in: bfloat16 [16384, 1024], P('batch'), may hold values from -6 to 6
- slot_stretch: int32 [32], replicated, may hold values from 0 to 31, each once
- seq_stretches: int32 [8], replicated, may hold values from 1 to 6, 32 in all
- w_qkv: bfloat16 [1024, 3, 1024], P(None, None, 'head'), may hold values from -0.1875 to 0.1875
- qv_bias: bfloat16 [2, 1024], P(None, 'head'), may hold values from -0.29882812 to 0.29882812
- w_out: bfloat16 [1024, 1024], P('head'), may hold values from -3 to 3
- out_bias: bfloat16 [1024], replicated, may hold values from -3 to 3
- norm1_gain: bfloat16 [1024], replicated, may hold values from 0.099609375 to 1.8984375
- norm1_shift: bfloat16 [1024], replicated, may hold values from -2 to 2
- w_up: bfloat16 [1024, 4096], P(None, 'head'), may hold values from -0.1875 to 0.1875
- up_bias: bfloat16 [4096], P('head'), may hold values from -3 to 3
- w_down: bfloat16 [4096, 1024], P('head'), may hold values from -0.09375 to 0.09375
- down_bias: bfloat16 [1024], replicated, may hold values from -3 to 3
- norm2_gain: bfloat16 [1024], replicated, may hold values from 0.099609375 to 1.8984375
- norm2_shift: bfloat16 [1024], replicated, may hold values from -2 to 2
- cotangent: bfloat16 [16384, 1024], P('batch'), may hold values from -6 to 6
Outputs:
- layer_out: bfloat16 [16384, 1024], P('batch')
- grad_in: float32 [16384, 1024], P('batch', 'head')
- grad_w_qkv: float32 [1024, 3, 1024], P(None, None, 'head')
- grad_qv_bias: float32 [2, 1024], P(None, 'head')
- grad_w_out: float32 [1024, 1024], P('head')
- grad_out_bias: float32 [1024], replicated
- grad_norm1_gain: float32 [1024], replicated
- grad_norm1_shift: float32 [1024], replicated
- grad_w_up: float32 [1024, 4096], P(None, 'head')
- grad_up_bias: float32 [4096], P('head')
- grad_w_down: float32 [4096, 1024], P('head')
- grad_down_bias: float32 [1024], replicated
- grad_norm2_gain: float32 [1024], replicated
- grad_norm2_shift: float32 [1024], replicated
Inputs may be any that keep to these rules, and one draw needn't show every extreme that they name: `seq_stretches`: lengths in stretches of 512 tokens, in the order in which stretches are numbered; they sum to 32 and the largest is exactly 6. Slot s, rows s * 512 to s * 512 + 511, holds stretch slot_stretch[s]; every stretch is in exactly one slot.
All inputs are finite; a program needn't handle non-finite values.
Results may differ from a plain program's by a relative error of at most 0.02.
Values may be sent and summed in bfloat16 or wider, within the bound.
No kernel may reach another device: no remote copies, remote signals or barrier semaphores. Data moves between devices by JAX's collectives and lax.ppermute only.
A program may use at most 320 MiB of HBM per device.

v0:
```python
import jax
import jax.numpy as jnp
from jax import lax
from jax.sharding import PartitionSpec as P

HD = 64
CH = 512


EPSILON = 1e-05


def norm_forward(values, gain_vec, shift_vec):
    centre = jnp.mean(values, axis=-1, keepdims=True)
    centred = values - centre
    spread = jnp.mean(centred * centred, axis=-1, keepdims=True)
    inv_std = lax.rsqrt(spread + EPSILON)
    normed = centred * inv_std
    return (normed * gain_vec + shift_vec, normed, inv_std)


def norm_backward(gradient, normed, inv_std, gain_vec):
    scaled = gradient * gain_vec
    mean_one = jnp.mean(scaled, axis=-1, keepdims=True)
    mean_two = jnp.mean(scaled * normed, axis=-1, keepdims=True)
    back_grad = inv_std * (scaled - mean_one - normed * mean_two)
    return (back_grad, jnp.sum(gradient * normed, axis=0), jnp.sum(gradient, axis=0))


def gelu_exact(values):
    return jax.nn.gelu(values, approximate=False)


def lookup(table_vec, index_vec):
    table_width = table_vec.shape[0]
    is_match = index_vec[:, None] == jnp.arange(table_width, dtype=jnp.int32)[None, :]
    return jnp.sum(jnp.where(is_match, table_vec[None, :], 0), axis=1)


def pick_one(table_vec, position):
    return lax.dynamic_index_in_dim(table_vec, position, 0, keepdims=False)


def split_heads(block, head_count):
    return block.reshape(block.shape[0], head_count, HD)


def head_scores(query_block, key_block, head_count):
    return jnp.einsum(
        "qhd,khd->hqk",
        split_heads(query_block, head_count),
        split_heads(key_block, head_count),
        preferred_element_type=jnp.float32,
    ) * HD ** (-0.5)


def score_grads(
    query_block, key_block, value_block, grad_block, log_total, delta_block, head_count
):
    weights = jnp.exp(head_scores(query_block, key_block, head_count) - log_total[..., None])
    grad_weights = jnp.einsum(
        "qhd,khd->hqk",
        split_heads(grad_block, head_count),
        split_heads(value_block, head_count),
        preferred_element_type=jnp.float32,
    )
    grad_score = (weights * (grad_weights - delta_block[..., None])).astype(jnp.bfloat16)
    return (weights.astype(jnp.bfloat16), grad_score)


def stretch_tables(slot_stretch, seq_stretches):
    stretch_count = slot_stretch.shape[0]
    seq_ends = jnp.cumsum(seq_stretches)
    seq_starts = seq_ends - seq_stretches
    stretch_index = jnp.arange(stretch_count, dtype=jnp.int32)
    seq_of = jnp.sum((stretch_index[:, None] >= seq_ends[None, :]).astype(jnp.int32), axis=1)
    first_stretch = lookup(seq_starts, seq_of)
    stretch_span = lookup(seq_stretches, seq_of)
    is_match = slot_stretch[None, :] == stretch_index[:, None]
    stretch_slot = jnp.sum(jnp.where(is_match, stretch_index[None, :], 0), axis=1)
    return (first_stretch, stretch_span, stretch_slot)


def local(
    layer_in,
    slot_stretch,
    seq_stretches,
    w_qkv,
    qv_bias,
    w_out,
    out_bias,
    norm1_gain,
    norm1_shift,
    w_up,
    up_bias,
    w_down,
    down_bias,
    norm2_gain,
    norm2_shift,
    cotangent,
):
    tok_rows = layer_in.shape[0]
    model_width = layer_in.shape[1]
    slot_count = tok_rows // CH
    col_count = w_qkv.shape[2]
    head_count = col_count // HD
    score_scale = HD ** (-0.5)
    first_stretch, stretch_span, stretch_slot = stretch_tables(slot_stretch, seq_stretches)
    group_index = lax.axis_index("batch")
    local_stretches = lax.dynamic_slice_in_dim(slot_stretch, group_index * slot_count, slot_count)
    local_first = lookup(first_stretch, local_stretches)
    local_span = lookup(stretch_span, local_stretches)
    proj_weight = w_qkv.reshape(model_width, 3 * col_count)
    projected = jnp.dot(layer_in, proj_weight, preferred_element_type=jnp.float32)
    queries = (projected[:, :col_count] + qv_bias[0]).astype(jnp.bfloat16)
    key_rows = projected[:, col_count : 2 * col_count].astype(jnp.bfloat16)
    value_rows = (projected[:, 2 * col_count :] + qv_bias[1]).astype(jnp.bfloat16)
    query_slots = queries.reshape(slot_count, CH, col_count)
    own_keys = key_rows.reshape(slot_count, CH, col_count)
    own_values = value_rows.reshape(slot_count, CH, col_count)
    key_all, value_all = (
        lax.all_gather(own_keys, "batch", axis=0, tiled=True),
        lax.all_gather(own_values, "batch", axis=0, tiled=True),
    )

    def attend(inputs):
        query_block, begin_stretch, length = inputs

        def norm_step(offset, running):
            row_max, row_total = running
            key_slot = pick_one(stretch_slot, begin_stretch + offset)
            score_block = head_scores(query_block, pick_one(key_all, key_slot), head_count)
            new_max = jnp.maximum(row_max, jnp.max(score_block, axis=-1))
            row_total = row_total * jnp.exp(row_max - new_max) + jnp.sum(
                jnp.exp(score_block - new_max[..., None]), axis=-1
            )
            return (new_max, row_total)

        initial = (
            jnp.full((head_count, CH), -1e30, jnp.float32),
            jnp.zeros((head_count, CH), jnp.float32),
        )
        row_max, row_total = lax.fori_loop(0, length, norm_step, initial)
        log_total = row_max + jnp.log(row_total)

        def value_step(offset, summed):
            key_slot = pick_one(stretch_slot, begin_stretch + offset)
            score_block = head_scores(query_block, pick_one(key_all, key_slot), head_count)
            weights = jnp.exp(score_block - log_total[..., None]).astype(jnp.bfloat16)
            value_heads = split_heads(pick_one(value_all, key_slot), head_count)
            return summed + jnp.einsum(
                "hqk,khd->qhd", weights, value_heads, preferred_element_type=jnp.float32
            )

        summed = lax.fori_loop(0, length, value_step, jnp.zeros((CH, head_count, HD), jnp.float32))
        return (summed.reshape(CH, col_count), log_total)

    context, log_totals = lax.map(attend, (query_slots, local_first, local_span))
    context = context.reshape(tok_rows, col_count)
    context_low = context.astype(jnp.bfloat16)
    attn_part = jnp.dot(context_low, w_out, preferred_element_type=jnp.float32)
    hidden = (
        layer_in.astype(jnp.float32)
        + lax.psum(attn_part.astype(jnp.bfloat16), "head").astype(jnp.float32)
        + out_bias
    )
    first_norm, normed_one, inv_one = norm_forward(hidden, norm1_gain, norm1_shift)
    first_low = first_norm.astype(jnp.bfloat16)
    pre_act = jnp.dot(first_low, w_up, preferred_element_type=jnp.float32) + up_bias
    activation, gelu_back = jax.vjp(gelu_exact, pre_act)
    act_low = activation.astype(jnp.bfloat16)
    down_part = jnp.dot(act_low, w_down, preferred_element_type=jnp.float32)
    second_in = (
        first_norm
        + lax.psum(down_part.astype(jnp.bfloat16), "head").astype(jnp.float32)
        + down_bias
    )
    normed_out, normed_two, inv_two = norm_forward(second_in, norm2_gain, norm2_shift)
    grad_second, grad_gain_two, grad_shift_two = norm_backward(
        cotangent.astype(jnp.float32), normed_two, inv_two, norm2_gain
    )
    layer_out = normed_out.astype(jnp.bfloat16)
    second_low = grad_second.astype(jnp.bfloat16)
    grad_down = jnp.einsum("tf,td->fd", act_low, second_low, preferred_element_type=jnp.float32)
    grad_down_bias = jnp.sum(grad_second, axis=0)
    grad_act = jnp.einsum("td,fd->tf", second_low, w_down, preferred_element_type=jnp.float32)
    grad_pre_low = gelu_back(grad_act)[0].astype(jnp.bfloat16)
    grad_up = jnp.einsum("td,tf->df", first_low, grad_pre_low, preferred_element_type=jnp.float32)
    grad_up_bias = jnp.sum(grad_pre_low.astype(jnp.float32), axis=0)
    ffn_back = jnp.einsum("tf,df->td", grad_pre_low, w_up, preferred_element_type=jnp.float32)
    grad_first = lax.psum(ffn_back.astype(jnp.bfloat16), "head").astype(jnp.float32) + grad_second
    grad_hidden, grad_gain_one, grad_shift_one = norm_backward(
        grad_first, normed_one, inv_one, norm1_gain
    )
    grad_out_bias = jnp.sum(grad_hidden, axis=0)
    hidden_low = grad_hidden.astype(jnp.bfloat16)
    grad_out = jnp.einsum("tc,td->cd", context_low, hidden_low, preferred_element_type=jnp.float32)
    grad_context = jnp.einsum(
        "td,cd->tc", hidden_low, w_out, preferred_element_type=jnp.float32
    ).astype(jnp.bfloat16)
    delta_rows = jnp.sum(
        (grad_context.astype(jnp.float32) * context).reshape(tok_rows, head_count, HD), axis=-1
    )
    delta_slots = jnp.swapaxes(delta_rows.reshape(slot_count, CH, head_count), 1, 2)
    grad_slots = grad_context.reshape(slot_count, CH, col_count)

    def back_slot(key_total, inputs):
        query_block, grad_block, log_total, delta_block, begin_stretch, length = inputs

        def key_step(offset, running):
            grad_query, key_sum = running
            key_slot = pick_one(stretch_slot, begin_stretch + offset)
            key_block = pick_one(key_all, key_slot)
            value_block = pick_one(value_all, key_slot)
            weights_low, grad_score = score_grads(
                query_block, key_block, value_block, grad_block, log_total, delta_block, head_count
            )
            grad_query = (
                grad_query
                + jnp.einsum(
                    "hqk,khd->qhd",
                    grad_score,
                    split_heads(key_block, head_count),
                    preferred_element_type=jnp.float32,
                )
                * score_scale
            )
            grad_key = (
                jnp.einsum(
                    "hqk,qhd->khd",
                    grad_score,
                    split_heads(query_block, head_count),
                    preferred_element_type=jnp.float32,
                )
                * score_scale
            )
            grad_value = jnp.einsum(
                "hqk,qhd->khd",
                weights_low,
                split_heads(grad_block, head_count),
                preferred_element_type=jnp.float32,
            )
            update = jnp.concatenate(
                [grad_key.reshape(CH, col_count), grad_value.reshape(CH, col_count)], axis=1
            )
            key_sum = lax.dynamic_update_index_in_dim(
                key_sum, pick_one(key_sum, key_slot) + update, key_slot, 0
            )
            return (grad_query, key_sum)

        start_state = (jnp.zeros((CH, head_count, HD), jnp.float32), key_total)
        grad_query, key_total = lax.fori_loop(0, length, key_step, start_state)
        return (key_total, grad_query.reshape(CH, col_count))

    key_start = jnp.zeros((key_all.shape[0], CH, 2 * col_count), jnp.float32)
    key_total, grad_query_slots = lax.scan(
        back_slot,
        key_start,
        (query_slots, grad_slots, log_totals, delta_slots, local_first, local_span),
    )
    key_grads = lax.psum_scatter(
        key_total.astype(jnp.bfloat16), "batch", scatter_dimension=0, tiled=True
    ).astype(jnp.float32)
    grad_keys = key_grads[:, :, :col_count].astype(jnp.bfloat16)
    grad_values = key_grads[:, :, col_count:].astype(jnp.bfloat16)
    grad_queries = grad_query_slots.reshape(tok_rows, col_count).astype(jnp.bfloat16)
    grad_keys = grad_keys.reshape(tok_rows, col_count)
    grad_values = grad_values.reshape(tok_rows, col_count)
    grad_proj = jnp.concatenate([grad_queries, grad_keys, grad_values], axis=1)
    grad_qkv = jnp.einsum(
        "td,tc->dc", layer_in, grad_proj, preferred_element_type=jnp.float32
    ).reshape(model_width, 3, col_count)
    grad_qv = jnp.stack(
        [
            jnp.sum(grad_queries.astype(jnp.float32), axis=0),
            jnp.sum(grad_values.astype(jnp.float32), axis=0),
        ]
    )
    input_part = jnp.einsum("tc,dc->td", grad_proj, proj_weight, preferred_element_type=jnp.float32)
    own_width = model_width // lax.axis_size("head")
    own_grad = lax.dynamic_slice_in_dim(
        grad_hidden, lax.axis_index("head") * own_width, own_width, 1
    )
    grad_in = (
        lax.psum_scatter(
            input_part.astype(jnp.bfloat16), "head", scatter_dimension=1, tiled=True
        ).astype(jnp.float32)
        + own_grad
    )
    totals = (
        lax.psum(grad_qkv.astype(jnp.bfloat16), "batch").astype(jnp.float32),
        lax.psum(grad_qv.astype(jnp.bfloat16), "batch").astype(jnp.float32),
        lax.psum(grad_out.astype(jnp.bfloat16), "batch").astype(jnp.float32),
        lax.psum(grad_out_bias.astype(jnp.bfloat16), "batch").astype(jnp.float32),
        lax.psum(grad_gain_one.astype(jnp.bfloat16), "batch").astype(jnp.float32),
        lax.psum(grad_shift_one.astype(jnp.bfloat16), "batch").astype(jnp.float32),
        lax.psum(grad_up.astype(jnp.bfloat16), "batch").astype(jnp.float32),
        lax.psum(grad_up_bias.astype(jnp.bfloat16), "batch").astype(jnp.float32),
        lax.psum(grad_down.astype(jnp.bfloat16), "batch").astype(jnp.float32),
        lax.psum(grad_down_bias.astype(jnp.bfloat16), "batch").astype(jnp.float32),
        lax.psum(grad_gain_two.astype(jnp.bfloat16), "batch").astype(jnp.float32),
        lax.psum(grad_shift_two.astype(jnp.bfloat16), "batch").astype(jnp.float32),
    )
    return (
        layer_out,
        grad_in,
        totals[0],
        totals[1],
        totals[2],
        totals[3],
        totals[4],
        totals[5],
        totals[6],
        totals[7],
        totals[8],
        totals[9],
        totals[10],
        totals[11],
    )


def solution(mesh):
    in_specs = (
        P("batch", None),
        P(),
        P(),
        P(None, None, "head"),
        P(None, "head"),
        P("head", None),
        P(),
        P(),
        P(),
        P(None, "head"),
        P("head"),
        P("head", None),
        P(),
        P(),
        P(),
        P("batch", None),
    )
    out_specs = (
        P("batch", None),
        P("batch", "head"),
        P(None, None, "head"),
        P(None, "head"),
        P("head", None),
        P(),
        P(),
        P(),
        P(None, "head"),
        P("head"),
        P("head", None),
        P(),
        P(),
        P(),
    )
    return jax.shard_map(local, mesh=mesh, in_specs=in_specs, out_specs=out_specs, check_vma=False)
```

profile of v0, /device:TPU:0, one launch (start us, length us, event | category | flops | bytes accessed | tf_op | source)
XLA Modules:
  0.0 1713.6 jit_solution(12479954061696862332)
XLA Ops:
  7.3 4.8 copy.63
  12.0 5.3 fusion.54
  27.4 123.5 %all-gather.3.cloned.1.call-done = bf16[32,512,512]{2,1,0:T(8,128)(2,1)} async-done(((bf16[2,512,512]{2,1,0:T(8,128)(2,1)}), bf16[32,512,512]{2,1,0:T(8,128)(2,1)}) %all-gather.3.cloned.1.call-update) | async-done | bytes 16777232 | tf_op jit(solution)/shard_map/all_gather | solution.py:122
  151.0 22.5 %copy.65 = bf16[32,512,512]{1,2,0:T(8,128)(2,1)} copy(bf16[32,512,512]{2,1,0:T(8,128)(2,1)} %all-gather.3.cloned.1.call-done) | data formatting | bytes 33554432 | tf_op jit(solution)/shard_map/while | solution.py:158
  173.5 105.3 %all-gather.5.cloned.1.call-done = bf16[32,512,512]{2,1,0:T(8,128)(2,1)} async-done(((bf16[2,512,512]{2,1,0:T(8,128)(2,1)}), bf16[32,512,512]{2,1,0:T(8,128)(2,1)}) %all-gather.5.cloned.1.call-update) | async-done | bytes 16777232 | tf_op jit(solution)/shard_map/all_gather | solution.py:123
  278.8 22.5 %copy.66 = bf16[32,512,512]{1,2,0:T(8,128)(2,1)} copy(bf16[32,512,512]{2,1,0:T(8,128)(2,1)} %all-gather.5.cloned.1.call-done) | data formatting | bytes 33554432 | tf_op jit(solution)/shard_map/while | solution.py:158
  301.4 152.5 %while.68 = (s32[]{:T(128)}, f32[2,512,512]{2,1,0:T(8,128)}, f32[2,8,512]{2,1,0:T(8,128)S(1)}, s32[2]{0:T(128)S(1)}, s32[2]{0:T(128)S(1)}, /*index=5*/bf16[2,512...) while((s32[]{:T(128)}, f32[2,512,512]{2,1,0:T(8,128)}, ...), condition=%wide.region_14.15_spmd.clone, body=%wide.region_7.14_spmd.sunk.clone | while | flops 822358016 | bytes 31261492 | solution.py:158
  303.6 31.4 %while.66 = (s32[]{:T(128)}, f32[8,512]{1,0:T(8,128)S(1)}, f32[8,512]{1,0:T(8,128)S(1)}, s32[]{:T(128)}, s32[]{:T(128)}, /*index=5*/s32[32]{0:T(128)S(1)}, bf16[...) while((s32[]{:T(128)}, f32[8,512]{1,0:T(8,128)S(1)}, ...), condition=%wide.region_11.11_spmd, body=%wide.region_8.10_spmd.sunk | while | flops 278929408 | bytes 19087572 | solution.py:143
  336.1 38.9 %while.67 = (s32[]{:T(128)}, f32[512,8,64]{0,2,1:T(8,128)}, s32[]{:T(128)}, s32[]{:T(128)}, s32[32]{0:T(128)S(1)}, /*index=5*/bf16[32,512,512]{1,2,0:T(8,128)(2,...) while((s32[]{:T(128)}, f32[512,8,64]{0,2,1:T(8,128)}, ...), condition=%wide.region_13.13_spmd, body=%wide.region_12.12_spmd.sunk | while | flops 543424512 | bytes 5783773 | solution.py:155
  379.9 31.4 %while.66 = (s32[]{:T(128)}, f32[8,512]{1,0:T(8,128)S(1)}, f32[8,512]{1,0:T(8,128)S(1)}, s32[]{:T(128)}, s32[]{:T(128)}, /*index=5*/s32[32]{0:T(128)S(1)}, bf16[...) while((s32[]{:T(128)}, f32[8,512]{1,0:T(8,128)S(1)}, ...), condition=%wide.region_11.11_spmd, body=%wide.region_8.10_spmd.sunk | while | flops 278929408 | bytes 19087572 | solution.py:143
  412.4 38.9 %while.67 = (s32[]{:T(128)}, f32[512,8,64]{0,2,1:T(8,128)}, s32[]{:T(128)}, s32[]{:T(128)}, s32[32]{0:T(128)S(1)}, /*index=5*/bf16[32,512,512]{1,2,0:T(8,128)(2,...) while((s32[]{:T(128)}, f32[512,8,64]{0,2,1:T(8,128)}, ...), condition=%wide.region_13.13_spmd, body=%wide.region_12.12_spmd.sunk | while | flops 543424512 | bytes 5783773 | solution.py:155
  460.3 129.7 %all-reduce.7.cloned.1.call-done = bf16[1024,1024]{1,0:T(8,128)(2,1)} async-done(((bf16[1024,1024]{1,0:T(8,128)(2,1)}), bf16[1024,1024]{1,0:T(8,128)(2,1)}) %all-reduce.7.cloned.1.call-update) | async-done | bytes 2097168 | tf_op jit(solution)/shard_map/psum | solution.py:164
  593.6 25.3 %multiply_convert_fusion.1 = (bf16[1024,2048]{1,0:T(8,128)(2,1)S(1)}, f32[1024,2048]{1,0:T(8,128)}, f32[1024,2048]{1,0:T(8,128)}) fusion(f32[2048]{0:T(1024)S(1)} %convert_element_type.208, bf16[1024,2048]{1,0:T(8,128)(2,1)S(1)} %copy-done.55, f32[1024]{0:T(1024)S(1)} %convert_element_type.206, f32[1024]{0:T(1024)S(1)} %convert_element_type.205, ...), kind=kOutput, calls=%fused_computation.43 | convolution fusion | flops 4442816512 | bytes 29388800 | tf_op jit(solution)/shard_map/dot_general | solution.py:169
  620.9 5.7 convolution_convert_fusion.5
  627.1 62.6 %all-reduce.9.cloned.1.call-done = bf16[1024,1024]{1,0:T(8,128)(2,1)} async-done(((bf16[1024,1024]{1,0:T(8,128)(2,1)}), bf16[1024,1024]{1,0:T(8,128)(2,1)}) %all-reduce.9.cloned.1.call-update) | async-done | bytes 2097168 | tf_op jit(solution)/shard_map/psum | solution.py:175
  700.6 14.3 fusion.52
  714.9 9.3 convolution_convert_fusion.4
  725.5 61.8 %all-reduce.11.cloned.1.call-done = bf16[1024,1024]{1,0:T(8,128)(2,1)} async-done(((bf16[1024,1024]{1,0:T(8,128)(2,1)}), bf16[1024,1024]{1,0:T(8,128)(2,1)}) %all-reduce.11.cloned.1.call-update) | async-done | bytes 2097168 | tf_op jit(solution)/shard_map/psum | solution.py:191
  787.3 6.9 multiply_reduce_fusion
  804.6 21.3 %broadcast_in_dim.116 = f32[32,512,1024]{1,2,0:T(8,128)} broadcast(f32[]{:T(128)} %constant.88.clone.1), dimensions={} | broadcast | bytes 67108864 | tf_op jit(solution)/shard_map/broadcast_in_dim | solution.py:255
  825.9 137.0 %while.70 = (s32[]{:T(128)}, f32[32,512,1024]{1,2,0:T(8,128)}, bf16[2,512,512]{2,1,0:T(8,128)(2,1)}, s32[2]{0:T(128)S(1)}, s32[2]{0:T(128)S(1)}, /*index=5*/bf16...) while((s32[]{:T(128)}, f32[32,512,1024]{1,2,0:T(8,128)}, ...), condition=%wide.region_30.31_spmd.clone, body=%wide.region_27.30_spmd.sunk.clone | while | flops 1360789504 | bytes 60932680 | solution.py:256
  828.5 64.8 %while.69 = (s32[]{:T(128)}, f32[512,8,64]{0,2,1:T(8,128)S(1)}, f32[32,512,1024]{1,2,0:T(8,128)}, s32[]{:T(128)}, s32[]{:T(128)}, /*index=5*/s32[32]{0:T(128)S(1...) while((s32[]{:T(128)}, f32[512,8,64]{0,2,1:T(8,128)S(1)}, ...), condition=%wide.region_29.29_spmd, body=%wide.region_28.28_spmd.sunk | while | flops 1360789504 | bytes 54051064 | solution.py:252
  897.0 64.8 %while.69 = (s32[]{:T(128)}, f32[512,8,64]{0,2,1:T(8,128)S(1)}, f32[32,512,1024]{1,2,0:T(8,128)}, s32[]{:T(128)}, s32[]{:T(128)}, /*index=5*/s32[32]{0:T(128)S(1...) while((s32[]{:T(128)}, f32[512,8,64]{0,2,1:T(8,128)S(1)}, ...), condition=%wide.region_29.29_spmd, body=%wide.region_28.28_spmd.sunk | while | flops 1360789504 | bytes 54051064 | solution.py:252
  962.9 51.0 %copy.74 = bf16[32,512,1024]{2,1,0:T(8,128)(2,1)} copy(f32[32,512,1024]{1,2,0:T(8,128)} %get-tuple-element.1283) | data formatting | bytes 100663296 | tf_op jit(solution)/shard_map/while | solution.py:256
  1014.2 397.0 %reduce-scatter.3.cloned.1.call-done = bf16[2,512,1024]{2,1,0:T(8,128)(2,1)} async-done(((bf16[32,512,1024]{2,1,0:T(8,128)(2,1)}), bf16[2,512,1024]{2,1,0:T(8,128)(2,1)}) %reduce-scatter.3.cloned.1.call-update) | async-done | bytes 2097168 | tf_op jit(solution)/shard_map/reduce_scatter | solution.py:261
  1414.6 4.6 convolution_convert_fusion.3
  1419.4 10.2 convolution_convert_fusion.1
  1429.6 7.0 convolution_convert_fusion.2
  1438.9 5.0 convolution_convert_fusion
  1443.9 4.7 copy.75
  1450.9 63.0 %all-reduce = (bf16[2,512]{1,0:T(2,128)(2,1)S(1)}, bf16[1024]{0:T(1024)(128)(2,1)S(1)}, bf16[1024]{0:T(1024)(128)(2,1)S(1)}, bf16[1024]{0:T(1024)(128)(2,1)S(1)}...) all-reduce(bf16[2,512]{1,0:T(2,128)(2,1)S(1)} %pad_maximum_fusion.3, ...), channel_id=1, replica_groups=mesh['batch'=16,'head'=2] {'batch'}, use_global_device_ids=true, to_apply=%region_36.37 | all-reduce | flops 9216 | bytes 36864 | tf_op jit(solution)/shard_map/psum | solution.py:292
  1522.3 168.8 %all-reduce.13.cloned.1.call-done = (bf16[1024,3,512]{2,0,1:T(8,128)(2,1)}, bf16[512,1024]{1,0:T(8,128)(2,1)}, bf16[1024,2048]{1,0:T(8,128)(2,1)}, bf16[2048,1024]{1,0:T(8,128)(2,1)}) async-done(((bf16[1024,3,512]{2,0,1:T(8,128)(2,1)}, bf16[512,1024]{1,0:T(8,128)(2,1)}, bf16[1024,2048]{1,0:T(8,128)(2,1)}, bf16[2048,1024]{1,0:T(8,128)(2,1)}), (bf16[1024,3,512]{2,0,1:T(8,128)(2,1)}, ...) | async-done | bytes 12582928 | tf_op jit(solution)/shard_map/psum | solution.py:291
  (379 shorter events, 284.2 us)
Async XLA Ops:
  7.2 450.1 %copy-start = (bf16[512,1024]{1,0:T(8,128)(2,1)S(1)}, bf16[512,1024]{1,0:T(8,128)(2,1)}, u32[]{:S(2)}) copy-start(bf16[512,1024]{1,0:T(8,128)(2,1)} %param.31) | copy-start | bytes 3145732
  7.2 143.8 %all-gather.3.cloned.1.call-start = ((), (), s32[]{:S(2)}) async-start(), calls=%async_computation.2 | async-start | bytes 17825792 | tf_op jit(solution)/shard_map/all_gather | solution.py:122
  12.0 9.2 copy-start.43
  21.2 257.6 %all-gather.5.cloned.1.call-start = ((), (), s32[]{:S(2)}) async-start(), calls=%async_computation.3 | async-start | bytes 17825792 | tf_op jit(solution)/shard_map/all_gather | solution.py:123
  25.1 564.9 %all-reduce.7.cloned.1.call-start = ((), (), s32[]{:S(2)}) async-start(), calls=%async_computation.4 | async-start | bytes 4194304 | tf_op jit(solution)/shard_map/psum | solution.py:164
  457.2 132.7 %copy-start.3 = (bf16[1024,1024]{1,0:T(8,128)(2,1)S(1)}, bf16[1024,1024]{1,0:T(8,128)(2,1)}, u32[]{:S(2)}) copy-start(bf16[1024,1024]{1,0:T(8,128)(2,1)} %param.26) | copy-start | bytes 6291460
  459.9 229.8 %all-reduce.9.cloned.1.call-start = ((), (), s32[]{:S(2)}) async-start(), calls=%async_computation.5 | async-start | bytes 4194304 | tf_op jit(solution)/shard_map/psum | solution.py:175
  460.2 334.1 %copy-start.28 = (f32[1024]{0:T(1024)}, f32[1024]{0:T(1024)S(1)}, u32[]{:S(2)}) copy-start(f32[1024]{0:T(1024)S(1)} %convert_element_type.204) | copy-start | bytes 12292
  460.2 334.1 %copy-start.32 = (f32[1024]{0:T(1024)}, f32[1024]{0:T(1024)S(1)}, u32[]{:S(2)}) copy-start(f32[1024]{0:T(1024)S(1)} %convert_element_type.205) | copy-start | bytes 12292
  460.2 229.5 %copy-start.36 = (f32[1024]{0:T(1024)}, f32[1024]{0:T(1024)S(1)}, u32[]{:S(2)}) copy-start(f32[1024]{0:T(1024)S(1)} %convert_element_type.206) | copy-start | bytes 12292
  592.5 201.8 %copy-start.30 = (f32[1024]{0:T(1024)}, f32[1024]{0:T(1024)S(1)}, u32[]{:S(2)}) copy-start(f32[1024]{0:T(1024)S(1)} %broadcast_multiply_fusion.5) | copy-start | bytes 12292
  593.6 200.7 %copy-start.34 = (f32[1024]{0:T(1024)}, f32[1024]{0:T(1024)S(1)}, u32[]{:S(2)}) copy-start(f32[1024]{0:T(1024)S(1)} %add_rsqrt_fusion.1) | copy-start | bytes 12292
  593.6 27.3 %copy-start.53 = (bf16[2048,1024]{1,0:T(8,128)(2,1)S(1)}, bf16[2048,1024]{1,0:T(8,128)(2,1)}, u32[]{:S(2)}) copy-start(bf16[2048,1024]{1,0:T(8,128)(2,1)} %param.37) | copy-start | bytes 12582916
  626.6 160.8 %all-reduce.11.cloned.1.call-start = ((), (), s32[]{:S(2)}) async-start(), calls=%async_computation.6 | async-start | bytes 4194304 | tf_op jit(solution)/shard_map/psum | solution.py:191
  700.6 14.3 copy-start.8
  724.3 686.9 %reduce-scatter.3.cloned.1.call-start = ((), (), s32[]{:S(2)}) async-start(), calls=%async_computation.7 | async-start | bytes 35651584 | tf_op jit(solution)/shard_map/reduce_scatter | solution.py:261
  787.3 7.0 copy-start.9
  787.3 7.0 copy-start.15
  804.6 21.3 %copy-start.58 = (s32[32]{0:T(128)S(1)}, s32[32]{0:T(128)}, u32[]{:S(2)}) copy-start(s32[32]{0:T(128)} %copy-done.57) | copy-start | bytes 388
  1013.9 400.7 %copy-start.19 = (bf16[2,512,512]{2,1,0:T(8,128)(2,1)S(1)}, bf16[2,512,512]{2,1,0:T(8,128)(2,1)}, u32[]{:S(2)}) copy-start(bf16[2,512,512]{2,1,0:T(8,128)(2,1)} %get-tuple-element.1284) | copy-start | bytes 3145732
  1013.9 504.8 %reduce-scatter.5.cloned.1.call-start = ((), (), s32[]{:S(2)}) async-start(), calls=%async_computation.8 | async-start | bytes 3145728 | tf_op jit(solution)/shard_map/reduce_scatter | solution.py:285
  1419.2 10.3 copy-start.4
  1419.2 10.3 copy-start.29
  1419.2 10.3 copy-start.31
  1419.2 10.3 copy-start.33
  1419.3 10.3 copy-start.35
  1419.3 10.3 copy-start.37
  1419.3 271.8 %all-reduce.13.cloned.1.call-start = ((), (), s32[]{:S(2)}) async-start(), calls=%async_computation.9 | async-start | bytes 25165824 | tf_op jit(solution)/shard_map/psum | solution.py:291
  1419.3 10.3 copy-start.7
  1419.3 10.3 copy-start.60
  1429.6 7.0 copy-start.11
  1429.6 7.0 copy-start.23
  (37 other events, 114.8 us)
Sparse Core Ops, SparseCore 0:
  21.3 129.5 all-gather.2
  153.7 125.0 all-gather.4
  460.0 129.9 all-reduce.6
  626.7 62.9 all-reduce.8
  724.4 62.8 all-reduce.10
  1014.0 397.0 reduce-scatter.2
  1419.3 30.8 reduce-scatter.4
  1455.9 235.1 all-reduce.12
where the time goes:
time: 1720 us; the launch traced here: 1710 us
  waiting for transfers between devices  1050 us (61%)
  local copies, waits for them, and re-layouts  205 us (12%)
  matrix products  201 us (12%)
  other arithmetic  97.4 us (6%)
  loops' own time  82 us (5%)
  blocking collectives  63 us (4%)
    reduce_scatter x1, waiting for transfers between devices, local(): lax.psum_scatter(key_total.astype(jnp.bfloat16), 'batch', scatter_dimensi...  397 us
    psum x1, waiting for transfers between devices, local(): lax.psum(grad_qkv.astype(jnp.bfloat16), 'batch').astype(jnp.float32)  169 us
    psum x1, waiting for transfers between devices, local(): lax.psum(attn_part.astype(jnp.bfloat16), 'head').astype(jnp.float32)  130 us
    all_gather x1, waiting for transfers between devices, local(): lax.all_gather(own_keys, 'batch', axis=0, tiled=True)  124 us
    all_gather x1, waiting for transfers between devices, local(): lax.all_gather(own_values, 'batch', axis=0, tiled=True)  105 us
    psum x1, blocking collectives, local(): lax.psum(grad_qv.astype(jnp.bfloat16), 'batch').astype(jnp.float32)  63 us
    psum x1, waiting for transfers between devices, local(): lax.psum(down_part.astype(jnp.bfloat16), 'head').astype(jnp.float32)  62.6 us
    psum x1, waiting for transfers between devices, local(): lax.psum(ffn_back.astype(jnp.bfloat16), 'head').astype(jnp.float32)  61.8 us
  transfers between devices with their start and end apart: 8, of which 7 were waited for; matrix products, arithmetic and copies ran while one was open for 4% of the time, Pallas kernels for 0%

commit v1 on v0

--- a/solution.py
+++ b/solution.py
@@ -1,11 +1,17 @@
+import math
+
 import jax
 import jax.numpy as jnp
 from jax import lax
+from jax.experimental import pallas as pl
+from jax.experimental.pallas import tpu as pltpu
+from jax.sharding import Mesh
 from jax.sharding import PartitionSpec as P
 
 HD = 64
 CH = 512
-
+ATTEND_PARTS = 2
+BACK_PARTS = 2
 
 EPSILON = 1e-05
 
@@ -319,9 +325,641 @@
     )
 
 
+LOG2E = 1.4426950408889634
+SCORE = HD ** (-0.5)
+SWAP = [(0, 1), (1, 0)]
+VMEM_LIMIT = 56 * 1024 * 1024
+
+
+def nt(left, right):
+    return lax.dot_general(
+        left, right, (((1,), (1,)), ((), ())), preferred_element_type=jnp.float32
+    )
+
+
+def mm(left, right):
+    return jnp.dot(left, right, preferred_element_type=jnp.float32)
+
+
+def low_half(block):
+    lane = lax.broadcasted_iota(jnp.int32, block.shape, 1)
+    return lane < HD
+
+
+def project_kernel(x_ref, wq_ref, wk_ref, wv_ref, bias_ref, kv_ref, q_ref):
+    slot = pl.program_id(1)
+    rows = x_ref[...]
+    q_all = mm(rows, wq_ref[...]) + bias_ref[0:1, :].astype(jnp.float32)
+    k_all = mm(rows, wk_ref[...])
+    v_all = mm(rows, wv_ref[...]) + bias_ref[1:2, :].astype(jnp.float32)
+    for pair in range(q_all.shape[1] // 128):
+        cols = slice(pair * 128, pair * 128 + 128)
+        q_pair, k_pair, v_pair = q_all[:, cols], k_all[:, cols], v_all[:, cols]
+        low = low_half(q_pair)
+        kv_ref[2 * pair] = jnp.where(low, k_pair, pltpu.roll(v_pair, HD, 1)).astype(jnp.bfloat16)
+        kv_ref[2 * pair + 1] = jnp.where(low, pltpu.roll(k_pair, HD, 1), v_pair).astype(
+            jnp.bfloat16
+        )
+        q_low = q_pair.astype(jnp.bfloat16)
+        q_roll = pltpu.roll(q_pair, HD, 1).astype(jnp.bfloat16)
+
+        @pl.when(slot == 0)
+        def _():
+            q_ref[2 * pair, :, 0:HD] = q_low[:, 0:HD]
+            q_ref[2 * pair + 1, :, 0:HD] = q_roll[:, 0:HD]
+
+        @pl.when(slot == 1)
+        def _():
+            q_ref[2 * pair, :, HD:128] = q_roll[:, HD:128]
+            q_ref[2 * pair + 1, :, HD:128] = q_low[:, HD:128]
+
+
+def project(layer_in, weight, bias):
+    width = layer_in.shape[1]
+    heads = weight.shape[1] // 3 // HD
+    step = 4
+    groups = heads // step
+    cols = step * HD
+    return pl.pallas_call(
+        project_kernel,
+        grid=(groups, 2),
+        in_specs=[
+            pl.BlockSpec((CH, width), lambda g, s: (s, 0)),
+            pl.BlockSpec((width, cols), lambda g, s: (0, g)),
+            pl.BlockSpec((width, cols), lambda g, s: (0, groups + g)),
+            pl.BlockSpec((width, cols), lambda g, s: (0, 2 * groups + g)),
+            pl.BlockSpec((2, cols), lambda g, s: (0, g)),
+        ],
+        out_specs=[
+            pl.BlockSpec((step, CH, 128), lambda g, s: (g, s, 0)),
+            pl.BlockSpec((step, CH, 128), lambda g, s: (g, 0, 0)),
+        ],
+        out_shape=[
+            jax.ShapeDtypeStruct((heads, 2 * CH, 128), jnp.bfloat16),
+            jax.ShapeDtypeStruct((heads, CH, 128), jnp.bfloat16),
+        ],
+        compiler_params=pltpu.CompilerParams(vmem_limit_bytes=VMEM_LIMIT),
+        cost_estimate=pl.CostEstimate(
+            flops=2 * layer_in.size * weight.shape[1],
+            bytes_accessed=2 * (layer_in.size + weight.size) + 6 * layer_in.size,
+            transcendentals=0,
+        ),
+        name="project",
+    )(layer_in, weight, weight, weight, bias)
+
+
+def fill_tables(slot_ref, seq_ref, stretch_slot, seq_first, seq_length):
+    def place(slot, carry):
+        stretch_slot[slot_ref[slot]] = slot
+        return carry
+
+    lax.fori_loop(0, slot_ref.shape[0], place, 0)
+
+    def one_sequence(seq, start):
+        length = seq_ref[seq]
+
+        def one_stretch(offset, carry):
+            seq_first[start + offset] = start
+            seq_length[start + offset] = length
+            return carry
+
+        lax.fori_loop(0, length, one_stretch, 0)
+        return start + length
+
+    lax.fori_loop(0, seq_ref.shape[0], one_sequence, jnp.int32(0))
+
+
+def key_index(slot, core, half):
+    own = ((slot >> 1) & 1) == core
+    return jnp.where(own, 0, half) + ((slot >> 2) << 1) + (slot & 1)
+
+
+def load_keys(own_hbm, other_hbm, keys, sem):
+    half = own_hbm.shape[0]
+    first = pltpu.make_async_copy(own_hbm, keys.at[pl.ds(0, half)], sem.at[0])
+    second = pltpu.make_async_copy(other_hbm, keys.at[pl.ds(half, half)], sem.at[1])
+    first.start()
+    second.start()
+    first.wait()
+    second.wait()
+
+
+def pick_slot(packed, slot_bit):
+    wide = packed.astype(jnp.float32)
+    return jnp.where(slot_bit == 0, wide, pltpu.roll(wide, HD, 1))
+
+
+def attend_kernel(
+    slot_ref,
+    seq_ref,
+    core_ref,
+    q_ref,
+    own_hbm,
+    other_hbm,
+    ctx_ref,
+    ctx_t_ref,
+    lse_ref,
+    keys,
+    values_t,
+    stretch_slot,
+    seq_first,
+    seq_length,
+    sem,
+):
+    chip, bit = pl.program_id(0), pl.program_id(1)
+    half = own_hbm.shape[0]
+
+    @pl.when((chip == 0) & (bit == 0))
+    def _():
+        load_keys(own_hbm, other_hbm, keys, sem)
+        fill_tables(slot_ref, seq_ref, stretch_slot, seq_first, seq_length)
+
+        def turn(index, carry):
+            values_t[index] = keys[index].T[HD:128, :]
+            return carry
+
+        lax.fori_loop(0, 2 * half, turn, 0)
+
+    core = core_ref[0]
+    stretch = slot_ref[4 * chip + 2 * core + bit]
+    begin, length = seq_first[stretch], seq_length[stretch]
+    query = pick_slot(q_ref[0], bit)
+    query = jnp.where(low_half(query), query, 0.0).astype(jnp.bfloat16)
+    parts = ATTEND_PARTS
+    part = CH // parts
+
+    def step(offset, state):
+        index = key_index(stretch_slot[begin + offset], core, half)
+        block = keys[index]
+        block_t = values_t[index]
+        fresh = []
+        for n in range(parts):
+            top, total, acc = state[n]
+            score = nt(block, query[n * part : (n + 1) * part, :]) * (SCORE * LOG2E)
+            new_top = jnp.maximum(top, jnp.max(score, axis=0, keepdims=True))
+            weight = jnp.exp2(score - new_top)
+            scale = jnp.exp2(top - new_top)
+            total = total * scale + jnp.sum(weight, axis=0, keepdims=True)
+            acc = acc * scale + mm(block_t, weight.astype(jnp.bfloat16))
+            fresh.append((new_top, total, acc))
+        return tuple(fresh)
+
+    start = tuple(
+        (
+            jnp.full((1, part), -1e30, jnp.float32),
+            jnp.zeros((1, part), jnp.float32),
+            jnp.zeros((HD, part), jnp.float32),
+        )
+        for _ in range(parts)
+    )
+    final = lax.fori_loop(0, length, step, start)
+    for n in range(parts):
+        top, total, acc = final[n]
+        cols = slice(n * part, (n + 1) * part)
+        context_t = acc / total
+        ctx_t_ref[0, :, cols] = context_t
+        lse_ref[0, :, cols] = top + jnp.log2(total)
+        turned = context_t.T.astype(jnp.bfloat16)
+
+        @pl.when(bit == 0)
+        def _():
+            ctx_ref[0, cols, 0:HD] = turned
+
+        @pl.when(bit == 1)
+        def _():
+            ctx_ref[0, cols, HD:128] = turned
+
+
+def table_scratch(stretches):
+    return [pltpu.SMEM((stretches,), jnp.int32) for _ in range(3)] + [
+        pltpu.SemaphoreType.DMA((2,))
+    ]
+
+
+def attend(slot_stretch, seq_stretches, core, q_pack, own_keys, other_keys):
+    chips = q_pack.shape[0]
+    slots = 2 * chips
+    stretches = slot_stretch.shape[0]
+    pairs = slots * 5 * CH * CH
+    return pl.pallas_call(
+        attend_kernel,
+        grid_spec=pltpu.PrefetchScalarGridSpec(
+            num_scalar_prefetch=3,
+            grid=(chips, 2),
+            in_specs=[
+                pl.BlockSpec((1, CH, 128), lambda z, s, *_: (z, 0, 0)),
+                pl.BlockSpec(memory_space=pl.ANY),
+                pl.BlockSpec(memory_space=pl.ANY),
+            ],
+            out_specs=[
+                pl.BlockSpec((1, CH, 128), lambda z, s, *_: (z, 0, 0)),
+                pl.BlockSpec((1, HD, CH), lambda z, s, *_: (2 * z + s, 0, 0)),
+                pl.BlockSpec((1, 1, CH), lambda z, s, *_: (2 * z + s, 0, 0)),
+            ],
+            scratch_shapes=[
+                pltpu.VMEM((2 * slots, CH, 128), jnp.bfloat16),
+                pltpu.VMEM((2 * slots, HD, CH), jnp.bfloat16),
+            ]
+            + table_scratch(stretches),
+        ),
+        out_shape=[
+            jax.ShapeDtypeStruct((chips, CH, 128), jnp.bfloat16),
+            jax.ShapeDtypeStruct((slots, HD, CH), jnp.float32),
+            jax.ShapeDtypeStruct((slots, 1, CH), jnp.float32),
+        ],
+        compiler_params=pltpu.CompilerParams(vmem_limit_bytes=VMEM_LIMIT),
+        cost_estimate=pl.CostEstimate(
+            flops=4 * HD * pairs, bytes_accessed=16 * q_pack.size, transcendentals=pairs
+        ),
+        name="attend",
+    )(slot_stretch, seq_stretches, core, q_pack, own_keys, other_keys)
+
+
+def attend_back_kernel(
+    slot_ref,
+    seq_ref,
+    core_ref,
+    q_ref,
+    g_ref,
+    ctx_t_ref,
+    lse_ref,
+    own_hbm,
+    other_hbm,
+    dq_ref,
+    own_grad_ref,
+    other_grad_ref,
+    keys,
+    keys_t,
+    grads,
+    stretch_slot,
+    seq_first,
+    seq_length,
+    sem,
+):
+    chip, bit = pl.program_id(0), pl.program_id(1)
+    half = own_hbm.shape[0]
+
+    @pl.when((chip == 0) & (bit == 0))
+    def _():
+        load_keys(own_hbm, other_hbm, keys, sem)
+        fill_tables(slot_ref, seq_ref, stretch_slot, seq_first, seq_length)
+
+        def turn(index, carry):
+            keys_t[index] = keys[index].T[0:HD, :]
+            grads[index] = jnp.zeros((CH, 128), jnp.float32)
+            return carry
+
+        lax.fori_loop(0, 2 * half, turn, 0)
+
+    core = core_ref[0]
+    stretch = slot_ref[4 * chip + 2 * core + bit]
+    begin, length = seq_first[stretch], seq_length[stretch]
+    query = pick_slot(q_ref[0], bit)
+    low = low_half(query)
+    query = jnp.where(low, query, 0.0).astype(jnp.bfloat16)
+    grad = pick_slot(g_ref[0], 1 - bit)
+    grad = jnp.where(low, 0.0, grad)
+    delta = jnp.sum(grad.T[HD:128, :] * ctx_t_ref[0], axis=0, keepdims=True)
+    grad = grad.astype(jnp.bfloat16)
+    lse = lse_ref[0]
+    parts = BACK_PARTS
+    part = CH // parts
+
+    def step(offset, state):
+        index = key_index(stretch_slot[begin + offset], core, half)
+        block = keys[index]
+        block_t = keys_t[index]
+        fresh = []
+        total = None
+        for n in range(parts):
+            cols = slice(n * part, (n + 1) * part)
+            q_part, g_part = query[cols, :], grad[cols, :]
+            score = nt(block, q_part) * (SCORE * LOG2E)
+            weight = jnp.exp2(score - lse[:, cols])
+            slope = weight * (nt(block, g_part) - delta[:, cols])
+            slope = slope.astype(jnp.bfloat16)
+            weight = weight.astype(jnp.bfloat16)
+            fresh.append(state[n] + mm(block_t, slope))
+            update = mm(slope, q_part) + mm(weight, g_part)
+            total = update if total is None else total + update
+        grads[index] += total
+        return tuple(fresh)
+
+    start = tuple(jnp.zeros((HD, part), jnp.float32) for _ in range(parts))
+    final = lax.fori_loop(0, length, step, start)
+    for n in range(parts):
+        cols = slice(n * part, (n + 1) * part)
+        turned = (final[n] * SCORE).T.astype(jnp.bfloat16)
+
+        @pl.when(bit == 0)
+        def _():
+            dq_ref[0, cols, 0:HD] = turned
+
+        @pl.when(bit == 1)
+        def _():
+            dq_ref[0, cols, HD:128] = turned
+
+    @pl.when((chip == pl.num_programs(0) - 1) & (bit == 1))
+    def _():
+        scale = jnp.where(low, SCORE, 1.0)
+
+        def leave(index, carry):
+            own_grad_ref[index] = grads[index] * scale
+            other_grad_ref[index] = (grads[half + index] * scale).astype(jnp.bfloat16)
+            return carry
+
+        lax.fori_loop(0, half, leave, 0)
+
+
+def attend_back(
+    slot_stretch, seq_stretches, core, q_pack, g_pack, ctx_t, lse, own_keys, other_keys
+):
+    chips = q_pack.shape[0]
+    slots = 2 * chips
+    stretches = slot_stretch.shape[0]
+    pairs = slots * 5 * CH * CH
+    return pl.pallas_call(
+        attend_back_kernel,
+        grid_spec=pltpu.PrefetchScalarGridSpec(
+            num_scalar_prefetch=3,
+            grid=(chips, 2),
+            in_specs=[
+                pl.BlockSpec((1, CH, 128), lambda z, s, *_: (z, 0, 0)),
+                pl.BlockSpec((1, CH, 128), lambda z, s, *_: (z, 0, 0)),
+                pl.BlockSpec((1, HD, CH), lambda z, s, *_: (2 * z + s, 0, 0)),
+                pl.BlockSpec((1, 1, CH), lambda z, s, *_: (2 * z + s, 0, 0)),
+                pl.BlockSpec(memory_space=pl.ANY),
+                pl.BlockSpec(memory_space=pl.ANY),
+            ],
+            out_specs=[
+                pl.BlockSpec((1, CH, 128), lambda z, s, *_: (z, 0, 0)),
+                pl.BlockSpec((slots, CH, 128), lambda z, s, *_: (0, 0, 0)),
+                pl.BlockSpec((slots, CH, 128), lambda z, s, *_: (0, 0, 0)),
+            ],
+            scratch_shapes=[
+                pltpu.VMEM((2 * slots, CH, 128), jnp.bfloat16),
+                pltpu.VMEM((2 * slots, HD, CH), jnp.bfloat16),
+                pltpu.VMEM((2 * slots, CH, 128), jnp.float32),
+            ]
+            + table_scratch(stretches),
+        ),
+        out_shape=[
+            jax.ShapeDtypeStruct((chips, CH, 128), jnp.bfloat16),
+            jax.ShapeDtypeStruct((slots, CH, 128), jnp.float32),
+            jax.ShapeDtypeStruct((slots, CH, 128), jnp.bfloat16),
+        ],
+        compiler_params=pltpu.CompilerParams(vmem_limit_bytes=VMEM_LIMIT),
+        cost_estimate=pl.CostEstimate(
+            flops=10 * HD * pairs, bytes_accessed=24 * q_pack.size, transcendentals=pairs
+        ),
+        name="attend_back",
+    )(slot_stretch, seq_stretches, core, q_pack, g_pack, ctx_t, lse, own_keys, other_keys)
+
+
+def swap_across(block, axis_name):
+    return lax.ppermute(block, axis_name, SWAP)
+
+
+def spread(block):
+    return lax.all_to_all(block, "chip", 0, 0, tiled=True)
+
+
+def gelu_both(pre):
+    phi = 0.5 + 0.5 * lax.erf(pre * (2.0**-0.5))
+    density = jnp.exp(-0.5 * pre * pre) * ((2.0 * math.pi) ** -0.5)
+    return ((pre * phi).astype(jnp.bfloat16), phi + pre * density)
+
+
+def tn(left, right):
+    return lax.dot_general(
+        left, right, (((0,), (0,)), ((), ())), preferred_element_type=jnp.float32
+    )
+
+
+def fast_local(
+    layer_in,
+    slot_stretch,
+    seq_stretches,
+    w_qkv,
+    qv_bias,
+    w_out,
+    out_bias,
+    norm1_gain,
+    norm1_shift,
+    w_up,
+    up_bias,
+    w_down,
+    down_bias,
+    norm2_gain,
+    norm2_shift,
+    cotangent,
+):
+    width = layer_in.shape[1]
+    cols = w_qkv.shape[2]
+    heads = cols // HD
+    units = w_up.shape[1]
+    half = units // 2
+    side = lax.axis_index("head")
+    core = lax.axis_index("core")
+    core_vec = core.reshape(1).astype(jnp.int32)
+    low = jnp.bfloat16
+
+    def both_halves(array, axis):
+        mine = lax.dynamic_slice_in_dim(array, core * half, half, axis)
+        rest = lax.dynamic_slice_in_dim(array, (1 - core) * half, half, axis)
+        far_mine = swap_across(mine, "head")
+        return [mine, rest, far_mine, swap_across(far_mine, "core")]
+
+    proj_weight = w_qkv.reshape(width, 3 * cols)
+    send_kv, send_q = project(layer_in, proj_weight, qv_bias)
+    own_kv = spread(send_kv)
+    q_pack = spread(send_q)
+    other_kv = swap_across(own_kv, "core")
+    own_keys = own_kv.reshape(2 * heads, CH, 128)
+    other_keys = other_kv.reshape(2 * heads, CH, 128)
+
+    up_parts = both_halves(w_up, 1)
+    down_parts = both_halves(w_down, 0)
+    up_biases = both_halves(up_bias, 0)
+    w_out_far = swap_across(w_out, "head")
+
+    ctx, ctx_t, lse = attend(slot_stretch, seq_stretches, core_vec, q_pack, own_keys, other_keys)
+    ctx_in = spread(ctx).reshape(heads, CH, 2, HD)
+    ctx_in = ctx_in.transpose(2, 1, 0, 3).reshape(2, CH, cols)
+    ctx_own = lax.dynamic_index_in_dim(ctx_in, side, 0, keepdims=False)
+    ctx_far = swap_across(lax.dynamic_index_in_dim(ctx_in, 1 - side, 0, keepdims=False), "head")
+
+    row0 = side * CH
+    rows_in = lax.dynamic_slice_in_dim(layer_in, row0, CH, 0).astype(jnp.float32)
+    cot = lax.dynamic_slice_in_dim(cotangent, row0, CH, 0).astype(jnp.float32)
+    hidden = rows_in + (mm(ctx_own, w_out) + mm(ctx_far, w_out_far)) + out_bias
+    first_norm, normed_one, inv_one = norm_forward(hidden, norm1_gain, norm1_shift)
+    first_low = first_norm.astype(low)
+    acts, slopes = [], []
+    down_sum = None
+    for up, bias, down in zip(up_parts, up_biases, down_parts):
+        act, slope = gelu_both(mm(first_low, up) + bias)
+        acts.append(act)
+        slopes.append(slope)
+        term = mm(act, down)
+        down_sum = term if down_sum is None else down_sum + term
+    second_in = first_norm + down_sum + down_bias
+    normed_out, normed_two, inv_two = norm_forward(second_in, norm2_gain, norm2_shift)
+    grad_second, grad_gain_two, grad_shift_two = norm_backward(
+        cot, normed_two, inv_two, norm2_gain
+    )
+    out_rows = normed_out.astype(low)
+    second_low = grad_second.astype(low)
+    grad_pres = []
+    back_sum = None
+    for up, down, slope in zip(up_parts, down_parts, slopes):
+        grad_pre = (nt(second_low, down) * slope).astype(low)
+        grad_pres.append(grad_pre)
+        term = nt(grad_pre, up)
+        back_sum = term if back_sum is None else back_sum + term
+    grad_first = back_sum + grad_second
+    grad_hidden, grad_gain_one, grad_shift_one = norm_backward(
+        grad_first, normed_one, inv_one, norm1_gain
+    )
+    hidden_low = grad_hidden.astype(low)
+    gc_far = nt(hidden_low, w_out_far).astype(low)
+    gc_own = nt(hidden_low, w_out).astype(low)
+    gc_in = swap_across(gc_far, "head")
+
+    def head_major(first, second):
+        pair = jnp.stack([first, second]).reshape(2, CH, heads, HD)
+        return pair.transpose(2, 1, 0, 3).reshape(heads, CH, 128)
+
+    is_low = side == 0
+    g_pack = spread(
+        head_major(jnp.where(is_low, gc_own, gc_in), jnp.where(is_low, gc_in, gc_own))
+    )
+
+    def reduce_far(own, far):
+        kept = own[0] + swap_across(own[1].astype(low), "core").astype(jnp.float32)
+        gone = far[0] + swap_across(far[1].astype(low), "core").astype(jnp.float32)
+        return kept + swap_across(gone.astype(low), "head").astype(jnp.float32)
+
+    up_grads = [tn(first_low, part) for part in grad_pres]
+    down_grads = [tn(act, second_low) for act in acts]
+    half_rows = cols // 2
+
+    def rows_of(block, which):
+        return lax.dynamic_slice_in_dim(block, which * half_rows, half_rows, 1)
+
+    out_grads = [
+        tn(rows_of(block, which), hidden_low)
+        for block in (ctx_own, ctx_far)
+        for which in (core, 1 - core)
+    ]
+    sums = [
+        reduce_far(part[:2], part[2:]).astype(low) for part in (up_grads, down_grads, out_grads)
+    ]
+    sums = lax.psum(tuple(sums), "chip")
+
+    def join(mine, axis):
+        rest = swap_across(mine, "core")
+        is_first = core == 0
+        return jnp.concatenate(
+            [jnp.where(is_first, mine, rest), jnp.where(is_first, rest, mine)], axis=axis
+        ).astype(jnp.float32)
+
+    grad_up, grad_down, grad_out = join(sums[0], 1), join(sums[1], 0), join(sums[2], 0)
+
+    bias_grads = [jnp.sum(part.astype(jnp.float32), axis=0) for part in grad_pres]
+    is_first = core == 0
+
+    def ordered(first, second):
+        return jnp.concatenate(
+            [jnp.where(is_first, first, second), jnp.where(is_first, second, first)]
+        )
+
+    bias_own, bias_far = ordered(*bias_grads[:2]), ordered(*bias_grads[2:])
+    small = jnp.concatenate(
+        [
+            jnp.where(is_low, bias_own, bias_far),
+            jnp.where(is_low, bias_far, bias_own),
+            jnp.sum(grad_hidden, axis=0),
+            grad_gain_one,
+            grad_shift_one,
+            jnp.sum(grad_second, axis=0),
+            grad_gain_two,
+            grad_shift_two,
+        ]
+    )
+    small = lax.psum(small, ("chip", "core", "head"))
+    grad_up_bias = lax.dynamic_slice_in_dim(small, side * units, units)
+    vectors = small[2 * units :].reshape(6, width)
+
+    layer_out_pair = jnp.stack([out_rows, swap_across(out_rows, "head")])
+    layer_out = jnp.where(is_low, layer_out_pair, layer_out_pair[::-1]).reshape(2 * CH, width)
+
+    dq_pack, own_grad, other_grad = attend_back(
+        slot_stretch, seq_stretches, core_vec, q_pack, g_pack, ctx_t, lse, own_keys, other_keys
+    )
+    kv_grad = (own_grad + swap_across(other_grad, "core").astype(jnp.float32)).astype(low)
+    kv_grad = spread(kv_grad.reshape(heads, 2 * CH, 128))
+    dq_in = spread(dq_pack)
+
+    grad_q = dq_in.reshape(heads, CH, 2, HD).transpose(2, 1, 0, 3).reshape(2 * CH, cols)
+    kv_rows = kv_grad.reshape(heads, 2 * CH, 2, HD).transpose(1, 2, 0, 3)
+    grad_proj = jnp.concatenate([grad_q, kv_rows.reshape(2 * CH, 2 * cols)], axis=1)
+    grad_qkv = tn(layer_in, grad_proj).astype(low)
+    row_sums = jnp.sum(grad_proj.astype(jnp.float32), axis=0)
+    grad_qv = jnp.stack([row_sums[:cols], row_sums[2 * cols :]])
+    input_part = nt(grad_proj, proj_weight)
+    own_width = width // 2
+    far_part = lax.dynamic_slice_in_dim(input_part, (1 - side) * own_width, own_width, 1)
+    own_part = lax.dynamic_slice_in_dim(input_part, side * own_width, own_width, 1)
+    rows_pair = jnp.where(
+        jnp.arange(2)[:, None, None] == side, grad_hidden[None].astype(jnp.float32), 0.0
+    ).reshape(2 * CH, width)
+    far_hidden = lax.dynamic_slice_in_dim(rows_pair, (1 - side) * own_width, own_width, 1)
+    own_hidden = lax.dynamic_slice_in_dim(rows_pair, side * own_width, own_width, 1)
+    arrived = swap_across((far_part + far_hidden).astype(low), "head")
+    grad_in = own_part + own_hidden + arrived.astype(jnp.float32)
+    grad_qkv, grad_qv = lax.psum((grad_qkv, grad_qv.astype(low)), ("chip", "core"))
+    return (
+        layer_out,
+        grad_in,
+        grad_qkv.astype(jnp.float32).reshape(width, 3, cols),
+        grad_qv.astype(jnp.float32),
+        grad_out,
+        vectors[0],
+        vectors[1],
+        vectors[2],
+        grad_up,
+        grad_up_bias,
+        grad_down,
+        vectors[3],
+        vectors[4],
+        vectors[5],
+    )
+
+
 def solution(mesh):
+    batch, head = mesh.shape["batch"], mesh.shape["head"]
+
+    def whole(*arrays):
+        tokens, width = arrays[0].shape
+        heads = arrays[3].shape[2] // head // HD
+        fits = (
+            head == 2
+            and batch == 2 * heads
+            and tokens == batch * 2 * CH
+            and arrays[9].shape[1] % (4 * 128) == 0
+        )
+        if fits:
+            split = Mesh(mesh.devices.reshape(batch // 2, 2, head), ("chip", "core", "head"))
+            return run(fast_local, split, ("chip", "core"))(*arrays)
+        return run(local, mesh, "batch")(*arrays)
+
+    return whole
+
+
+def run(body, mesh, rows):
     in_specs = (
-        P("batch", None),
+        P(rows, None),
         P(),
         P(),
         P(None, None, "head"),
@@ -336,11 +974,11 @@
         P(),
         P(),
         P(),
-        P("batch", None),
+        P(rows, None),
     )
     out_specs = (
-        P("batch", None),
-        P("batch", "head"),
+        P(rows, None),
+        P(rows, "head"),
         P(None, None, "head"),
         P(None, "head"),
         P("head", None),
@@ -354,4 +992,4 @@
         P(),
         P(),
     )
-    return jax.shard_map(local, mesh=mesh, in_specs=in_specs, out_specs=out_specs, check_vma=False)
+    return jax.shard_map(body, mesh=mesh, in_specs=in_specs, out_specs=out_specs, check_vma=False)

time: 1720 us -> 890 us (0.52)
  waiting for transfers between devices: 1050 us -> 257 us
  Pallas kernels: 0 us -> 194 us
  local copies, waits for them, and re-layouts: 205 us -> 37.6 us
  blocking collectives: 63 us -> 186 us
  matrix products: 201 us -> 85.6 us
  loops' own time: 82 us -> 0 us
  starting transfers between devices: 1.5 us -> 45.4 us
  other arithmetic: 97.4 us -> 61.5 us
    reduce_scatter x2 -> x0, waiting for transfers between devices: 397 us -> none  [the longest x1 397 us: local(): lax.psum_scatter(key_total.astype(jnp.bfloat16), 'batch', scatter_dimensi...]
    psum x4 -> x2, waiting for transfers between devices: 423 us -> 130 us  [the longest x1 71.8 us: fast_local(): sums = lax.psum(tuple(sums), 'chip')]
    all_gather x2 -> x0, waiting for transfers between devices: 229 us -> none  [the longest x1 124 us: local(): lax.all_gather(own_keys, 'batch', axis=0, tiled=True)]
    pallas_call x0 -> x3, Pallas kernels: none -> 194 us  [the longest x1 98 us: attend_back(): pl.pallas_call(attend_back_kernel, grid_spec=pltpu.PrefetchScalarGridSpec...]
    dot_general x68 -> x34, matrix products: 201 us -> 85.6 us  [the longest x13 35.6 us: tn(): lax.dot_general(left, right, (((0,), (0,)), ((), ())), preferred_element_...]
    while x12 -> x0, local copies, waits for them, and re-layouts: 97.4 us -> none  [the longest x1 51 us: local(): lax.scan(back_slot, key_start, (query_slots, grad_slots, log_totals, delt...]
    another operation x8 -> x0, loops' own time: 82 us -> none  [the longest x2 27.7 us: attend(): row_max, row_total = lax.fori_loop(0, length, norm_step, initial)]
    psum x1 -> x2, blocking collectives: 63 us -> 131 us  [the longest x1 97.9 us: fast_local(): small = lax.psum(small, ('chip', 'core', 'head'))]
  transfers between devices with their start and end apart: 8 -> 32, of which waited for: 7 -> 9; matrix products, arithmetic and copies ran while one was open for 4% -> 14% of each run, Pallas kernels for 0% -> 21%
where the time goes in v1:
time: 890 us; the launch traced here: 884 us
  waiting for transfers between devices  257 us (29%)
  Pallas kernels  194 us (22%)
  blocking collectives  186 us (21%)
  matrix products  85.6 us (10%)
  other arithmetic  61.5 us (7%)
  starting transfers between devices  45.4 us (5%)
  local copies, waits for them, and re-layouts  37.6 us (4%)
  between operations  16.7 us (2%)
    pallas_call x1, Pallas kernels, attend_back(): pl.pallas_call(attend_back_kernel, grid_spec=pltpu.PrefetchScalarGridSpec...  98 us
    psum x1, blocking collectives, fast_local(): small = lax.psum(small, ('chip', 'core', 'head'))  97.9 us
    pallas_call x1, Pallas kernels, attend(): pl.pallas_call(attend_kernel, grid_spec=pltpu.PrefetchScalarGridSpec(num_...  87.6 us
    psum x1, waiting for transfers between devices, fast_local(): sums = lax.psum(tuple(sums), 'chip')  71.8 us
    ppermute x25, waiting for transfers between devices, swap_across(): return lax.ppermute(block, axis_name, SWAP)  64.2 us
    all_to_all x5, waiting for transfers between devices, spread(): return lax.all_to_all(block, 'chip', 0, 0, tiled=True)  63 us
    psum x1, waiting for transfers between devices, fast_local(): lax.psum((grad_qkv, grad_qv.astype(low)), ('chip', 'core'))  57.9 us
    all_to_all x1, blocking collectives, spread(): return lax.all_to_all(block, 'chip', 0, 0, tiled=True)  55.5 us
  transfers between devices with their start and end apart: 32, of which 9 were waited for; matrix products, arithmetic and copies ran while one was open for 14% of the time, Pallas kernels for 21%

profile of v1, /device:TPU:0, one launch (start us, length us, event | category | flops | bytes accessed | tf_op | source)
XLA Modules:
  0.0 884.0 jit_solution(15764955604429271726)
XLA Ops:
  14.5 8.5 project.1
  23.1 55.5 %all_to_all.30 = bf16[8,1024,128]{2,1,0:T(8,128)(2,1)S(1)} all-to-all(bf16[8,1024,128]{2,1,0:T(8,128)(2,1)} %get-tuple-element.23), channel_id=1, replica_groups=mesh['chip'=8,'core'=2,'head'=2] {'chip'}, dimensions={0} | all-to-all | bytes 4194304 | tf_op jit(solution)/shard_map/all_to_all | solution.py:724
  86.8 22.1 %all-to-all-done.q_ref = bf16[8,512,128]{2,1,0:T(8,128)(2,1)S(1)} async-done(((bf16[8,512,128]{2,1,0:T(8,128)(2,1)}), bf16[8,512,128]{2,1,0:T(8,128)(2,1)S(1)}, u32[]{:S(2)}, u32[]{:S(2)}) %all-to-all-start) | async-done | bytes 1048608 | tf_op jit(solution)/shard_map/all_to_all | solution.py:724
  109.8 87.6 %attend.1 = (bf16[8,512,128]{2,1,0:T(8,128)(2,1)}, f32[16,64,512]{2,1,0:T(8,128)}, f32[16,1,512]{2,1,0:T(1,128)}) custom-call(s32[32]{0:T(128)} %slot_ref.3, s32[8]{0:T(128)} %seq_ref.3, s32[1]{0:T(128)} %bitcast.core_ref, bf16[8,512,128]{2,1,0:T(8,128)(2,1)} %copy-done.26, bf16[16,512,128]{2,1,0:T(8,128)(2,1)} %bitcast.122, ...), custom_call_target="tpu_custom_call" | custom-call | flops 5368709120 | bytes 8388608 | tf_op jit(solution)/shard_map/attend/pallas_call | solution.py:544
  197.4 3.6 all-to-all-start.2
  206.2 20.2 %all-to-all-done.2 = bf16[8,512,128]{2,1,0:T(8,128)(2,1)S(1)} async-done(((bf16[8,512,128]{2,1,0:T(8,128)(2,1)}), bf16[8,512,128]{2,1,0:T(8,128)(2,1)S(1)}, u32[]{:S(2)}, u32[]{:S(2)}) %all-to-all-start.2) | async-done | bytes 1048608 | tf_op jit(solution)/shard_map/all_to_all | solution.py:724
  229.3 54.7 %collective-permute-done.4 = bf16[1024]{0:T(1024)(128)(2,1)S(1)} collective-permute-done((bf16[1024]{0:T(1024)(128)(2,1)S(1)}, bf16[1024]{0:T(1024)(128)(2,1)S(1)}, u32[]{:S(2)}, u32[]{:S(2)}) %collective-permute-start.4) | collective-permute-done | bytes 2080 | tf_op jit(solution)/shard_map/ppermute | solution.py:720
  327.0 3.8 convert_reduce_fusion.4
  338.8 3.7 convert_reduce_fusion.2
  357.1 8.7 collective-permute-done.10
  369.2 6.2 all-to-all-start.3
  383.7 4.2 add_convert_fusion.3
  388.4 3.8 add_convert_fusion.1
  393.7 7.3 all-to-all-done.3.g_ref
  401.0 98.0 %attend_back.1 = (bf16[8,512,128]{2,1,0:T(8,128)(2,1)}, f32[16,512,128]{2,1,0:T(8,128)}, bf16[16,512,128]{2,1,0:T(8,128)(2,1)}) custom-call(s32[32]{0:T(128)} %slot_ref.3, s32[8]{0:T(128)} %seq_ref.3, s32[1]{0:T(128)} %bitcast.core_ref, bf16[8,512,128]{2,1,0:T(8,128)(2,1)} %copy-done.26, bf16[8,512,128]{2,1,0:T(8,128)(2,1)} %all-to-all-done.3.g_ref, ...), custom_call_target="tpu_custom_call" | custom-call | flops 13421772800 | bytes 12582912 | tf_op jit(solution)/shard_map/attend_back/pallas_call | solution.py:681
  508.2 5.2 all-to-all-start.4
  517.4 5.0 add_convert_fusion.2
  522.4 4.8 add_convert_fusion
  527.3 4.7 add_convert_fusion.4
  532.0 4.2 copy.47
  536.1 13.4 %all-to-all-done.4 = bf16[8,512,128]{2,1,0:T(8,128)(2,1)} async-done(((bf16[8,512,128]{2,1,0:T(8,128)(2,1)}), bf16[8,512,128]{2,1,0:T(8,128)(2,1)}, u32[]{:S(2)}, u32[]{:S(2)}) %all-to-all-start.4) | async-done | bytes 1048608 | tf_op jit(solution)/shard_map/all_to_all | solution.py:724
  549.5 4.3 all-to-all-start.5
  558.1 97.9 %psum.45 = f32[10240]{0:T(1024)S(1)} all-reduce(f32[10240]{0:T(1024)S(1)} %constant_dynamic-update-slice_fusion), channel_id=1, replica_groups=mesh['chip'=8,'core'=2,'head'=2] {'chip','core','head'}, use_global_device_ids=true, to_apply=%region_22.23 | all-reduce | flops 10240 | bytes 81920 | tf_op jit(solution)/shard_map/psum | solution.py:890
  670.8 71.8 %all-reduce.6.cloned.1.call-done = (bf16[256,1024]{1,0:T(8,128)(2,1)}, bf16[1024,1024]{1,0:T(8,128)(2,1)}, bf16[1024,1024]{1,0:T(8,128)(2,1)}) async-done(((bf16[256,1024]{1,0:T(8,128)(2,1)}, bf16[1024,1024]{1,0:T(8,128)(2,1)}, bf16[1024,1024]{1,0:T(8,128)(2,1)}), (bf16[256,1024]{1,0:T(8,128)(2,1)}, bf16[1024,1024]{1,0:T(8,128)(2,1)}, bf16[1024,1024]{1,0:T(8,128)(2,1)})) %all-reduce.6.cloned.1.call-update) | async-done | bytes 4718608 | tf_op jit(solution)/shard_map/psum | solution.py:858
  742.6 7.1 convolution_convert_fusion
  749.7 4.7 copy.49
  759.2 32.7 %psum.43 = bf16[2,512]{1,0:T(2,128)(2,1)S(1)} all-reduce(bf16[2,512]{1,0:T(2,128)(2,1)S(1)} %pad_maximum_fusion.7), channel_id=1, replica_groups=mesh['chip'=8,'core'=2,'head'=2] {'chip','core'}, use_global_device_ids=true, to_apply=%region_10.11 | all-reduce | flops 1024 | bytes 4096 | tf_op jit(solution)/shard_map/psum | solution.py:921
  792.5 4.4 convert_add_fusion
  799.6 57.9 %all-reduce.4.cloned.1.call-done = bf16[1024,3,512]{2,0,1:T(8,128)(2,1)} async-done(((bf16[1024,3,512]{2,0,1:T(8,128)(2,1)}), bf16[1024,3,512]{2,0,1:T(8,128)(2,1)}) %all-reduce.4.cloned.1.call-update) | async-done | bytes 3145744 | tf_op jit(solution)/shard_map/psum | solution.py:921
  857.5 5.5 reshape.166
  864.8 4.4 maximum_convert_fusion
  871.8 4.5 maximum_convert_fusion.1
  (230 shorter events, 146.7 us)
Async XLA Ops:
  78.6 30.2 %collective-permute-start = (bf16[8,1024,128]{2,1,0:T(8,128)(2,1)S(1)}, bf16[8,1024,128]{2,1,0:T(8,128)(2,1)}, u32[]{:S(2)}, u32[]{:S(2)}) collective-permute-start(bf16[8,1024,128]{2,1,0:T(8,128)(2,1)S(1)} %all_to_all.30), channel_id=1, source_target_pairs={{0,2},{2,0},{1,3},{3,1},{4,6},{6,4},{5,7},{7,5},{8,10},{10,8},{9,1... | collective-permute-start | bytes 6291464 | tf_op jit(solution)/shard_map/ppermute | solution.py:720
  78.6 30.2 %all-to-all-start = ((bf16[8,512,128]{2,1,0:T(8,128)(2,1)}), bf16[8,512,128]{2,1,0:T(8,128)(2,1)S(1)}, u32[]{:S(2)}, u32[]{:S(2)}) async-start(bf16[8,512,128]{2,1,0:T(8,128)(2,1)} %get-tuple-element.22), calls=%async_computation | async-start | bytes 2097152 | tf_op jit(solution)/shard_map/all_to_all | solution.py:724
  85.3 202.1 %collective-permute-start.5 = (bf16[1024,1024]{1,0:T(8,128)(2,1)}, bf16[1024,1024]{1,0:T(8,128)(2,1)}, u32[]{:S(2)}, u32[]{:S(2)}) collective-permute-start(bf16[1024,1024]{1,0:T(8,128)(2,1)} %constant_dynamic-slice_fusion), channel_id=1, source_target_pairs={{0,1},{1,0},{2,3},{3,2},{4,5},{5,4},{6,7},{7,6},{8,9},{9,8},{10,11... | collective-permute-start | bytes 6291464 | tf_op jit(solution)/shard_map/ppermute | solution.py:720
  197.4 29.0 %all-to-all-start.2 = ((bf16[8,512,128]{2,1,0:T(8,128)(2,1)}), bf16[8,512,128]{2,1,0:T(8,128)(2,1)S(1)}, u32[]{:S(2)}, u32[]{:S(2)}) async-start(bf16[8,512,128]{2,1,0:T(8,128)(2,1)} %get-tuple-element.24), calls=%async_computation.2 | async-start | bytes 2097152 | tf_op jit(solution)/shard_map/all_to_all | solution.py:724
  204.2 83.5 %collective-permute-start.3 = (bf16[1024,1024]{1,0:T(8,128)(2,1)}, bf16[1024,1024]{1,0:T(8,128)(2,1)}, u32[]{:S(2)}, u32[]{:S(2)}) collective-permute-start(bf16[1024,1024]{1,0:T(8,128)(2,1)} %constant_dynamic-slice_fusion.1), channel_id=1, source_target_pairs={{0,1},{1,0},{2,3},{3,2},{4,5},{5,4},{6,7},{7,6},{8,9},{9,8},{10,11... | collective-permute-start | bytes 6291464 | tf_op jit(solution)/shard_map/ppermute | solution.py:720
  205.7 82.9 %collective-permute-start.2 = (bf16[512,1024]{1,0:T(8,128)(2,1)S(1)}, bf16[512,1024]{1,0:T(8,128)(2,1)}, u32[]{:S(2)}, u32[]{:S(2)}) collective-permute-start(bf16[512,1024]{1,0:T(8,128)(2,1)S(1)} %copy-done.22), channel_id=1, source_target_pairs={{0,1},{1,0},{2,3},{3,2},{4,5},{5,4},{6,7},{7,6},{8,9},{9,8},{10,11... | collective-permute-start | bytes 3145736 | tf_op jit(solution)/shard_map/ppermute | solution.py:720
  227.2 61.5 %collective-permute-start.1 = (bf16[512,512]{0,1:T(8,128)(2,1)S(1)}, bf16[512,512]{0,1:T(8,128)(2,1)S(1)}, u32[]{:S(2)}, u32[]{:S(2)}) collective-permute-start(bf16[512,512]{0,1:T(8,128)(2,1)S(1)} %dynamic-slice_bitcast_fusion), channel_id=1, source_target_pairs={{0,1},{1,0},{2,3},{3,2},{4,5},{5,4},{6,7},{7,6},{8,9},{9,8},{10,11... | collective-permute-start | bytes 1572872 | tf_op jit(solution)/shard_map/ppermute | solution.py:720
  228.7 55.2 %collective-permute-start.4 = (bf16[1024]{0:T(1024)(128)(2,1)S(1)}, bf16[1024]{0:T(1024)(128)(2,1)S(1)}, u32[]{:S(2)}, u32[]{:S(2)}) collective-permute-start(bf16[1024]{0:T(1024)(128)(2,1)S(1)} %get-tuple-element.46), channel_id=1, source_target_pairs={{0,1},{1,0},{2,3},{3,2},{4,5},{5,4},{6,7},{7,6},{8,9},{9,8},{10,11... | collective-permute-start | bytes 6152 | tf_op jit(solution)/shard_map/ppermute | solution.py:720
  283.9 3.4 collective-permute-start.7
  287.3 23.8 %collective-permute-start.8 = (bf16[1024,1024]{1,0:T(8,128)(2,1)}, bf16[1024,1024]{1,0:T(8,128)(2,1)S(1)}, u32[]{:S(2)}, u32[]{:S(2)}) collective-permute-start(bf16[1024,1024]{1,0:T(8,128)(2,1)} %collective-permute-done.5), channel_id=1, source_target_pairs={{0,2},{2,0},{1,3},{3,1},{4,6},{6,4},{5,7},{7,5},{8,10},{10,8},{9,1... | collective-permute-start | bytes 6291464 | tf_op jit(solution)/shard_map/ppermute | solution.py:720
  287.7 15.9 %collective-permute-start.6 = (bf16[1024,1024]{1,0:T(8,128)(2,1)}, bf16[1024,1024]{1,0:T(8,128)(2,1)S(1)}, u32[]{:S(2)}, u32[]{:S(2)}) collective-permute-start(bf16[1024,1024]{1,0:T(8,128)(2,1)} %collective-permute-done.3), channel_id=1, source_target_pairs={{0,2},{2,0},{1,3},{3,1},{4,6},{6,4},{5,7},{7,5},{8,10},{10,8},{9,1... | collective-permute-start | bytes 6291464 | tf_op jit(solution)/shard_map/ppermute | solution.py:720
  351.5 14.3 %collective-permute-start.10 = (bf16[512,512]{0,1:T(8,128)(2,1)S(1)}, bf16[512,512]{0,1:T(8,128)(2,1)S(1)}, u32[]{:S(2)}, u32[]{:S(2)}) collective-permute-start(bf16[512,512]{0,1:T(8,128)(2,1)S(1)} %convolution_convert_fusion.7), channel_id=1, source_target_pairs={{0,1},{1,0},{2,3},{3,2},{4,5},{5,4},{6,7},{7,6},{8,9},{9,8},{10,11... | collective-permute-start | bytes 1572872 | tf_op jit(solution)/shard_map/ppermute | solution.py:720
  353.1 29.1 %collective-permute-start.18 = (bf16[1024,1024]{1,0:T(8,128)(2,1)}, bf16[1024,1024]{1,0:T(8,128)(2,1)}, u32[]{:S(2)}, u32[]{:S(2)}) collective-permute-start(bf16[1024,1024]{1,0:T(8,128)(2,1)} %convolution_convert_fusion.3), channel_id=1, source_target_pairs={{0,2},{2,0},{1,3},{3,1},{4,6},{6,4},{5,7},{7,5},{8,10},{10,8},{9,1... | collective-permute-start | bytes 6291464 | tf_op jit(solution)/shard_map/ppermute | solution.py:720
  353.2 34.7 %collective-permute-start.22 = (bf16[1024,1024]{1,0:T(8,128)(2,1)}, bf16[1024,1024]{1,0:T(8,128)(2,1)}, u32[]{:S(2)}, u32[]{:S(2)}) collective-permute-start(bf16[1024,1024]{1,0:T(8,128)(2,1)} %convolution_convert_fusion.1), channel_id=1, source_target_pairs={{0,2},{2,0},{1,3},{3,1},{4,6},{6,4},{5,7},{7,5},{8,10},{10,8},{9,1... | collective-permute-start | bytes 6291464 | tf_op jit(solution)/shard_map/ppermute | solution.py:720
  369.2 31.8 %all-to-all-start.3 = ((bf16[8,512,128]{2,1,0:T(8,128)(2,1)}), bf16[8,512,128]{2,1,0:T(8,128)(2,1)}, u32[]{:S(2)}, u32[]{:S(2)}) async-start(bf16[8,512,128]{2,1,0:T(8,128)(2,1)} %copy.44), calls=%async_computation.3 | async-start | bytes 2097152 | tf_op jit(solution)/shard_map/all_to_all | solution.py:724
  377.0 3.5 collective-permute-start.14
  378.4 13.7 %collective-permute-start.13 = (bf16[256,1024]{1,0:T(8,128)(2,1)S(1)}, bf16[256,1024]{1,0:T(8,128)(2,1)}, u32[]{:S(2)}, u32[]{:S(2)}) collective-permute-start(bf16[256,1024]{1,0:T(8,128)(2,1)S(1)} %convolution_convert_fusion.6), channel_id=1, source_target_pairs={{0,2},{2,0},{1,3},{3,1},{4,6},{6,4},{5,7},{7,5},{8,10},{10,8},{9,1... | collective-permute-start | bytes 1572872 | tf_op jit(solution)/shard_map/ppermute | solution.py:720
  379.0 138.3 %collective-permute-start.17 = (bf16[1024,1024]{1,0:T(8,128)(2,1)}, bf16[1024,1024]{1,0:T(8,128)(2,1)}, u32[]{:S(2)}, u32[]{:S(2)}) collective-permute-start(bf16[1024,1024]{1,0:T(8,128)(2,1)} %convolution_convert_fusion.4), channel_id=1, source_target_pairs={{0,2},{2,0},{1,3},{3,1},{4,6},{6,4},{5,7},{7,5},{8,10},{10,8},{9,1... | collective-permute-start | bytes 6291464 | tf_op jit(solution)/shard_map/ppermute | solution.py:720
  380.4 142.0 %collective-permute-start.21 = (bf16[1024,1024]{1,0:T(8,128)(2,1)}, bf16[1024,1024]{1,0:T(8,128)(2,1)}, u32[]{:S(2)}, u32[]{:S(2)}) collective-permute-start(bf16[1024,1024]{1,0:T(8,128)(2,1)} %convolution_convert_fusion.2), channel_id=1, source_target_pairs={{0,2},{2,0},{1,3},{3,1},{4,6},{6,4},{5,7},{7,5},{8,10},{10,8},{9,1... | collective-permute-start | bytes 6291464 | tf_op jit(solution)/shard_map/ppermute | solution.py:720
  382.2 116.9 %collective-permute-start.15 = (bf16[256,1024]{1,0:T(8,128)(2,1)}, bf16[256,1024]{1,0:T(8,128)(2,1)}, u32[]{:S(2)}, u32[]{:S(2)}) collective-permute-start(bf16[256,1024]{1,0:T(8,128)(2,1)} %fusion.42), channel_id=1, source_target_pairs={{0,1},{1,0},{2,3},{3,2},{4,5},{5,4},{6,7},{7,6},{8,9},{9,8},{10,11... | collective-permute-start | bytes 1572872 | tf_op jit(solution)/shard_map/ppermute | solution.py:720
  387.9 129.5 %collective-permute-start.19 = (bf16[1024,1024]{1,0:T(8,128)(2,1)}, bf16[1024,1024]{1,0:T(8,128)(2,1)}, u32[]{:S(2)}, u32[]{:S(2)}) collective-permute-start(bf16[1024,1024]{1,0:T(8,128)(2,1)} %add_convert_fusion.3), channel_id=1, source_target_pairs={{0,1},{1,0},{2,3},{3,2},{4,5},{5,4},{6,7},{7,6},{8,9},{9,8},{10,11... | collective-permute-start | bytes 6291464 | tf_op jit(solution)/shard_map/ppermute | solution.py:720
  392.2 130.2 %collective-permute-start.23 = (bf16[1024,1024]{1,0:T(8,128)(2,1)}, bf16[1024,1024]{1,0:T(8,128)(2,1)}, u32[]{:S(2)}, u32[]{:S(2)}) collective-permute-start(bf16[1024,1024]{1,0:T(8,128)(2,1)} %add_convert_fusion.1), channel_id=1, source_target_pairs={{0,1},{1,0},{2,3},{3,2},{4,5},{5,4},{6,7},{7,6},{8,9},{9,8},{10,11... | collective-permute-start | bytes 6291464 | tf_op jit(solution)/shard_map/ppermute | solution.py:720
  499.1 28.1 %collective-permute-start.11 = (bf16[16,512,128]{2,1,0:T(8,128)(2,1)}, bf16[16,512,128]{2,1,0:T(8,128)(2,1)}, u32[]{:S(2)}, u32[]{:S(2)}) collective-permute-start(bf16[16,512,128]{2,1,0:T(8,128)(2,1)} %get-tuple-element.29), channel_id=1, source_target_pairs={{0,2},{2,0},{1,3},{3,1},{4,6},{6,4},{5,7},{7,5},{8,10},{10,8},{9,1... | collective-permute-start | bytes 6291464 | tf_op jit(solution)/shard_map/ppermute | solution.py:720
  508.2 41.3 %all-to-all-start.4 = ((bf16[8,512,128]{2,1,0:T(8,128)(2,1)}), bf16[8,512,128]{2,1,0:T(8,128)(2,1)}, u32[]{:S(2)}, u32[]{:S(2)}) async-start(bf16[8,512,128]{2,1,0:T(8,128)(2,1)} %get-tuple-element.27), calls=%async_computation.4 | async-start | bytes 2097152 | tf_op jit(solution)/shard_map/all_to_all | solution.py:724
  513.5 229.2 %all-reduce.6.cloned.1.call-start = ((), (), s32[]{:S(2)}) async-start(), calls=%async_computation.7 | async-start | bytes 9437184 | tf_op jit(solution)/shard_map/psum | solution.py:858
  549.5 110.5 %all-to-all-start.5 = ((bf16[8,1024,128]{1,2,0:T(8,128)(2,1)}), bf16[8,1024,128]{1,2,0:T(8,128)(2,1)}, u32[]{:S(2)}, u32[]{:S(2)}) async-start(bf16[8,1024,128]{1,2,0:T(8,128)(2,1)} %copy.47), calls=%async_computation.5 | async-start | bytes 4194304 | tf_op jit(solution)/shard_map/all_to_all | solution.py:724
  553.9 303.6 %all-reduce.4.cloned.1.call-start = ((), (), s32[]{:S(2)}) async-start(), calls=%async_computation.6 | async-start | bytes 6291456 | tf_op jit(solution)/shard_map/psum | solution.py:921
  554.1 200.4 %collective-permute-start.9 = (bf16[512,1024]{1,0:T(8,128)(2,1)}, bf16[512,1024]{1,0:T(8,128)(2,1)}, u32[]{:S(2)}, u32[]{:S(2)}) collective-permute-start(bf16[512,1024]{1,0:T(8,128)(2,1)} %get-tuple-element.51), channel_id=1, source_target_pairs={{0,1},{1,0},{2,3},{3,2},{4,5},{5,4},{6,7},{7,6},{8,9},{9,8},{10,11... | collective-permute-start | bytes 3145736 | tf_op jit(solution)/shard_map/ppermute | solution.py:720
  668.6 123.9 %collective-permute-start.12 = (bf16[1024,512]{1,0:T(8,128)(2,1)}, bf16[1024,512]{1,0:T(8,128)(2,1)}, u32[]{:S(2)}, u32[]{:S(2)}) collective-permute-start(bf16[1024,512]{1,0:T(8,128)(2,1)} %add_convert_fusion.5), channel_id=1, source_target_pairs={{0,1},{1,0},{2,3},{3,2},{4,5},{5,4},{6,7},{7,6},{8,9},{9,8},{10,11... | collective-permute-start | bytes 3145736 | tf_op jit(solution)/shard_map/ppermute | solution.py:720
  742.6 120.3 %collective-permute-start.20 = (bf16[1024,1024]{1,0:T(8,128)(2,1)}, bf16[1024,1024]{1,0:T(8,128)(2,1)}, u32[]{:S(2)}, u32[]{:S(2)}) collective-permute-start(bf16[1024,1024]{1,0:T(8,128)(2,1)} %get-tuple-element.39), channel_id=1, source_target_pairs={{0,2},{2,0},{1,3},{3,1},{4,6},{6,4},{5,7},{7,5},{8,10},{10,8},{9,1... | collective-permute-start | bytes 6291464 | tf_op jit(solution)/shard_map/ppermute | solution.py:720
  758.1 111.2 %collective-permute-start.24 = (bf16[1024,1024]{1,0:T(8,128)(2,1)}, bf16[1024,1024]{1,0:T(8,128)(2,1)}, u32[]{:S(2)}, u32[]{:S(2)}) collective-permute-start(bf16[1024,1024]{1,0:T(8,128)(2,1)} %get-tuple-element.40), channel_id=1, source_target_pairs={{0,2},{2,0},{1,3},{3,1},{4,6},{6,4},{5,7},{7,5},{8,10},{10,8},{9,1... | collective-permute-start | bytes 6291464 | tf_op jit(solution)/shard_map/ppermute | solution.py:720
  759.1 37.8 %collective-permute-start.16 = (bf16[256,1024]{1,0:T(8,128)(2,1)}, bf16[256,1024]{1,0:T(8,128)(2,1)S(1)}, u32[]{:S(2)}, u32[]{:S(2)}) collective-permute-start(bf16[256,1024]{1,0:T(8,128)(2,1)} %get-tuple-element.38), channel_id=1, source_target_pairs={{0,2},{2,0},{1,3},{3,1},{4,6},{6,4},{5,7},{7,5},{8,10},{10,8},{9,1... | collective-permute-start | bytes 1572872 | tf_op jit(solution)/shard_map/ppermute | solution.py:720
  (39 other events, 852.0 us)
Sparse Core Ops, SparseCore 0:
  527.4 215.2 all-reduce.5
Sparse Core Ops, SparseCore 1:
  754.5 102.9 all-reduce.3

commit v2 on v0

--- a/solution.py
+++ b/solution.py
@@ -1,11 +1,16 @@
+import functools
+import math
+
 import jax
 import jax.numpy as jnp
 from jax import lax
+from jax.experimental import pallas as pl
+from jax.experimental.pallas import tpu as pltpu
+from jax.sharding import Mesh
 from jax.sharding import PartitionSpec as P
 
 HD = 64
 CH = 512
-
 
 EPSILON = 1e-05
 
@@ -319,9 +324,1086 @@
     )
 
 
+MAXCH = 6
+LOG2E = 1.4426950408889634
+SCORE = HD ** (-0.5)
+SWAP = [(0, 1), (1, 0)]
+VMEM_LIMIT = 56 * 1024 * 1024
+
+
+def nt(left, right):
+    return lax.dot_general(
+        left, right, (((1,), (1,)), ((), ())), preferred_element_type=jnp.float32
+    )
+
+
+def mm(left, right):
+    return jnp.dot(left, right, preferred_element_type=jnp.float32)
+
+
+def low_half(block):
+    lane = lax.broadcasted_iota(jnp.int32, block.shape, 1)
+    return lane < HD
+
+
+def unfold(packed):
+    wide = packed.astype(jnp.float32)
+    return wide, pltpu.roll(wide, HD, 1)
+
+
+def project_kernel(side_ref, x_ref, wq_ref, wk_ref, wv_ref, bias_ref, kv_ref, far_ref, near_ref):
+    order = pl.program_id(1)
+    rows = x_ref[...]
+    q_all = mm(rows, wq_ref[0]) + bias_ref[0:1, :].astype(jnp.float32)
+    k_all = mm(rows, wk_ref[0])
+    v_all = mm(rows, wv_ref[0]) + bias_ref[1:2, :].astype(jnp.float32)
+    packs = []
+    for pair in range(q_all.shape[1] // 128):
+        cols = slice(pair * 128, pair * 128 + 128)
+        q_pair, k_pair, v_pair = q_all[:, cols], k_all[:, cols], v_all[:, cols]
+        low = low_half(q_pair)
+        kv_ref[2 * pair] = jnp.where(low, k_pair, pltpu.roll(v_pair, HD, 1)).astype(jnp.bfloat16)
+        kv_ref[2 * pair + 1] = jnp.where(low, pltpu.roll(k_pair, HD, 1), v_pair).astype(
+            jnp.bfloat16
+        )
+        top, bottom = q_pair[: CH // 2], q_pair[CH // 2 :]
+        low = low[: CH // 2]
+        packs.append(jnp.where(low, top, pltpu.roll(bottom, HD, 1)).astype(jnp.bfloat16))
+        packs.append(jnp.where(low, pltpu.roll(top, HD, 1), bottom).astype(jnp.bfloat16))
+
+    @pl.when(order == 0)
+    def _():
+        for head, pack in enumerate(packs):
+            far_ref[head] = pack
+
+    @pl.when(order == 1)
+    def _():
+        for head, pack in enumerate(packs):
+            near_ref[head] = pack
+
+
+def project(side, layer_in, weight, bias):
+    width = layer_in.shape[1]
+    heads = weight.shape[2] // HD
+    step = 4
+    groups = heads // step
+    cols = step * HD
+
+    def slot_of(order, side_ref):
+        return (order + side_ref[0] + 1) % 2
+
+    return pl.pallas_call(
+        project_kernel,
+        grid_spec=pltpu.PrefetchScalarGridSpec(
+            num_scalar_prefetch=1,
+            grid=(groups, 2),
+            in_specs=[
+                pl.BlockSpec((CH, width), lambda g, o, side: (slot_of(o, side), 0)),
+                pl.BlockSpec((1, width, cols), lambda g, o, side: (0, 0, g)),
+                pl.BlockSpec((1, width, cols), lambda g, o, side: (1, 0, g)),
+                pl.BlockSpec((1, width, cols), lambda g, o, side: (2, 0, g)),
+                pl.BlockSpec((2, cols), lambda g, o, side: (0, g)),
+            ],
+            out_specs=[
+                pl.BlockSpec((step, CH, 128), lambda g, o, side: (g, slot_of(o, side), 0)),
+                pl.BlockSpec((step, CH // 2, 128), lambda g, o, side: (g, 0, 0)),
+                pl.BlockSpec((step, CH // 2, 128), lambda g, o, side: (g, 0, 0)),
+            ],
+        ),
+        out_shape=[
+            jax.ShapeDtypeStruct((heads, 2 * CH, 128), jnp.bfloat16),
+            jax.ShapeDtypeStruct((heads, CH // 2, 128), jnp.bfloat16),
+            jax.ShapeDtypeStruct((heads, CH // 2, 128), jnp.bfloat16),
+        ],
+        compiler_params=pltpu.CompilerParams(vmem_limit_bytes=VMEM_LIMIT),
+        cost_estimate=pl.CostEstimate(
+            flops=6 * layer_in.size * weight.shape[2],
+            bytes_accessed=2 * (layer_in.size + weight.size) + 6 * layer_in.size,
+            transcendentals=0,
+        ),
+        name="project",
+    )(side, layer_in, weight, weight, weight, bias)
+
+
+def fill_tables(slot_ref, seq_ref, stretch_slot, seq_first, seq_length):
+    def place(slot, carry):
+        stretch_slot[slot_ref[slot]] = slot
+        return carry
+
+    lax.fori_loop(0, slot_ref.shape[0], place, 0)
+
+    def one_sequence(seq, start):
+        length = seq_ref[seq]
+
+        def one_stretch(offset, carry):
+            seq_first[start + offset] = start
+            seq_length[start + offset] = length
+            return carry
+
+        lax.fori_loop(0, length, one_stretch, 0)
+        return start + length
+
+    lax.fori_loop(0, seq_ref.shape[0], one_sequence, jnp.int32(0))
+
+
+def key_index(slot, core, half):
+    own = ((slot >> 1) & 1) == core
+    return jnp.where(own, 0, half) + ((slot >> 2) << 1) + (slot & 1)
+
+
+def load_keys(own_hbm, other_hbm, keys, sem):
+    half = own_hbm.shape[0]
+    first = pltpu.make_async_copy(own_hbm, keys.at[pl.ds(0, half)], sem.at[0])
+    second = pltpu.make_async_copy(other_hbm, keys.at[pl.ds(half, half)], sem.at[1])
+    first.start()
+    second.start()
+    first.wait()
+    second.wait()
+
+
+def my_slot(place_ref, chip):
+    return 4 * chip + 2 * place_ref[0] + place_ref[1]
+
+
+def attend_kernel(
+    slot_ref,
+    seq_ref,
+    place_ref,
+    q_ref,
+    own_hbm,
+    other_hbm,
+    ctx_ref,
+    ctx_t_ref,
+    lse_ref,
+    keys,
+    values_t,
+    held,
+    stretch_slot,
+    seq_first,
+    seq_length,
+    sem,
+):
+    chip = pl.program_id(0)
+    half = own_hbm.shape[0]
+
+    @pl.when(chip == 0)
+    def _():
+        load_keys(own_hbm, other_hbm, keys, sem)
+        fill_tables(slot_ref, seq_ref, stretch_slot, seq_first, seq_length)
+
+        def turn(index, carry):
+            values_t[index] = keys[index].T[HD:128, :]
+            return carry
+
+        lax.fori_loop(0, 2 * half, turn, 0)
+
+    core = place_ref[0]
+    stretch = slot_ref[my_slot(place_ref, chip)]
+    begin, length = seq_first[stretch], seq_length[stretch]
+    part = CH // 2
+    low = low_half(q_ref[0])
+    queries = [jnp.where(low, q, 0.0).astype(jnp.bfloat16) for q in unfold(q_ref[0])]
+
+    def scores(offset, tops):
+        index = key_index(stretch_slot[begin + offset], core, half)
+        block = keys[index]
+        fresh = []
+        for n in range(2):
+            score = nt(block, queries[n]) * (SCORE * LOG2E)
+            held[offset, :, n * part : (n + 1) * part] = score
+            fresh.append(jnp.maximum(tops[n], jnp.max(score.reshape(CH // 8, 8, part), axis=0)))
+        return tuple(fresh)
+
+    lowest = jnp.full((8, part), -3e38, jnp.float32)
+    tops = lax.fori_loop(0, length, scores, (lowest, lowest))
+    tops = [jnp.max(top, axis=0, keepdims=True) for top in tops]
+
+    def step(offset, state):
+        index = key_index(stretch_slot[begin + offset], core, half)
+        block_t = values_t[index]
+        fresh = []
+        for n in range(2):
+            total, acc = state[n]
+            weight = jnp.exp2(held[offset, :, n * part : (n + 1) * part] - tops[n])
+            total = total + jnp.sum(weight.reshape(CH // 8, 8, part), axis=0)
+            acc = acc + mm(block_t, weight.astype(jnp.bfloat16))
+            fresh.append((total, acc))
+        return tuple(fresh)
+
+    start = (jnp.zeros((8, part), jnp.float32), jnp.zeros((HD, part), jnp.float32))
+    final = lax.fori_loop(0, length, step, (start, start))
+    final = [(tops[n], jnp.sum(final[n][0], axis=0, keepdims=True), final[n][1]) for n in range(2)]
+    for n in range(2):
+        top, total, acc = final[n]
+        cols = slice(n * part, (n + 1) * part)
+        context_t = acc / total
+        ctx_t_ref[0, :, cols] = context_t
+        lse_ref[0, :, cols] = top + jnp.log2(total)
+        ctx_ref[0, :, n * HD : (n + 1) * HD] = context_t.T.astype(jnp.bfloat16)
+
+
+def table_scratch(stretches):
+    return [pltpu.SMEM((stretches,), jnp.int32) for _ in range(3)] + [
+        pltpu.SemaphoreType.DMA((2,))
+    ]
+
+
+def attend(slot_stretch, seq_stretches, place, q_pack, own_keys, other_keys):
+    chips = q_pack.shape[0]
+    keys = 2 * own_keys.shape[0]
+    stretches = slot_stretch.shape[0]
+    pairs = chips * 5 * CH * CH
+    return pl.pallas_call(
+        attend_kernel,
+        grid_spec=pltpu.PrefetchScalarGridSpec(
+            num_scalar_prefetch=3,
+            grid=(chips,),
+            in_specs=[
+                pl.BlockSpec((1, CH // 2, 128), lambda z, *_: (z, 0, 0)),
+                pl.BlockSpec(memory_space=pl.ANY),
+                pl.BlockSpec(memory_space=pl.ANY),
+            ],
+            out_specs=[
+                pl.BlockSpec((1, CH // 2, 128), lambda z, *_: (z, 0, 0)),
+                pl.BlockSpec((1, HD, CH), lambda z, *_: (z, 0, 0)),
+                pl.BlockSpec((1, 1, CH), lambda z, *_: (z, 0, 0)),
+            ],
+            scratch_shapes=[
+                pltpu.VMEM((keys, CH, 128), jnp.bfloat16),
+                pltpu.VMEM((keys, HD, CH), jnp.bfloat16),
+                pltpu.VMEM((MAXCH, CH, CH), jnp.float32),
+            ]
+            + table_scratch(stretches),
+        ),
+        out_shape=[
+            jax.ShapeDtypeStruct((chips, CH // 2, 128), jnp.bfloat16),
+            jax.ShapeDtypeStruct((chips, HD, CH), jnp.float32),
+            jax.ShapeDtypeStruct((chips, 1, CH), jnp.float32),
+        ],
+        compiler_params=pltpu.CompilerParams(vmem_limit_bytes=24 * 1024 * 1024),
+        cost_estimate=pl.CostEstimate(
+            flops=HD * pairs, bytes_accessed=16 * q_pack.size, transcendentals=0
+        ),
+        name="attend",
+    )(slot_stretch, seq_stretches, place, q_pack, own_keys, other_keys)
+
+
+def attend_back_kernel(first, slot_ref, seq_ref, place_ref, *refs):
+    q_ref, g_ref, ctx_t_ref, lse_ref, own_hbm, other_hbm = refs[:6]
+    if first:
+        dq_ref, total_ref = refs[6:8]
+    else:
+        total_hbm, dq_ref, own_grad_ref, other_grad_ref = refs[6:10]
+    keys, keys_t, grads, stretch_slot, seq_first, seq_length, sem = refs[-7:]
+    chip = pl.program_id(0)
+    half = own_hbm.shape[0]
+
+    @pl.when(chip == 0)
+    def _():
+        if not first:
+            copy = pltpu.make_async_copy(total_hbm, grads, sem.at[2])
+            copy.start()
+        load_keys(own_hbm, other_hbm, keys, sem)
+        fill_tables(slot_ref, seq_ref, stretch_slot, seq_first, seq_length)
+
+        def turn(index, carry):
+            keys_t[index] = keys[index].T[0:HD, :]
+            if first:
+                grads[index] = jnp.zeros((CH, 128), jnp.float32)
+            return carry
+
+        lax.fori_loop(0, 2 * half, turn, 0)
+        if not first:
+            copy.wait()
+
+    core = place_ref[0]
+    stretch = slot_ref[my_slot(place_ref, chip)]
+    begin, length = seq_first[stretch], seq_length[stretch]
+    part = CH // 2
+    low = low_half(q_ref[0])
+    queries = [jnp.where(low, q, 0.0).astype(jnp.bfloat16) for q in unfold(q_ref[0])]
+    wide, rolled = unfold(g_ref[0])
+    slopes = [jnp.where(low, 0.0, g) for g in (rolled, wide)]
+    delta = [
+        jnp.sum(slopes[n].T[HD:128, :] * ctx_t_ref[0, :, n * part : (n + 1) * part], axis=0)[None]
+        for n in range(2)
+    ]
+    slopes = [g.astype(jnp.bfloat16) for g in slopes]
+    lse = [lse_ref[0, :, n * part : (n + 1) * part] for n in range(2)]
+
+    def step(offset, state):
+        index = key_index(stretch_slot[begin + offset], core, half)
+        block = keys[index]
+        block_t = keys_t[index]
+        fresh = []
+        total = None
+        for n in range(2):
+            score = nt(block, queries[n]) * (SCORE * LOG2E)
+            weight = jnp.exp2(score - lse[n])
+            slope = weight * (nt(block, slopes[n]) - delta[n])
+            slope = slope.astype(jnp.bfloat16)
+            weight = weight.astype(jnp.bfloat16)
+            fresh.append(state[n] + mm(block_t, slope))
+            update = mm(slope, queries[n]) + mm(weight, slopes[n])
+            total = update if total is None else total + update
+        grads[index] += total
+        return tuple(fresh)
+
+    start = tuple(jnp.zeros((HD, part), jnp.float32) for _ in range(2))
+    final = lax.fori_loop(0, length, step, start)
+    for n in range(2):
+        dq_ref[0, :, n * HD : (n + 1) * HD] = (final[n] * SCORE).T.astype(jnp.bfloat16)
+
+    @pl.when(chip == pl.num_programs(0) - 1)
+    def _():
+        if first:
+            copy = pltpu.make_async_copy(grads, total_ref, sem.at[2])
+            copy.start()
+            copy.wait()
+        else:
+            scale = jnp.where(low_half(keys[0]), SCORE, 1.0)
+
+            def leave(index, carry):
+                own_grad_ref[index] = (grads[index] * scale).astype(jnp.bfloat16)
+                other_grad_ref[index] = (grads[half + index] * scale).astype(jnp.bfloat16)
+                return carry
+
+            lax.fori_loop(0, half, leave, 0)
+
+
+def attend_back(tables, place, q_pack, g_pack, ctx_t, lse, own_keys, other_keys, total=None):
+    first = total is None
+    chips = q_pack.shape[0]
+    slots = own_keys.shape[0]
+    stretches = tables[0].shape[0]
+    pairs = chips * 5 * CH * CH
+    pack = pl.BlockSpec((1, CH // 2, 128), lambda z, *_: (z, 0, 0))
+    anywhere = pl.BlockSpec(memory_space=pl.ANY)
+    in_specs = [
+        pack,
+        pack,
+        pl.BlockSpec((1, HD, CH), lambda z, *_: (z, 0, 0)),
+        pl.BlockSpec((1, 1, CH), lambda z, *_: (z, 0, 0)),
+        anywhere,
+        anywhere,
+    ]
+    pack_shape = jax.ShapeDtypeStruct((chips, CH // 2, 128), jnp.bfloat16)
+    if first:
+        out_specs = [pack, anywhere]
+        out_shape = [pack_shape, jax.ShapeDtypeStruct((2 * slots, CH, 128), jnp.float32)]
+    else:
+        in_specs = in_specs + [anywhere]
+        whole = pl.BlockSpec((slots, CH, 128), lambda z, *_: (0, 0, 0))
+        out_specs = [pack, whole, whole]
+        out_shape = [
+            pack_shape,
+            jax.ShapeDtypeStruct((slots, CH, 128), jnp.bfloat16),
+            jax.ShapeDtypeStruct((slots, CH, 128), jnp.bfloat16),
+        ]
+    operands = (q_pack, g_pack, ctx_t, lse, own_keys, other_keys) + (() if first else (total,))
+    return pl.pallas_call(
+        functools.partial(attend_back_kernel, first),
+        grid_spec=pltpu.PrefetchScalarGridSpec(
+            num_scalar_prefetch=3,
+            grid=(chips,),
+            in_specs=in_specs,
+            out_specs=out_specs,
+            scratch_shapes=[
+                pltpu.VMEM((2 * slots, CH, 128), jnp.bfloat16),
+                pltpu.VMEM((2 * slots, HD, CH), jnp.bfloat16),
+                pltpu.VMEM((2 * slots, CH, 128), jnp.float32),
+            ]
+            + table_scratch(stretches)[:3]
+            + [pltpu.SemaphoreType.DMA((3,))],
+        ),
+        out_shape=out_shape,
+        compiler_params=pltpu.CompilerParams(vmem_limit_bytes=36 * 1024 * 1024),
+        cost_estimate=pl.CostEstimate(
+            flops=HD * pairs, bytes_accessed=24 * q_pack.size, transcendentals=0
+        ),
+        name="attend_back",
+    )(*tables, place, *operands)
+
+
+def swap_across(block, axis_name):
+    return lax.ppermute(block, axis_name, SWAP)
+
+
+def spread(block):
+    return lax.all_to_all(block, ("z", "y"), 0, 0, tiled=True)
+
+
+def gelu_both(pre):
+    phi = 0.5 + 0.5 * lax.erf(pre * (2.0**-0.5))
+    density = jnp.exp(-0.5 * pre * pre) * ((2.0 * math.pi) ** -0.5)
+    return ((pre * phi).astype(jnp.bfloat16), phi + pre * density)
+
+
+def tn(left, right):
+    return lax.dot_general(
+        left, right, (((0,), (0,)), ((), ())), preferred_element_type=jnp.float32
+    )
+
+
+BLOCK = 64
+TILE = 256
+
+
+def row_block(step):
+    return pl.ds(pl.multiple_of(step * BLOCK, BLOCK), BLOCK)
+
+
+def weight_slot(part, side):
+    return 2 * (part % 2) + (side if part < 2 else 1 - side)
+
+
+def forward_kernel(side_ref, own_pack, far_pack, layer_in, cotangent, vectors_ref, bias_ref, *refs):
+    up_hbm, down_hbm, out_hbm = refs[0:4], refs[4:8], refs[8:10]
+    out_ref, ctx_ref, first_low, act_ref, slope_ref, second_low, grad_second = refs[10:17]
+    normed_one, inv_one, sums_ref = refs[17:20]
+    ups, downs, outs, rows_in, cot, acc, first_norm, sem = refs[20:]
+    low = jnp.bfloat16
+    width = acc.shape[1]
+    start = pl.multiple_of(side_ref[0] * CH, CH)
+    copies = [
+        pltpu.make_async_copy(layer_in.at[pl.ds(start, CH)], rows_in, sem.at[0]),
+        pltpu.make_async_copy(out_hbm[0], outs.at[0], sem.at[1]),
+        pltpu.make_async_copy(out_hbm[1], outs.at[1], sem.at[2]),
+    ]
+    copies.append(pltpu.make_async_copy(cotangent.at[pl.ds(start, CH)], cot, sem.at[11]))
+    for copy in copies[:3]:
+        copy.start()
+    for n in range(4):
+        slot = weight_slot(n, side_ref[0])
+        pltpu.make_async_copy(up_hbm[n], ups.at[slot], sem.at[3 + 2 * slot]).start()
+        pltpu.make_async_copy(down_hbm[n], downs.at[slot], sem.at[4 + 2 * slot]).start()
+    copies[3].start()
+    out_bias, gain_one, shift_one, down_bias, gain_two, shift_two = (
+        vectors_ref[n : n + 1, :] for n in range(6)
+    )
+    heads = own_pack.shape[0]
+    half = CH // 2
+
+    for source, pack in enumerate((own_pack, far_pack)):
+        for pair in range(heads // 2):
+            first, first_roll = unfold(pack[2 * pair])
+            second, second_roll = unfold(pack[2 * pair + 1])
+            lanes = low_half(first)
+            base = (source * heads // 2 + pair) * 128
+            ctx_ref[0:half, base : base + 128] = jnp.where(lanes, first, second_roll).astype(low)
+            ctx_ref[half:CH, base : base + 128] = jnp.where(lanes, first_roll, second).astype(low)
+    for copy in copies[:3]:
+        copy.wait()
+    span = heads * HD
+    acc[...] = mm(ctx_ref[:, 0:span], outs[0]) + mm(ctx_ref[:, span : 2 * span], outs[1])
+
+    def first_step(step, carry):
+        at = row_block(step)
+        hidden = rows_in[at, :].astype(jnp.float32) + acc[at, :] + out_bias
+        value, normed, inv = norm_forward(hidden, gain_one, shift_one)
+        first_norm[at, :] = value
+        normed_one[at, :] = normed
+        inv_one[at, :] = jnp.broadcast_to(inv, (BLOCK, 128))
+        first_low[at, :] = value.astype(low)
+        return carry
+
+    lax.fori_loop(0, CH // BLOCK, first_step, 0)
+    acc[...] = jnp.zeros(acc.shape, jnp.float32)
+
+    def forward(n, carry):
+        pltpu.make_async_copy(up_hbm[0], ups.at[n], sem.at[3 + 2 * n]).wait()
+        base = pl.multiple_of(n * width, width)
+        for c in range(0, width, TILE):
+            for r in range(0, CH, TILE):
+                rows = slice(r, r + TILE)
+                pre = mm(first_low[rows, :], ups[n, :, c : c + TILE]) + bias_ref[n, :, c : c + TILE]
+                act, slope = gelu_both(pre)
+                act_ref[rows, pl.ds(base + c, TILE)] = act
+                slope_ref[rows, pl.ds(base + c, TILE)] = slope.astype(low)
+        pltpu.make_async_copy(down_hbm[0], downs.at[n], sem.at[4 + 2 * n]).wait()
+        acc[...] += mm(act_ref[:, pl.ds(base, width)], downs[n])
+        return carry
+
+    lax.fori_loop(0, 4, forward, 0)
+    copies[-1].wait()
+    zero = jnp.zeros((1, width), jnp.float32)
+
+    def second_step(step, carry):
+        at = row_block(step)
+        second = first_norm[at, :] + acc[at, :] + down_bias
+        value, normed, inv = norm_forward(second, gain_two, shift_two)
+        out_ref[at, :] = value.astype(low)
+        gradient = cot[at, :].astype(jnp.float32)
+        grad, gain_sum, shift_sum = norm_backward(gradient, normed, inv, gain_two)
+        grad_second[at, :] = grad
+        second_low[at, :] = grad.astype(low)
+        return (
+            carry[0] + jnp.sum(grad, axis=0, keepdims=True),
+            carry[1] + gain_sum[None],
+            carry[2] + shift_sum[None],
+        )
+
+    sums = lax.fori_loop(0, CH // BLOCK, second_step, (zero, zero, zero))
+    for n in range(3):
+        sums_ref[n : n + 1, :] = sums[n]
+
+
+def backward_kernel(side_ref, slope_ref, second_low, grad_second, normed_one, inv_one, gain_ref, *refs):
+    up_hbm, down_hbm, out_hbm = refs[0:4], refs[4:8], refs[8:10]
+    grad_pre_ref, hidden_ref, hidden_low, gc_own, gc_far, sums_ref, bias_grad_ref = refs[10:17]
+    ups, downs, outs, acc, sem = refs[17:]
+    low = jnp.bfloat16
+    width = acc.shape[1]
+    for n in range(4):
+        slot = weight_slot(n, side_ref[0])
+        pltpu.make_async_copy(down_hbm[n], downs.at[slot], sem.at[2 * slot]).start()
+        pltpu.make_async_copy(up_hbm[n], ups.at[slot], sem.at[2 * slot + 1]).start()
+    copies = [pltpu.make_async_copy(out_hbm[n], outs.at[n], sem.at[8 + n]) for n in range(2)]
+    for copy in copies:
+        copy.start()
+    heads = gc_own.shape[0]
+    half = CH // 2
+    acc[...] = jnp.zeros(acc.shape, jnp.float32)
+
+    def backward(n, carry):
+        pltpu.make_async_copy(down_hbm[0], downs.at[n], sem.at[2 * n]).wait()
+        base = pl.multiple_of(n * width, width)
+        for c in range(0, width, TILE):
+            total = None
+            for r in range(0, CH, TILE):
+                rows = slice(r, r + TILE)
+                grad_act = nt(second_low[rows, :], downs[n, c : c + TILE, :])
+                slope = slope_ref[rows, pl.ds(base + c, TILE)].astype(jnp.float32)
+                grad_pre = (grad_act * slope).astype(low)
+                grad_pre_ref[rows, pl.ds(base + c, TILE)] = grad_pre
+                part = jnp.sum(grad_pre.astype(jnp.float32), axis=0, keepdims=True)
+                total = part if total is None else total + part
+            bias_grad_ref[n, :, c : c + TILE] = total
+        pltpu.make_async_copy(up_hbm[0], ups.at[n], sem.at[2 * n + 1]).wait()
+        acc[...] += nt(grad_pre_ref[:, pl.ds(base, width)], ups[n])
+        return carry
+
+    lax.fori_loop(0, 4, backward, 0)
+    zero = jnp.zeros((1, width), jnp.float32)
+    gain_one = gain_ref[...]
+
+    def last_step(step, carry):
+        at = row_block(step)
+        gradient = acc[at, :] + grad_second[at, :]
+        grad, gain_sum, shift_sum = norm_backward(
+            gradient, normed_one[at, :], inv_one[at, 0:1], gain_one
+        )
+        hidden_ref[at, :] = grad
+        hidden_low[at, :] = grad.astype(low)
+        return (
+            carry[0] + jnp.sum(grad, axis=0, keepdims=True),
+            carry[1] + gain_sum[None],
+            carry[2] + shift_sum[None],
+        )
+
+    sums = lax.fori_loop(0, CH // BLOCK, last_step, (zero, zero, zero))
+    for n in range(3):
+        sums_ref[n : n + 1, :] = sums[n]
+    for copy in copies:
+        copy.wait()
+    for source, pack in enumerate((gc_own, gc_far)):
+        for pair in range(heads // 2):
+            both = nt(hidden_low[...], outs[source, pair * 128 : pair * 128 + 128, :])
+            top, bottom = both[:half], both[half:]
+            lanes = low_half(top)
+            pack[2 * pair] = jnp.where(lanes, top, pltpu.roll(bottom, HD, 1)).astype(low)
+            pack[2 * pair + 1] = jnp.where(lanes, pltpu.roll(top, HD, 1), bottom).astype(low)
+
+
+def dense_call(kernel, name, in_specs, operands, weights, shapes, scratch, width):
+    low = jnp.bfloat16
+    vmem, anywhere = pl.BlockSpec(memory_space=pltpu.VMEM), pl.BlockSpec(memory_space=pl.ANY)
+    return pl.pallas_call(
+        kernel,
+        in_specs=in_specs + [anywhere] * 10,
+        out_specs=[vmem] * len(shapes),
+        out_shape=[jax.ShapeDtypeStruct(shape, dtype) for shape, dtype in shapes],
+        scratch_shapes=[
+            pltpu.VMEM((4, width, width), low),
+            pltpu.VMEM((4, width, width), low),
+            pltpu.VMEM((2,) + weights[-1].shape, low),
+        ]
+        + scratch
+        + [pltpu.SemaphoreType.DMA((12,))],
+        compiler_params=pltpu.CompilerParams(vmem_limit_bytes=VMEM_LIMIT),
+        cost_estimate=pl.CostEstimate(
+            flops=8 * CH * width * width, bytes_accessed=8 << 20, transcendentals=0
+        ),
+        name=name,
+    )(*operands, *weights)
+
+
+def forward_rows(side, own_pack, far_pack, layer_in, cotangent, vectors, biases, weights):
+    width = layer_in.shape[1]
+    units = 4 * width
+    low = jnp.bfloat16
+    vmem, anywhere = pl.BlockSpec(memory_space=pltpu.VMEM), pl.BlockSpec(memory_space=pl.ANY)
+    return dense_call(
+        forward_kernel,
+        "forward_rows",
+        [pl.BlockSpec(memory_space=pltpu.SMEM), vmem, vmem, anywhere, anywhere, vmem, vmem],
+        (side, own_pack, far_pack, layer_in, cotangent, vectors, biases),
+        weights,
+        [
+            ((CH, width), low),
+            ((CH, width), low),
+            ((CH, width), low),
+            ((CH, units), low),
+            ((CH, units), low),
+            ((CH, width), low),
+            ((CH, width), jnp.float32),
+            ((CH, width), jnp.float32),
+            ((CH, 128), jnp.float32),
+            ((3, width), jnp.float32),
+        ],
+        [
+            pltpu.VMEM((CH, width), low),
+            pltpu.VMEM((CH, width), low),
+            pltpu.VMEM((CH, width), jnp.float32),
+            pltpu.VMEM((CH, width), jnp.float32),
+        ],
+        width,
+    )
+
+
+def backward_rows(side, slopes, second_low, grad_second, normed_one, inv_one, gain, heads, weights):
+    width = second_low.shape[1]
+    units = 4 * width
+    low = jnp.bfloat16
+    return dense_call(
+        backward_kernel,
+        "backward_rows",
+        [pl.BlockSpec(memory_space=pltpu.SMEM)] + [pl.BlockSpec(memory_space=pltpu.VMEM)] * 6,
+        (side, slopes, second_low, grad_second, normed_one, inv_one, gain),
+        weights,
+        [
+            ((CH, units), low),
+            ((CH, width), jnp.float32),
+            ((CH, width), low),
+            ((heads, CH // 2, 128), low),
+            ((heads, CH // 2, 128), low),
+            ((3, width), jnp.float32),
+            ((4, 1, width), jnp.float32),
+        ],
+        [pltpu.VMEM((CH, width), jnp.float32)],
+        width,
+    )
+
+
+def project_back_kernel(
+    side_ref, near_ref, kv_ref, layer_t, w_ref, hidden_ref, *refs
+):
+    grad_w, far_out, own_out, sums_ref, grad_q, grad_k, grad_v = refs
+    low = jnp.bfloat16
+    side = side_ref[0]
+    half = CH // 2
+    heads = kv_ref.shape[0]
+    near_row = pl.multiple_of(side * CH, CH)
+    far_row = pl.multiple_of((1 - side) * CH, CH)
+    for pair in range(heads // 2):
+        cols = slice(pair * 128, pair * 128 + 128)
+        for pack, base in ((near_ref, near_row), (kv_ref.at[:, 2 * CH :], far_row)):
+            first, first_roll = unfold(pack[2 * pair])
+            second, second_roll = unfold(pack[2 * pair + 1])
+            lanes = low_half(first)
+            grad_q[pl.ds(base, half), cols] = jnp.where(lanes, first, second_roll).astype(low)
+            grad_q[pl.ds(base + half, half), cols] = jnp.where(lanes, first_roll, second).astype(low)
+        for r in range(0, 2 * CH, half):
+            rows = slice(r, r + half)
+            first, first_roll = unfold(kv_ref[2 * pair, rows, :])
+            second, second_roll = unfold(kv_ref[2 * pair + 1, rows, :])
+            lanes = low_half(first)
+            grad_k[rows, cols] = jnp.where(lanes, first, second_roll).astype(low)
+            grad_v[rows, cols] = jnp.where(lanes, first_roll, second).astype(low)
+    parts = (grad_q, grad_k, grad_v)
+    width = layer_t.shape[0]
+    own_width = width // 2
+    near_cols = pl.ds(pl.multiple_of(side * own_width, own_width), own_width)
+    far_cols = pl.ds(pl.multiple_of((1 - side) * own_width, own_width), own_width)
+    far = own = None
+    for n, part in enumerate(parts):
+        far_term, own_term = nt(part[...], w_ref[n, far_cols, :]), nt(part[...], w_ref[n, near_cols, :])
+        far = far_term if far is None else far + far_term
+        own = own_term if own is None else own + own_term
+    far_out[...] = far.astype(low)
+    own_out[...] = own
+    near_rows = pl.ds(near_row, CH)
+    far_out[near_rows, :] = (far_out[near_rows, :].astype(jnp.float32) + hidden_ref[:, far_cols]).astype(low)
+    own_out[near_rows, :] += hidden_ref[:, near_cols]
+    count, _, piece, _ = grad_w.shape
+    for n, part in enumerate(parts):
+        total = mm(layer_t[...], part[...]).astype(low)
+        grad_w[:, n] = total.reshape(count, piece, total.shape[1])
+    sums_ref[0:1, :] = jnp.sum(grad_q[...].astype(jnp.float32), axis=0, keepdims=True)
+    sums_ref[1:2, :] = jnp.sum(grad_v[...].astype(jnp.float32), axis=0, keepdims=True)
+
+
+def project_back(side, near, kv, layer_t, weight, hidden, pieces):
+    heads = kv.shape[0]
+    cols = heads * HD
+    width, rows = layer_t.shape
+    low = jnp.bfloat16
+    vmem = pl.BlockSpec(memory_space=pltpu.VMEM)
+    return pl.pallas_call(
+        project_back_kernel,
+        in_specs=[pl.BlockSpec(memory_space=pltpu.SMEM)] + [vmem] * 5,
+        out_specs=[vmem] * 4,
+        out_shape=[
+            jax.ShapeDtypeStruct((pieces, 3, width // pieces, cols), low),
+            jax.ShapeDtypeStruct((rows, width // 2), low),
+            jax.ShapeDtypeStruct((rows, width // 2), jnp.float32),
+            jax.ShapeDtypeStruct((2, cols), jnp.float32),
+        ],
+        scratch_shapes=[pltpu.VMEM((rows, cols), low)] * 3,
+        compiler_params=pltpu.CompilerParams(vmem_limit_bytes=40 * 1024 * 1024),
+        cost_estimate=pl.CostEstimate(
+            flops=2 * rows * width * cols, bytes_accessed=8 << 20, transcendentals=0
+        ),
+        name="project_back",
+    )(side, near, kv, layer_t, weight, hidden)
+
+
+def fast_local(
+    layer_in,
+    slot_stretch,
+    seq_stretches,
+    w_qkv,
+    qv_bias,
+    w_out,
+    out_bias,
+    norm1_gain,
+    norm1_shift,
+    w_up,
+    up_bias,
+    w_down,
+    down_bias,
+    norm2_gain,
+    norm2_shift,
+    cotangent,
+):
+    width = layer_in.shape[1]
+    cols = w_qkv.shape[2]
+    heads = cols // HD
+    units = w_up.shape[1]
+    half = units // 2
+    side = lax.axis_index("head")
+    core = lax.axis_index("core")
+    far_place = jnp.stack([core, 1 - side]).astype(jnp.int32)
+    near_place = jnp.stack([core, side]).astype(jnp.int32)
+    side_vec = side.reshape(1).astype(jnp.int32)
+    tables = (slot_stretch, seq_stretches)
+    low = jnp.bfloat16
+
+    w_three = w_qkv.transpose(1, 0, 2)
+    layer_t = layer_in.T
+    send_kv, send_far, send_near = project(side_vec, layer_in, w_three, qv_bias)
+    send_kv, w_up, w_down, w_out, up_bias = lax.optimization_barrier(
+        (send_kv, w_up, w_down, w_out, up_bias)
+    )
+    own_kv = spread(send_kv)
+    low_slices = [
+        lax.dynamic_slice_in_dim(array, place * half, half, axis)
+        for array, axis in ((w_up, 1), (w_down, 0), (up_bias, 0))
+        for place in (core, 1 - core)
+    ]
+    up_far = swap_across(low_slices[0], "head")
+    own_kv, low_slices, w_out, up_far = lax.optimization_barrier(
+        (own_kv, low_slices, w_out, up_far)
+    )
+    other_kv = swap_across(own_kv, "core")
+    own_keys = own_kv.reshape(2 * heads, CH, 128)
+    other_keys = other_kv.reshape(2 * heads, CH, 128)
+
+    q_far = spread(send_far)
+    q_near = spread(send_near)
+
+    downs, biases = (
+        (low_slices[n], low_slices[n + 1], swap_across(low_slices[n], "head")) for n in (2, 4)
+    )
+    ups, down_far = low_slices[:2], downs[2]
+    w_out_far = swap_across(w_out, "head")
+    ctx_far, ctx_t_far, lse_far = attend(*tables, far_place, q_far, own_keys, other_keys)
+    q_near, ctx_far, down_far = lax.optimization_barrier((q_near, ctx_far, down_far))
+    ctx_far = swap_across(ctx_far, "head")
+    ctx_near, ctx_t_near, lse_near = attend(*tables, near_place, q_near, own_keys, other_keys)
+
+    def row_major(pack):
+        block = pack.reshape(heads, CH // 2, 2, HD).transpose(2, 1, 0, 3)
+        return block.reshape(CH, cols)
+
+    ctx_other = spread(ctx_far)
+    ctx_near, up_far, down_far, w_out_far, bias_far = lax.optimization_barrier(
+        (ctx_near, up_far, down_far, w_out_far, biases[2])
+    )
+    ctx_own = spread(ctx_near)
+    up_parts = [ups[0], ups[1], up_far, swap_across(up_far, "core")]
+    down_parts = [downs[0], downs[1], down_far, swap_across(down_far, "core")]
+    up_biases = [biases[0], biases[1], bias_far, swap_across(bias_far, "core")]
+    vectors = jnp.stack([out_bias, norm1_gain, norm1_shift, down_bias, norm2_gain, norm2_shift])
+    vectors = vectors.astype(jnp.float32)
+    weights = (*up_parts, *down_parts, w_out, w_out_far)
+    is_low = side == 0
+    own_biases, far_biases = jnp.stack(up_biases[:2]), jnp.stack(up_biases[2:])
+    biases = jnp.stack(
+        [jnp.where(is_low, own_biases, far_biases), jnp.where(is_low, far_biases, own_biases)],
+        axis=1,
+    )
+    (
+        out_rows,
+        ctx_rows,
+        first_low,
+        acts,
+        slopes,
+        second_low,
+        grad_second,
+        normed_one,
+        inv_one,
+        second_sums,
+    ) = forward_rows(
+        side_vec,
+        ctx_own,
+        ctx_other,
+        layer_in,
+        cotangent,
+        vectors,
+        biases.astype(jnp.float32).reshape(4, 1, half),
+        weights,
+    )
+    is_low = side == 0
+
+    is_first = core == 0
+    row = lax.axis_index("y")
+
+    def add_low(kept, got):
+        return (kept.astype(jnp.float32) + got.astype(jnp.float32)).astype(low)
+
+    def on_chip(pair):
+        return add_low(pair[0], swap_across(pair[1].astype(low), "core"))
+
+    def halves(block, bit):
+        size = block.shape[0] // 2
+        return (
+            lax.dynamic_slice_in_dim(block, bit * size, size, 0),
+            lax.dynamic_slice_in_dim(block, (1 - bit) * size, size, 0),
+        )
+
+    def partner(block, step):
+        if step == "y":
+            return swap_across(block, "y")
+        hop = 1 if step == "z_near" else 2
+        return lax.ppermute(block, "z", [(n, n ^ hop) for n in range(lax.axis_size("z"))])
+
+    place_in_z = lax.axis_index("z")
+    bits = {"y": row, "z_near": place_in_z % 2, "z_far": place_in_z // 2}
+
+    def reduce_send(block, step):
+        kept, gone = halves(block, bits[step])
+        return kept, partner(gone, step)
+
+    def reduce_step(block, step):
+        return add_low(*reduce_send(block, step))
+
+    def gather_step(block, step):
+        return in_order(bits[step] == 0, block, partner(block, step), 0)
+
+    def scatter_sum(block):
+        return lax.psum_scatter(block, ("head", "z", "y"), scatter_dimension=0, tiled=True)
+
+    def collect(block):
+        return lax.all_gather(block, ("z", "y"), axis=0, tiled=True)
+
+    def sum_over(vector, steps):
+        for step in steps:
+            if step in ("core", "head"):
+                vector = vector + swap_across(vector, step)
+            else:
+                vector = vector + partner(vector, step)
+        return vector
+
+    def in_order(bit, mine, rest, axis):
+        return jnp.concatenate(
+            [jnp.where(bit, mine, rest), jnp.where(bit, rest, mine)], axis=axis
+        )
+
+    def join(mine, step, axis):
+        rest = partner(mine, step)
+        mine_far, rest_far = swap_across(mine, "core"), swap_across(rest, "core")
+        bit = bits[step] == 0
+        own, other = in_order(bit, mine, rest, 0), in_order(bit, mine_far, rest_far, 0)
+        return in_order(is_first, own, other, axis).astype(jnp.float32)
+
+    half_rows = cols // 2
+
+    def parts_of(block):
+        return [block[:, n * width : (n + 1) * width] for n in range(4)]
+
+    pair = 2 * width
+
+    down_sum = on_chip([tn(acts[:, n : n + pair], second_low) for n in (0, pair)])
+    down_sum = down_sum.reshape(2, width, width)
+    down_own = lax.dynamic_index_in_dim(down_sum, side, 0, keepdims=False)
+    down_far = lax.dynamic_index_in_dim(down_sum, 1 - side, 0, keepdims=False)
+    down_far, grad_second = lax.optimization_barrier((down_far, grad_second))
+    down_got = swap_across(down_far, "head")
+    grad_pres, grad_hidden, hidden_low, gc_own, gc_far, first_sums, bias_grads = backward_rows(
+        side_vec, slopes, second_low, grad_second, normed_one, inv_one, vectors[1:2], heads, weights
+    )
+    gc_in = swap_across(gc_far, "head")
+    g_near = spread(gc_own)
+    def take(block, start, size):
+        return lax.dynamic_slice_in_dim(block, start, size, 1)
+
+    up_own, up_far = (
+        on_chip([tn(first_low, take(grad_pres, (n + place) * width, width)) for n in (0, 2)])
+        for place in (side, 1 - side)
+    )
+    out_own, out_far = (
+        on_chip(
+            [
+                tn(take(ctx_rows, base + which * half_rows, half_rows), hidden_low)
+                for which in (core, 1 - core)
+            ]
+        )
+        for base in (0, cols)
+    )
+
+    def ordered(first, second):
+        return jnp.concatenate(
+            [jnp.where(is_first, first, second), jnp.where(is_first, second, first)]
+        )
+
+    small = jnp.concatenate(
+        [
+            ordered(bias_grads[0, 0], bias_grads[2, 0]),
+            ordered(bias_grads[1, 0], bias_grads[3, 0]),
+            first_sums.reshape(-1),
+            second_sums.reshape(-1),
+        ]
+    )
+    small = small.reshape(-1, 128)
+    small = sum_over(small.reshape(-1, 128), ("core",))
+    down_kept, down_sent = halves(add_low(down_own, down_got), bits["y"])
+    g_near, gc_in, up_far, out_far, small, down_sent = lax.optimization_barrier(
+        (g_near, gc_in, up_far, out_far, small, down_sent)
+    )
+    up_got, out_got = swap_across(up_far, "head"), swap_across(out_far, "head")
+    small_got = swap_across(small, "head")
+    down_got = partner(down_sent, "y")
+    g_far = spread(gc_in)
+    dq_near, part_grad = attend_back(
+        tables, near_place, q_near, g_near, ctx_t_near, lse_near, own_keys, other_keys
+    )
+    part_grad, g_far, down_got, up_got, out_got, small_got = lax.optimization_barrier(
+        (part_grad, g_far, down_got, up_got, out_got, small_got)
+    )
+    both_sum = jnp.concatenate([add_low(up_own, up_got), add_low(out_own, out_got)])
+    down_kept, down_sent = halves(add_low(down_kept, down_got), bits["z_near"])
+    small = small + small_got
+    part_grad, both_sum, small, down_sent = lax.optimization_barrier(
+        (part_grad, both_sum, small, down_sent)
+    )
+    both_sum = lax.psum_scatter(both_sum, ("z", "y"), scatter_dimension=0, tiled=True)
+    small_got = partner(small, "z_near")
+    down_got = partner(down_sent, "z_near")
+    dq_far, own_grad, other_grad = attend_back(
+        tables, far_place, q_far, g_far, ctx_t_far, lse_far, own_keys, other_keys, part_grad
+    )
+    dq_near = spread(dq_near)
+    own_grad, other_grad, dq_far, dq_near, small_got, down_got = lax.optimization_barrier(
+        (own_grad, other_grad, dq_far, dq_near, small_got, down_got)
+    )
+    kv_grad = add_low(own_grad, swap_across(other_grad, "core"))
+    kv_grad = jnp.concatenate([kv_grad.reshape(heads, 2 * CH, 128), dq_far], axis=1)
+    kv_grad, both_sum = lax.optimization_barrier((kv_grad, both_sum))
+    kv_grad = spread(kv_grad)
+    small = small + small_got
+    small_got = partner(small, "y")
+    down_sum = reduce_step(add_low(down_kept, down_got), "z_far")
+    kv_grad, small_got, both_sum, down_sum = lax.optimization_barrier(
+        (kv_grad, small_got, both_sum, down_sum)
+    )
+    both_sum = collect(both_sum)
+    small = small + small_got
+    small_got = partner(small, "z_far")
+    down_sum = gather_step(down_sum, "z_far")
+    deep = lax.axis_size("z")
+    grad_w, far_part, own_part, grad_qv = project_back(
+        side_vec, dq_near, kv_grad, layer_t, w_three, grad_hidden, 4 * deep
+    )
+    arrived = swap_across(far_part, "head")
+    kept, gone = halves(grad_w, core)
+    kept, gone = halves(add_low(kept, swap_across(gone, "core")), row)
+    kept = add_low(kept, swap_across(gone, "y"))
+    pieces = lax.all_to_all(kept, "z", 0, 0, tiled=True)
+    layer_out_pair = jnp.stack([out_rows, swap_across(out_rows, "head")])
+    layer_out = jnp.where(is_low, layer_out_pair, layer_out_pair[::-1]).reshape(2 * CH, width)
+    small = small + small_got
+    down_sum = gather_step(down_sum, "z_near")
+    grad_qv = sum_over(grad_qv.reshape(-1, 128), ("core", "y"))
+    pieces, grad_qv, both_sum, down_sum = lax.optimization_barrier(
+        (pieces, grad_qv, both_sum, down_sum)
+    )
+    mine = jnp.sum(pieces.astype(jnp.float32), axis=0).astype(low)
+    every = lax.all_to_all(jnp.broadcast_to(mine[None], pieces.shape), "z", 0, 0, tiled=True)
+    bit = bits["y"] == 0
+    grad_down = join(down_sum, "y", 0)
+    both_far = swap_across(both_sum, "core")
+    grad_up = in_order(is_first, both_sum[:width], both_far[:width], 1).astype(jnp.float32)
+    grad_out = in_order(is_first, both_sum[width:], both_far[width:], 0).astype(jnp.float32)
+    grad_qv = sum_over(grad_qv, ("z_near", "z_far")).reshape(2, cols)
+    small = small.reshape(-1)
+    grad_up_bias = lax.dynamic_slice_in_dim(small, side * units, units)
+    vectors = small[2 * units : 2 * units + 6 * width].reshape(6, width)
+    every = in_order(bit, every, swap_across(every, "y"), 0)
+    every = in_order(is_first, every, swap_across(every, "core"), 0)
+    grad_qkv = every.astype(jnp.float32).transpose(0, 2, 1, 3).reshape(width, 3, cols)
+    grad_in = own_part + arrived.astype(jnp.float32)
+    return (
+        layer_out,
+        grad_in,
+        grad_qkv,
+        grad_qv,
+        grad_out,
+        vectors[0],
+        vectors[1],
+        vectors[2],
+        grad_up,
+        grad_up_bias,
+        grad_down,
+        vectors[3],
+        vectors[4],
+        vectors[5],
+    )
+
+
 def solution(mesh):
+    batch, head = mesh.shape["batch"], mesh.shape["head"]
+
+    def whole(*arrays):
+        tokens, width = arrays[0].shape
+        heads = arrays[3].shape[2] // head // HD
+        fits = (
+            head == 2
+            and batch == 2 * heads
+            and tokens == batch * 2 * CH
+            and arrays[9].shape[1] % (4 * 128) == 0
+        )
+        if fits:
+            split = Mesh(mesh.devices.reshape(batch // 4, 2, 2, head), ("z", "y", "core", "head"))
+            return run(fast_local, split, ("z", "y", "core"))(*arrays)
+        return run(local, mesh, "batch")(*arrays)
+
+    return whole
+
+
+def run(body, mesh, rows):
     in_specs = (
-        P("batch", None),
+        P(rows, None),
         P(),
         P(),
         P(None, None, "head"),
@@ -336,11 +1418,11 @@
         P(),
         P(),
         P(),
-        P("batch", None),
+        P(rows, None),
     )
     out_specs = (
-        P("batch", None),
-        P("batch", "head"),
+        P(rows, None),
+        P(rows, "head"),
         P(None, None, "head"),
         P(None, "head"),
         P("head", None),
@@ -354,4 +1436,4 @@
         P(),
         P(),
     )
-    return jax.shard_map(local, mesh=mesh, in_specs=in_specs, out_specs=out_specs, check_vma=False)
+    return jax.shard_map(body, mesh=mesh, in_specs=in_specs, out_specs=out_specs, check_vma=False)

time: 1720 us -> 732 us (0.43)
  waiting for transfers between devices: 1050 us -> 254 us
  Pallas kernels: 0 us -> 232 us
  matrix products: 201 us -> 38.7 us
  local copies, waits for them, and re-layouts: 205 us -> 42.7 us
  starting transfers between devices: 1.5 us -> 94.6 us
  loops' own time: 82 us -> 0 us
  blocking collectives: 63 us -> 0 us
  other arithmetic: 97.4 us -> 51.7 us
    psum x4 -> x0, waiting for transfers between devices: 423 us -> none  [the longest x1 169 us: local(): lax.psum(grad_qkv.astype(jnp.bfloat16), 'batch').astype(jnp.float32)]
    reduce_scatter x2 -> x1, waiting for transfers between devices: 397 us -> 15.6 us  [fast_local(): lax.psum_scatter(both_sum, ('z', 'y'), scatter_dimension=0, tiled=True)]
    pallas_call x0 -> x8, Pallas kernels: none -> 232 us  [the longest x2 103 us: attend_back(): pl.pallas_call(functools.partial(attend_back_kernel, first), grid_spec=pl...]
    all_gather x2 -> x1, waiting for transfers between devices: 229 us -> 0.01 us  [collect(): return lax.all_gather(block, ('z', 'y'), axis=0, tiled=True)]
    ppermute x0 -> x43, waiting for transfers between devices: none -> 213 us  [the longest x35 121 us: swap_across(): return lax.ppermute(block, axis_name, SWAP)]
    dot_general x68 -> x10, matrix products: 201 us -> 38.7 us  [tn(): lax.dot_general(left, right, (((0,), (0,)), ((), ())), preferred_element_...]
    while x12 -> x0, local copies, waits for them, and re-layouts: 97.4 us -> none  [the longest x1 51 us: local(): lax.scan(back_slot, key_start, (query_slots, grad_slots, log_totals, delt...]
    another operation x8 -> x0, loops' own time: 82 us -> none  [the longest x2 27.7 us: attend(): row_max, row_total = lax.fori_loop(0, length, norm_step, initial)]
  transfers between devices with their start and end apart: 8 -> 56, of which waited for: 7 -> 19; matrix products, arithmetic and copies ran while one was open for 4% -> 13% of each run, Pallas kernels for 0% -> 27%
where the time goes in v2:
time: 732 us; the launch traced here: 730 us
  waiting for transfers between devices  254 us (35%)
  Pallas kernels  232 us (32%)
  starting transfers between devices  94.6 us (13%)
  other arithmetic  51.7 us (7%)
  local copies, waits for them, and re-layouts  42.7 us (6%)
  matrix products  38.7 us (5%)
  between operations  15.3 us (2%)
    ppermute x35, waiting for transfers between devices, swap_across(): return lax.ppermute(block, axis_name, SWAP)  121 us
    pallas_call x2, Pallas kernels, attend_back(): pl.pallas_call(functools.partial(attend_back_kernel, first), grid_spec=pl...  103 us
    ppermute x8, waiting for transfers between devices, partner(): lax.ppermute(block, 'z', [(n, n ^ hop) for n in range(lax.axis_size('z'))])  91.5 us
    pallas_call x2, Pallas kernels, attend(): pl.pallas_call(attend_kernel, grid_spec=pltpu.PrefetchScalarGridSpec(num_...  61.1 us
    pallas_call x2, Pallas kernels, dense_call(): pl.pallas_call(kernel, in_specs=in_specs + [anywhere] * 10, out_specs=[vm...  49.5 us
    all_to_all x9, starting transfers between devices, spread(): return lax.all_to_all(block, ('z', 'y'), 0, 0, tiled=True)  45.3 us
    dot_general x10, matrix products, tn(): lax.dot_general(left, right, (((0,), (0,)), ((), ())), preferred_element_...  38.7 us
    ppermute x35, starting transfers between devices, swap_across(): return lax.ppermute(block, axis_name, SWAP)  28.4 us
  transfers between devices with their start and end apart: 56, of which 19 were waited for; matrix products, arithmetic and copies ran while one was open for 13% of the time, Pallas kernels for 27%

profile of v2, /device:TPU:0, one launch (start us, length us, event | category | flops | bytes accessed | tf_op | source)
XLA Modules:
  0.0 730.0 jit_solution(4060182915530790782)
XLA Ops:
  7.2 7.9 %project.1 = (bf16[8,1024,128]{2,1,0:T(8,128)(2,1)}, bf16[8,256,128]{2,1,0:T(8,128)(2,1)}, bf16[8,256,128]{2,1,0:T(8,128)(2,1)}) custom-call(s32[1]{0:T(128)} %bitcast.side_ref, bf16[1024,1024]{1,0:T(8,128)(2,1)} %layer_in.1, bf16[3,1024,512]{2,1,0:T(8,128)(2,1)} %bitcast.58, bf16[3,1024,512]{2,1,0:T(8,128)(2,1)} %bitcast.59, ...), custom_call_target="tpu_custom_call" | custom-call | flops 3221225472 | bytes 11534336 | tf_op jit(solution)/shard_map/project/pallas_call | solution.py:395
  15.1 7.3 all-to-all-start.2
  30.5 43.3 %collective-permute-done.refs_2_ = bf16[1024,1024]{1,0:T(8,128)(2,1)} collective-permute-done((bf16[1024,1024]{1,0:T(8,128)(2,1)S(1)}, bf16[1024,1024]{1,0:T(8,128)(2,1)}, u32[]{:S(2)}, u32[]{:S(2)}) %collective-permute-start) | collective-permute-done | bytes 2097184 | tf_op jit(solution)/shard_map/ppermute | solution.py:729
  75.3 5.7 all-to-all-start.1
  81.5 14.3 %all-to-all-done.1.q_ref.refs_0_ = bf16[8,256,128]{2,1,0:T(8,128)(2,1)S(1)} async-done(((bf16[8,256,128]{2,1,0:T(8,128)(2,1)}), bf16[8,256,128]{2,1,0:T(8,128)(2,1)S(1)}, u32[]{:S(2)}, u32[]{:S(2)}) %all-to-all-start.1) | async-done | bytes 524320 | tf_op jit(solution)/shard_map/all_to_all | solution.py:733
  100.2 29.4 %attend.2 = (bf16[8,256,128]{2,1,0:T(8,128)(2,1)S(1)}, f32[8,64,512]{2,1,0:T(8,128)S(1)}, f32[8,1,512]{2,1,0:T(1,128)S(1)}) custom-call(s32[32]{0:T(128)S(1)} %copy-done.16, s32[8]{0:T(128)S(1)} %copy-done.17, s32[2]{0:T(128)S(1)} %pad_add_fusion.1.place_ref, bf16[8,256,128]{2,1,0:T(8,128)(2,1)S(1)} %all-to-all-done.1.q_ref.refs_0_, ...), custom_call_target="tpu_custom_call" | custom-call | flops 671088640 | bytes 4194304 | tf_op jit(solution)/shard_map/attend/pallas_call | solution.py:556
  131.3 31.8 %attend.3 = (bf16[8,256,128]{2,1,0:T(8,128)(2,1)S(1)}, f32[8,64,512]{2,1,0:T(8,128)S(1)}, f32[8,1,512]{2,1,0:T(1,128)S(1)}) custom-call(s32[32]{0:T(128)S(1)} %copy-done.16, s32[8]{0:T(128)S(1)} %copy-done.17, s32[2]{0:T(128)S(1)} %pad_add_fusion.place_ref, bf16[8,256,128]{2,1,0:T(8,128)(2,1)S(1)} %all-to-all-done.q_ref.refs_0_, ...), custom_call_target="tpu_custom_call" | custom-call | flops 671088640 | bytes 4194304 | tf_op jit(solution)/shard_map/attend/pallas_call | solution.py:556
  165.5 5.7 all-to-all-start.3
  172.7 12.5 %collective-permute-done.5 = bf16[8,256,128]{2,1,0:T(8,128)(2,1)} collective-permute-done((bf16[8,256,128]{2,1,0:T(8,128)(2,1)}, bf16[8,256,128]{2,1,0:T(8,128)(2,1)}, u32[]{:S(2)}, u32[]{:S(2)}) %collective-permute-start.5) | collective-permute-done | bytes 524320 | tf_op jit(solution)/shard_map/ppermute | solution.py:729
  186.1 5.1 all-to-all-start.4
  194.0 10.8 %all-to-all-done.4.far_pack = bf16[8,256,128]{2,1,0:T(8,128)(2,1)} async-done(((bf16[8,256,128]{2,1,0:T(8,128)(2,1)}), bf16[8,256,128]{2,1,0:T(8,128)(2,1)}, u32[]{:S(2)}, u32[]{:S(2)}) %all-to-all-start.4) | async-done | bytes 524320 | tf_op jit(solution)/shard_map/all_to_all | solution.py:733
  204.7 27.9 %forward_rows.1 = (bf16[512,1024]{1,0:T(8,128)(2,1)}, bf16[512,1024]{1,0:T(8,128)(2,1)}, bf16[512,1024]{1,0:T(8,128)(2,1)}, bf16[512,4096]{1,0:T(8,128)(2,1)}, b...) custom-call(s32[1]{0:T(128)} %bitcast.side_ref, ...), custom_call_target="tpu_custom_call" | custom-call | flops 4294967296 | bytes 8388608 | tf_op jit(solution)/shard_map/forward_rows/pallas_call | solution.py:921
  232.6 6.3 convolution_convert_fusion
  239.5 6.9 collective-permute-done.10
  246.4 5.5 add_convert_fusion
  256.1 21.6 %backward_rows.1 = (bf16[512,4096]{1,0:T(8,128)(2,1)}, f32[512,1024]{1,0:T(8,128)}, bf16[512,1024]{1,0:T(8,128)(2,1)}, bf16[8,256,128]{2,1,0:T(8,128)(2,1)}, bf1...) custom-call(s32[1]{0:T(128)} %bitcast.side_ref, ...), custom_call_target="tpu_custom_call" | custom-call | flops 4294967296 | bytes 8388608 | tf_op jit(solution)/shard_map/backward_rows/pallas_call | solution.py:921
  299.0 4.4 collective-permute-done.15
  308.0 4.6 add_convert_fusion.4
  326.3 4.8 add_convert_fusion.3
  331.1 52.4 %attend_back.2 = (bf16[8,256,128]{2,1,0:T(8,128)(2,1)S(1)}, f32[32,512,128]{2,1,0:T(8,128)S(1)}) custom-call(s32[32]{0:T(128)S(1)} %copy-done.16, s32[8]{0:T(128)S(1)} %copy-done.17, s32[2]{0:T(128)S(1)} %pad_add_fusion.place_ref, bf16[8,256,128]{2,1,0:T(8,128)(2,1)S(1)} %all-to-all-done.q_ref.refs_0_, bf16[8,256,128]{2,1,0:T(8,128)(2,1)} %all-to-all-done.5.refs_1_, ...), custom_call_target="tpu_custom_call" | custom-call | flops 671088640 | bytes 6291456 | tf_op jit(solution)/shard_map/attend_back/pallas_call | solution.py:704
  397.9 5.9 all-to-all-start.7
  407.1 50.4 %attend_back.3 = (bf16[8,256,128]{2,1,0:T(8,128)(2,1)S(1)}, bf16[16,512,128]{2,1,0:T(8,128)(2,1)S(1)}, bf16[16,512,128]{2,1,0:T(8,128)(2,1)S(1)}) custom-call(s32[32]{0:T(128)S(1)} %copy-done.16, s32[8]{0:T(128)S(1)} %copy-done.17, s32[2]{0:T(128)S(1)} %pad_add_fusion.1.place_ref, bf16[8,256,128]{2,1,0:T(8,128)(2,1)S(1)} %all-to-all-done.1.q_ref.refs_0_, ...), custom_call_target="tpu_custom_call" | custom-call | flops 671088640 | bytes 6291456 | tf_op jit(solution)/shard_map/attend_back/pallas_call | solution.py:704
  470.4 15.6 %reduce-scatter.2.cloned.1.call-done = bf16[160,1024]{1,0:T(8,128)(2,1)} async-done(((bf16[1280,1024]{1,0:T(8,128)(2,1)}), bf16[160,1024]{1,0:T(8,128)(2,1)}) %reduce-scatter.2.cloned.1.call-update) | async-done | bytes 327696 | tf_op jit(solution)/shard_map/reduce_scatter | solution.py:1310
  500.5 59.3 %collective-permute-done.26 = bf16[128,1024]{1,0:T(8,128)(2,1)} collective-permute-done((bf16[128,1024]{1,0:T(8,128)(2,1)S(1)}, bf16[128,1024]{1,0:T(8,128)(2,1)}, u32[]{:S(2)}, u32[]{:S(2)}) %collective-permute-start.26) | collective-permute-done | bytes 262176 | tf_op jit(solution)/shard_map/ppermute | solution.py:1199
  564.1 11.2 %project_back.1 = (bf16[16,3,64,512]{3,2,1,0:T(8,128)(2,1)}, bf16[1024,512]{1,0:T(8,128)(2,1)S(1)}, f32[1024,512]{1,0:T(8,128)S(1)}, f32[2,512]{1,0:T(2,128)S(1)}) custom-call(s32[1]{0:T(128)} %bitcast.side_ref, bf16[8,256,128]{2,1,0:T(8,128)(2,1)S(1)} %copy-done.7, bf16[8,1280,128]{2,1,0:T(8,128)(2,1)S(1)} %all-to-all-done.8.kv_ref, ...), custom_call_target="tpu_custom_call" | custom-call | flops 1073741824 | bytes 8388608 | tf_op jit(solution)/shard_map/project_back/pallas_call | solution.py:1052
  586.2 32.2 %collective-permute-done.29 = bf16[4,3,64,512]{3,2,1,0:T(8,128)(2,1)S(1)} collective-permute-done((bf16[4,3,64,512]{3,2,1,0:T(8,128)(2,1)S(1)}, bf16[4,3,64,512]{3,2,1,0:T(8,128)(2,1)S(1)}, u32[]{:S(2)}, u32[]{:S(2)}) %collective-permute-start.29) | collective-permute-done | bytes 786464 | tf_op jit(solution)/shard_map/ppermute | solution.py:729
  630.8 19.1 %collective-permute-done.33 = bf16[256,1024]{1,0:T(8,128)(2,1)S(1)} collective-permute-done((bf16[256,1024]{1,0:T(8,128)(2,1)S(1)}, bf16[256,1024]{1,0:T(8,128)(2,1)S(1)}, u32[]{:S(2)}, u32[]{:S(2)}) %collective-permute-start.33) | collective-permute-done | bytes 524320 | tf_op jit(solution)/shard_map/ppermute | solution.py:1199
  652.3 5.0 all-to-all-start.10
  666.2 13.1 %collective-permute-done.39 = f32[80,128]{1,0:T(8,128)S(1)} collective-permute-done((f32[80,128]{1,0:T(8,128)S(1)}, f32[80,128]{1,0:T(8,128)S(1)}, u32[]{:S(2)}, u32[]{:S(2)}) %collective-permute-start.39) | collective-permute-done | bytes 40992 | tf_op jit(solution)/shard_map/ppermute | solution.py:1199
  690.6 10.3 %collective-permute-done.34 = bf16[4,3,64,512]{3,2,0,1:T(8,128)(2,1)} collective-permute-done((bf16[4,3,64,512]{3,2,0,1:T(8,128)(2,1)}, bf16[4,3,64,512]{3,2,0,1:T(8,128)(2,1)}, u32[]{:S(2)}, u32[]{:S(2)}) %collective-permute-start.34) | collective-permute-done | bytes 786464 | tf_op jit(solution)/shard_map/ppermute | solution.py:729
  705.3 4.5 maximum_convert_fusion.1
  715.1 4.4 maximum_convert_fusion
  (270 shorter events, 175.6 us)
Async XLA Ops:
  15.1 58.7 %all-to-all-start.2 = ((bf16[8,1024,128]{2,1,0:T(8,128)(2,1)}), bf16[8,1024,128]{2,1,0:T(8,128)(2,1)S(1)}, u32[]{:S(2)}, u32[]{:S(2)}) async-start(bf16[8,1024,128]{2,1,0:T(8,128)(2,1)} %get-tuple-element.108), calls=%async_computation.2 | async-start | bytes 4194304 | tf_op jit(solution)/shard_map/all_to_all | solution.py:733
  26.6 47.2 %collective-permute-start = (bf16[1024,1024]{1,0:T(8,128)(2,1)S(1)}, bf16[1024,1024]{1,0:T(8,128)(2,1)}, u32[]{:S(2)}, u32[]{:S(2)}) collective-permute-start(bf16[1024,1024]{1,0:T(8,128)(2,1)S(1)} %get-tuple-element.126.refs_0_), channel_id=1, source_target_pairs={{0,1},{1,0},{2,3},{3,2},{4,5},{5,4},{6,7},{7,6},{8,9},{9,8},{10,11... | collective-permute-start | bytes 6291464 | tf_op jit(solution)/shard_map/ppermute | solution.py:729
  73.8 26.4 %collective-permute-start.1 = (bf16[8,1024,128]{2,1,0:T(8,128)(2,1)S(1)}, bf16[8,1024,128]{2,1,0:T(8,128)(2,1)}, u32[]{:S(2)}, u32[]{:S(2)}) collective-permute-start(bf16[8,1024,128]{2,1,0:T(8,128)(2,1)S(1)} %all-to-all-done.2), channel_id=1, source_target_pairs={{0,2},{2,0},{1,3},{3,1},{4,6},{6,4},{5,7},{7,5},{8,10},{10,8},{9,1... | collective-permute-start | bytes 6291464 | tf_op jit(solution)/shard_map/ppermute | solution.py:729
  73.8 57.6 %collective-permute-start.2 = (bf16[1024,1024]{1,0:T(8,128)(2,1)}, bf16[1024,1024]{1,0:T(8,128)(2,1)}, u32[]{:S(2)}, u32[]{:S(2)}) collective-permute-start(bf16[1024,1024]{1,0:T(8,128)(2,1)} %get-tuple-element.115.refs_4_), channel_id=1, source_target_pairs={{0,1},{1,0},{2,3},{3,2},{4,5},{5,4},{6,7},{7,6},{8,9},{9,8},{10,11... | collective-permute-start | bytes 6291464 | tf_op jit(solution)/shard_map/ppermute | solution.py:729
  81.0 83.2 %collective-permute-start.3 = (bf16[512,1024]{1,0:T(8,128)(2,1)}, bf16[512,1024]{1,0:T(8,128)(2,1)}, u32[]{:S(2)}, u32[]{:S(2)}) collective-permute-start(bf16[512,1024]{1,0:T(8,128)(2,1)} %refs_8_.1), channel_id=1, source_target_pairs={{0,1},{1,0},{2,3},{3,2},{4,5},{5,4},{6,7},{7,6},{8,9},{9,8},{10,11... | collective-permute-start | bytes 3145736 | tf_op jit(solution)/shard_map/ppermute | solution.py:729
  95.8 35.5 %all-to-all-start = ((bf16[8,256,128]{2,1,0:T(8,128)(2,1)}), bf16[8,256,128]{2,1,0:T(8,128)(2,1)S(1)}, u32[]{:S(2)}, u32[]{:S(2)}) async-start(bf16[8,256,128]{2,1,0:T(8,128)(2,1)} %get-tuple-element.105), calls=%async_computation | async-start | bytes 1048576 | tf_op jit(solution)/shard_map/all_to_all | solution.py:733
  99.6 64.5 %collective-permute-start.4 = (bf16[1024]{0:T(1024)(128)(2,1)S(1)}, bf16[1024]{0:T(1024)(128)(2,1)S(1)}, u32[]{:S(2)}, u32[]{:S(2)}) collective-permute-start(bf16[1024]{0:T(1024)(128)(2,1)S(1)} %get-tuple-element.121), channel_id=1, source_target_pairs={{0,1},{1,0},{2,3},{3,2},{4,5},{5,4},{6,7},{7,6},{8,9},{9,8},{10,11... | collective-permute-start | bytes 6152 | tf_op jit(solution)/shard_map/ppermute | solution.py:729
  164.1 40.6 %collective-permute-start.7 = (bf16[1024,1024]{1,0:T(8,128)(2,1)}, bf16[1024,1024]{1,0:T(8,128)(2,1)}, u32[]{:S(2)}, u32[]{:S(2)}) collective-permute-start(bf16[1024,1024]{1,0:T(8,128)(2,1)} %collective-permute-done.refs_2_), channel_id=1, source_target_pairs={{0,2},{2,0},{1,3},{3,1},{4,6},{6,4},{5,7},{7,5},{8,10},{10,8},{9,1... | collective-permute-start | bytes 6291464 | tf_op jit(solution)/shard_map/ppermute | solution.py:729
  164.8 39.9 %collective-permute-start.8 = (bf16[1024,1024]{1,0:T(8,128)(2,1)}, bf16[1024,1024]{1,0:T(8,128)(2,1)}, u32[]{:S(2)}, u32[]{:S(2)}) collective-permute-start(bf16[1024,1024]{1,0:T(8,128)(2,1)} %collective-permute-done.2.refs_6_), channel_id=1, source_target_pairs={{0,2},{2,0},{1,3},{3,1},{4,6},{6,4},{5,7},{7,5},{8,10},{10,8},{9,1... | collective-permute-start | bytes 6291464 | tf_op jit(solution)/shard_map/ppermute | solution.py:729
  254.6 48.8 %collective-permute-start.15 = (bf16[1024,1024]{1,0:T(8,128)(2,1)}, bf16[1024,1024]{1,0:T(8,128)(2,1)}, u32[]{:S(2)}, u32[]{:S(2)}) collective-permute-start(bf16[1024,1024]{1,0:T(8,128)(2,1)} %dynamic-slice_bitcast_fusion), channel_id=1, source_target_pairs={{0,1},{1,0},{2,3},{3,2},{4,5},{5,4},{6,7},{7,6},{8,9},{9,8},{10,11... | collective-permute-start | bytes 6291464 | tf_op jit(solution)/shard_map/ppermute | solution.py:729
  284.9 28.9 %collective-permute-start.11 = (bf16[8,256,128]{2,1,0:T(8,128)(2,1)}, bf16[8,256,128]{2,1,0:T(8,128)(2,1)}, u32[]{:S(2)}, u32[]{:S(2)}) collective-permute-start(bf16[8,256,128]{2,1,0:T(8,128)(2,1)} %get-tuple-element.141), channel_id=1, source_target_pairs={{0,1},{1,0},{2,3},{3,2},{4,5},{5,4},{6,7},{7,6},{8,9},{9,8},{10,11... | collective-permute-start | bytes 1572872 | tf_op jit(solution)/shard_map/ppermute | solution.py:729
  296.4 28.3 %collective-permute-start.20 = (bf16[1024,1024]{1,0:T(8,128)(2,1)}, bf16[1024,1024]{1,0:T(8,128)(2,1)}, u32[]{:S(2)}, u32[]{:S(2)}) collective-permute-start(bf16[1024,1024]{1,0:T(8,128)(2,1)} %convolution_convert_fusion.1), channel_id=1, source_target_pairs={{0,2},{2,0},{1,3},{3,1},{4,6},{6,4},{5,7},{7,5},{8,10},{10,8},{9,1... | collective-permute-start | bytes 6291464 | tf_op jit(solution)/shard_map/ppermute | solution.py:729
  313.8 73.9 %collective-permute-start.17 = (bf16[1024,1024]{1,0:T(8,128)(2,1)}, bf16[1024,1024]{1,0:T(8,128)(2,1)}, u32[]{:S(2)}, u32[]{:S(2)}) collective-permute-start(bf16[1024,1024]{1,0:T(8,128)(2,1)} %add_convert_fusion.4), channel_id=1, source_target_pairs={{0,1},{1,0},{2,3},{3,2},{4,5},{5,4},{6,7},{7,6},{8,9},{9,8},{10,11... | collective-permute-start | bytes 6291464 | tf_op jit(solution)/shard_map/ppermute | solution.py:729
  315.3 72.4 %collective-permute-start.16 = (bf16[512,1024]{1,0:T(8,128)(2,1)}, bf16[512,1024]{1,0:T(8,128)(2,1)}, u32[]{:S(2)}, u32[]{:S(2)}) collective-permute-start(bf16[512,1024]{1,0:T(8,128)(2,1)} %constant_dynamic-slice_fusion.4), channel_id=1, source_target_pairs={{0,4},{4,0},{1,5},{5,1},{2,6},{6,2},{3,7},{7,3},{8,12},{12,8},{9,1... | collective-permute-start | bytes 3145736 | tf_op jit(solution)/shard_map/ppermute | solution.py:729
  316.8 70.9 %all-to-all-start.6 = ((bf16[8,256,128]{2,1,0:T(8,128)(2,1)}), bf16[8,256,128]{2,1,0:T(8,128)(2,1)}, u32[]{:S(2)}, u32[]{:S(2)}) async-start(bf16[8,256,128]{2,1,0:T(8,128)(2,1)} %collective-permute-done.11), calls=%async_computation.6 | async-start | bytes 1048576 | tf_op jit(solution)/shard_map/all_to_all | solution.py:733
  320.9 165.0 %reduce-scatter.2.cloned.1.call-start = ((), (), s32[]{:S(2)}) async-start(), calls=%async_computation.12 | async-start | bytes 2949120 | tf_op jit(solution)/shard_map/reduce_scatter | solution.py:1310
  321.5 66.2 %collective-permute-start.18 = (bf16[256,1024]{1,0:T(8,128)(2,1)}, bf16[256,1024]{1,0:T(8,128)(2,1)}, u32[]{:S(2)}, u32[]{:S(2)}) collective-permute-start(bf16[256,1024]{1,0:T(8,128)(2,1)} %fusion.3), channel_id=1, source_target_pairs={{0,1},{1,0},{2,3},{3,2},{4,5},{5,4},{6,7},{7,6},{8,9},{9,8},{10,11... | collective-permute-start | bytes 1572872 | tf_op jit(solution)/shard_map/ppermute | solution.py:729
  324.7 69.6 %collective-permute-start.21 = (bf16[256,1024]{1,0:T(8,128)(2,1)}, bf16[256,1024]{1,0:T(8,128)(2,1)}, u32[]{:S(2)}, u32[]{:S(2)}) collective-permute-start(bf16[256,1024]{1,0:T(8,128)(2,1)} %convolution_convert_fusion.3), channel_id=1, source_target_pairs={{0,2},{2,0},{1,3},{3,1},{4,6},{6,4},{5,7},{7,5},{8,10},{10,8},{9,1... | collective-permute-start | bytes 1572872 | tf_op jit(solution)/shard_map/ppermute | solution.py:729
  324.7 63.0 %collective-permute-start.19 = (f32[80,128]{1,0:T(8,128)S(1)}, f32[80,128]{1,0:T(8,128)S(1)}, u32[]{:S(2)}, u32[]{:S(2)}) collective-permute-start(f32[80,128]{1,0:T(8,128)S(1)} %bitcast_add_fusion), channel_id=1, source_target_pairs={{0,1},{1,0},{2,3},{3,2},{4,5},{5,4},{6,7},{7,6},{8,9},{9,8},{10,11... | collective-permute-start | bytes 122888 | tf_op jit(solution)/shard_map/ppermute | solution.py:729
  397.9 63.0 %all-to-all-start.7 = ((bf16[8,256,128]{2,1,0:T(8,128)(2,1)}), bf16[8,256,128]{2,1,0:T(8,128)(2,1)S(1)}, u32[]{:S(2)}, u32[]{:S(2)}) async-start(bf16[8,256,128]{2,1,0:T(8,128)(2,1)} %copy-done.14), calls=%async_computation.7 | async-start | bytes 1048576 | tf_op jit(solution)/shard_map/all_to_all | solution.py:733
  403.8 57.2 %collective-permute-start.23 = (bf16[256,1024]{1,0:T(8,128)(2,1)}, bf16[256,1024]{1,0:T(8,128)(2,1)}, u32[]{:S(2)}, u32[]{:S(2)}) collective-permute-start(bf16[256,1024]{1,0:T(8,128)(2,1)} %constant_dynamic-slice_fusion.3), channel_id=1, source_target_pairs={{0,8},{8,0},{16,24},{24,16},{1,9},{9,1},{17,25},{25,17},{2,10},{10... | collective-permute-start | bytes 1572872 | tf_op jit(solution)/shard_map/ppermute | solution.py:1199
  405.8 55.1 %collective-permute-start.22 = (f32[80,128]{1,0:T(8,128)S(1)}, f32[80,128]{1,0:T(8,128)S(1)}, u32[]{:S(2)}, u32[]{:S(2)}) collective-permute-start(f32[80,128]{1,0:T(8,128)S(1)} %add.190), channel_id=1, source_target_pairs={{0,8},{8,0},{16,24},{24,16},{1,9},{9,1},{17,25},{25,17},{2,10},{10... | collective-permute-start | bytes 122888 | tf_op jit(solution)/shard_map/ppermute | solution.py:1199
  486.0 74.9 %all-to-all-start.8 = ((bf16[8,1280,128]{2,1,0:T(8,128)(2,1)}), bf16[8,1280,128]{2,1,0:T(8,128)(2,1)S(1)}, u32[]{:S(2)}, u32[]{:S(2)}) async-start(bf16[8,1280,128]{2,1,0:T(8,128)(2,1)} %pad_maximum_fusion.1), calls=%async_computation.9 | async-start | bytes 5242880 | tf_op jit(solution)/shard_map/all_to_all | solution.py:733
  489.6 161.6 %all-gather.2.cloned.1.call-start = ((), (), s32[]{:S(2)}) async-start(), calls=%async_computation.13 | async-start | bytes 2949120 | tf_op jit(solution)/shard_map/all_gather | solution.py:1218
  492.1 67.7 %collective-permute-start.26 = (bf16[128,1024]{1,0:T(8,128)(2,1)S(1)}, bf16[128,1024]{1,0:T(8,128)(2,1)}, u32[]{:S(2)}, u32[]{:S(2)}) collective-permute-start(bf16[128,1024]{1,0:T(8,128)(2,1)S(1)} %constant_dynamic-slice_fusion.2), channel_id=1, source_target_pairs={{0,16},{8,24},{16,0},{24,8},{1,17},{9,25},{17,1},{25,9},{2,18},{10... | collective-permute-start | bytes 786440 | tf_op jit(solution)/shard_map/ppermute | solution.py:1199
  498.9 62.0 %collective-permute-start.25 = (f32[80,128]{1,0:T(8,128)S(1)}, f32[80,128]{1,0:T(8,128)S(1)}, u32[]{:S(2)}, u32[]{:S(2)}) collective-permute-start(f32[80,128]{1,0:T(8,128)S(1)} %add.196), channel_id=1, source_target_pairs={{0,4},{4,0},{1,5},{5,1},{2,6},{6,2},{3,7},{7,3},{8,12},{12,8},{9,1... | collective-permute-start | bytes 122888 | tf_op jit(solution)/shard_map/ppermute | solution.py:729
  584.6 33.7 %collective-permute-start.29 = (bf16[4,3,64,512]{3,2,1,0:T(8,128)(2,1)S(1)}, bf16[4,3,64,512]{3,2,1,0:T(8,128)(2,1)S(1)}, u32[]{:S(2)}, u32[]{:S(2)}) collective-permute-start(bf16[4,3,64,512]{3,2,1,0:T(8,128)(2,1)S(1)} %constant_dynamic-slice_fusion), channel_id=1, source_target_pairs={{0,4},{4,0},{1,5},{5,1},{2,6},{6,2},{3,7},{7,3},{8,12},{12,8},{9,1... | collective-permute-start | bytes 2359304 | tf_op jit(solution)/shard_map/ppermute | solution.py:729
  586.1 36.8 %collective-permute-start.32 = (bf16[128,1024]{1,0:T(8,128)(2,1)S(1)}, bf16[128,1024]{1,0:T(8,128)(2,1)}, u32[]{:S(2)}, u32[]{:S(2)}) collective-permute-start(bf16[128,1024]{1,0:T(8,128)(2,1)S(1)} %add_convert_fusion.9), channel_id=1, source_target_pairs={{0,16},{8,24},{16,0},{24,8},{1,17},{9,25},{17,1},{25,9},{2,18},{10... | collective-permute-start | bytes 786440 | tf_op jit(solution)/shard_map/ppermute | solution.py:1199
  619.4 31.8 %all-to-all-start.9 = ((bf16[4,3,64,512]{3,2,1,0:T(8,128)(2,1)}), bf16[4,3,64,512]{3,2,1,0:T(8,128)(2,1)S(1)}, u32[]{:S(2)}, u32[]{:S(2)}) async-start(bf16[4,3,64,512]{3,2,1,0:T(8,128)(2,1)} %add_convert_fusion.7), calls=%async_computation.10 | async-start | bytes 1572864 | tf_op jit(solution)/shard_map/all_to_all | solution.py:1342
  628.7 30.9 %collective-permute-start.9 = (bf16[512,1024]{1,0:T(8,128)(2,1)}, bf16[512,1024]{1,0:T(8,128)(2,1)}, u32[]{:S(2)}, u32[]{:S(2)}) collective-permute-start(bf16[512,1024]{1,0:T(8,128)(2,1)} %get-tuple-element.132), channel_id=1, source_target_pairs={{0,1},{1,0},{2,3},{3,2},{4,5},{5,4},{6,7},{7,6},{8,9},{9,8},{10,11... | collective-permute-start | bytes 3145736 | tf_op jit(solution)/shard_map/ppermute | solution.py:729
  652.3 27.0 %all-to-all-start.10 = ((bf16[4,3,64,512]{3,2,1,0:T(8,128)(2,1)}), bf16[4,3,64,512]{3,2,1,0:T(8,128)(2,1)}, u32[]{:S(2)}, u32[]{:S(2)}) async-start(bf16[4,3,64,512]{3,2,1,0:T(8,128)(2,1)} %broadcast_in_dim.2), calls=%async_computation.11 | async-start | bytes 1572864 | tf_op jit(solution)/shard_map/all_to_all | solution.py:1352
  664.3 45.5 %collective-permute-start.38 = (bf16[1280,1024]{1,0:T(8,128)(2,1)}, bf16[1280,1024]{1,0:T(8,128)(2,1)}, u32[]{:S(2)}, u32[]{:S(2)}) collective-permute-start(bf16[1280,1024]{1,0:T(8,128)(2,1)} %all-gather.2.cloned.1.call-done), channel_id=1, source_target_pairs={{0,2},{2,0},{1,3},{3,1},{4,6},{6,4},{5,7},{7,5},{8,10},{10,8},{9,1... | collective-permute-start | bytes 7864328 | tf_op jit(solution)/shard_map/ppermute | solution.py:729
  (68 other events, 878.2 us)
Sparse Core Ops, SparseCore 0:
  398.0 87.8 reduce-scatter.1
  561.1 68.2 all-gather.1

commit v3 on v2

--- a/solution.py
+++ b/solution.py
@@ -757,7 +757,7 @@
     return 2 * (part % 2) + (side if part < 2 else 1 - side)
 
 
-def forward_kernel(side_ref, own_pack, far_pack, layer_in, cotangent, vectors_ref, bias_ref, *refs):
+def forward_kernel(side_ref, pack_ref, layer_in, cotangent, vectors_ref, bias_ref, *refs):
     up_hbm, down_hbm, out_hbm = refs[0:4], refs[4:8], refs[8:10]
     out_ref, ctx_ref, first_low, act_ref, slope_ref, second_low, grad_second = refs[10:17]
     normed_one, inv_one, sums_ref = refs[17:20]
@@ -781,13 +781,14 @@
     out_bias, gain_one, shift_one, down_bias, gain_two, shift_two = (
         vectors_ref[n : n + 1, :] for n in range(6)
     )
-    heads = own_pack.shape[0]
+    heads = pack_ref.shape[0]
     half = CH // 2
 
-    for source, pack in enumerate((own_pack, far_pack)):
+    for source in range(2):
+        at = slice(source * half, source * half + half)
         for pair in range(heads // 2):
-            first, first_roll = unfold(pack[2 * pair])
-            second, second_roll = unfold(pack[2 * pair + 1])
+            first, first_roll = unfold(pack_ref[2 * pair, at, :])
+            second, second_roll = unfold(pack_ref[2 * pair + 1, at, :])
             lanes = low_half(first)
             base = (source * heads // 2 + pair) * 128
             ctx_ref[0:half, base : base + 128] = jnp.where(lanes, first, second_roll).astype(low)
@@ -938,7 +939,7 @@
     )(*operands, *weights)
 
 
-def forward_rows(side, own_pack, far_pack, layer_in, cotangent, vectors, biases, weights):
+def forward_rows(side, pack, layer_in, cotangent, vectors, biases, weights):
     width = layer_in.shape[1]
     units = 4 * width
     low = jnp.bfloat16
@@ -946,8 +947,8 @@
     return dense_call(
         forward_kernel,
         "forward_rows",
-        [pl.BlockSpec(memory_space=pltpu.SMEM), vmem, vmem, anywhere, anywhere, vmem, vmem],
-        (side, own_pack, far_pack, layer_in, cotangent, vectors, biases),
+        [pl.BlockSpec(memory_space=pltpu.SMEM), vmem, anywhere, anywhere, vmem, vmem],
+        (side, pack, layer_in, cotangent, vectors, biases),
         weights,
         [
             ((CH, width), low),
@@ -1129,18 +1130,17 @@
     w_out_far = swap_across(w_out, "head")
     ctx_far, ctx_t_far, lse_far = attend(*tables, far_place, q_far, own_keys, other_keys)
     q_near, ctx_far, down_far = lax.optimization_barrier((q_near, ctx_far, down_far))
-    ctx_far = swap_across(ctx_far, "head")
+    ctx_other = swap_across(ctx_far, "head")
     ctx_near, ctx_t_near, lse_near = attend(*tables, near_place, q_near, own_keys, other_keys)
 
     def row_major(pack):
         block = pack.reshape(heads, CH // 2, 2, HD).transpose(2, 1, 0, 3)
         return block.reshape(CH, cols)
 
-    ctx_other = spread(ctx_far)
-    ctx_near, up_far, down_far, w_out_far, bias_far = lax.optimization_barrier(
-        (ctx_near, up_far, down_far, w_out_far, biases[2])
-    )
-    ctx_own = spread(ctx_near)
+    ctx_near, ctx_other, up_far, down_far, w_out_far, bias_far = lax.optimization_barrier(
+        (ctx_near, ctx_other, up_far, down_far, w_out_far, biases[2])
+    )
+    ctx_pack = spread(jnp.concatenate([ctx_near, ctx_other], axis=1))
     up_parts = [ups[0], ups[1], up_far, swap_across(up_far, "core")]
     down_parts = [downs[0], downs[1], down_far, swap_across(down_far, "core")]
     up_biases = [biases[0], biases[1], bias_far, swap_across(bias_far, "core")]
@@ -1166,8 +1166,7 @@
         second_sums,
     ) = forward_rows(
         side_vec,
-        ctx_own,
-        ctx_other,
+        ctx_pack,
         layer_in,
         cotangent,
         vectors,
@@ -1324,8 +1323,9 @@
     small = small + small_got
     small_got = partner(small, "y")
     down_sum = reduce_step(add_low(down_kept, down_got), "z_far")
-    kv_grad, small_got, both_sum, down_sum = lax.optimization_barrier(
-        (kv_grad, small_got, both_sum, down_sum)
+    out_other = swap_across(out_rows, "head")
+    kv_grad, small_got, both_sum, down_sum, out_other = lax.optimization_barrier(
+        (kv_grad, small_got, both_sum, down_sum, out_other)
     )
     both_sum = collect(both_sum)
     small = small + small_got
@@ -1340,13 +1340,13 @@
     kept, gone = halves(add_low(kept, swap_across(gone, "core")), row)
     kept = add_low(kept, swap_across(gone, "y"))
     pieces = lax.all_to_all(kept, "z", 0, 0, tiled=True)
-    layer_out_pair = jnp.stack([out_rows, swap_across(out_rows, "head")])
+    layer_out_pair = jnp.stack([out_rows, out_other])
     layer_out = jnp.where(is_low, layer_out_pair, layer_out_pair[::-1]).reshape(2 * CH, width)
     small = small + small_got
     down_sum = gather_step(down_sum, "z_near")
     grad_qv = sum_over(grad_qv.reshape(-1, 128), ("core", "y"))
-    pieces, grad_qv, both_sum, down_sum = lax.optimization_barrier(
-        (pieces, grad_qv, both_sum, down_sum)
+    pieces, grad_qv, both_sum, down_sum, arrived = lax.optimization_barrier(
+        (pieces, grad_qv, both_sum, down_sum, arrived)
     )
     mine = jnp.sum(pieces.astype(jnp.float32), axis=0).astype(low)
     every = lax.all_to_all(jnp.broadcast_to(mine[None], pieces.shape), "z", 0, 0, tiled=True)
@@ -1359,6 +1359,7 @@
     small = small.reshape(-1)
     grad_up_bias = lax.dynamic_slice_in_dim(small, side * units, units)
     vectors = small[2 * units : 2 * units + 6 * width].reshape(6, width)
+    every, grad_up, grad_out = lax.optimization_barrier((every, grad_up, grad_out))
     every = in_order(bit, every, swap_across(every, "y"), 0)
     every = in_order(is_first, every, swap_across(every, "core"), 0)
     grad_qkv = every.astype(jnp.float32).transpose(0, 2, 1, 3).reshape(width, 3, cols)

time: 732 us -> 724 us (0.989)
  blocking collectives: 0 us -> 20.4 us
  waiting for transfers between devices: 254 us -> 235 us
  starting transfers between devices: 94.6 us -> 80.1 us
    all_to_all x0 -> x1, blocking collectives: none -> 20.4 us  [spread(): return lax.all_to_all(block, ('z', 'y'), 0, 0, tiled=True)]
    ppermute x35, waiting for transfers between devices: 121 us -> 108 us  [swap_across(): return lax.ppermute(block, axis_name, SWAP)]
    ppermute x8, waiting for transfers between devices: 91.5 us -> 79.6 us  [partner(): lax.ppermute(block, 'z', [(n, n ^ hop) for n in range(lax.axis_size('z'))])]
    all_to_all x1, waiting for transfers between devices: 0.01 us -> 10.7 us  [fast_local(): lax.all_to_all(jnp.broadcast_to(mine[None], pieces.shape), 'z', 0, 0, til...]
    all_to_all x9 -> x7, starting transfers between devices: 45.3 us -> 35 us  [spread(): return lax.all_to_all(block, ('z', 'y'), 0, 0, tiled=True)]
    all_to_all x9 -> x7, waiting for transfers between devices: 26 us -> 23.3 us  [spread(): return lax.all_to_all(block, ('z', 'y'), 0, 0, tiled=True)]
    unnamed x96 -> x98, local copies, waits for them, and re-layouts: 24.8 us -> 25.7 us
  transfers between devices with their start and end apart: 56 -> 54, of which waited for: 19 -> 18; matrix products, arithmetic and copies ran while one was open for 13% -> 13% of each run, Pallas kernels for 27% -> 27%
where the time goes in v3:
time: 724 us; the launch traced here: 721 us
  waiting for transfers between devices  235 us (32%)
  Pallas kernels  233 us (32%)
  starting transfers between devices  80.1 us (11%)
  other arithmetic  55.2 us (8%)
  local copies, waits for them, and re-layouts  43.4 us (6%)
  matrix products  38.7 us (5%)
  blocking collectives  20.4 us (3%)
  between operations  15.2 us (2%)
    ppermute x35, waiting for transfers between devices, swap_across(): return lax.ppermute(block, axis_name, SWAP)  108 us
    pallas_call x2, Pallas kernels, attend_back(): pl.pallas_call(functools.partial(attend_back_kernel, first), grid_spec=pl...  103 us
    ppermute x8, waiting for transfers between devices, partner(): lax.ppermute(block, 'z', [(n, n ^ hop) for n in range(lax.axis_size('z'))])  79.6 us
    pallas_call x2, Pallas kernels, attend(): pl.pallas_call(attend_kernel, grid_spec=pltpu.PrefetchScalarGridSpec(num_...  61.2 us
    pallas_call x2, Pallas kernels, dense_call(): pl.pallas_call(kernel, in_specs=in_specs + [anywhere] * 10, out_specs=[vm...  49.5 us
    dot_general x10, matrix products, tn(): lax.dot_general(left, right, (((0,), (0,)), ((), ())), preferred_element_...  38.7 us
    all_to_all x7, starting transfers between devices, spread(): return lax.all_to_all(block, ('z', 'y'), 0, 0, tiled=True)  35 us
    ppermute x35, starting transfers between devices, swap_across(): return lax.ppermute(block, axis_name, SWAP)  28 us
  transfers between devices with their start and end apart: 54, of which 18 were waited for; matrix products, arithmetic and copies ran while one was open for 13% of the time, Pallas kernels for 27%

profile of v3, /device:TPU:0, one launch (start us, length us, event | category | flops | bytes accessed | tf_op | source)
XLA Modules:
  0.0 720.8 jit_solution(3543431596474299581)
XLA Ops:
  7.2 7.9 %project.1 = (bf16[8,1024,128]{2,1,0:T(8,128)(2,1)}, bf16[8,256,128]{2,1,0:T(8,128)(2,1)}, bf16[8,256,128]{2,1,0:T(8,128)(2,1)}) custom-call(s32[1]{0:T(128)} %bitcast.side_ref, bf16[1024,1024]{1,0:T(8,128)(2,1)} %layer_in.1, bf16[3,1024,512]{2,1,0:T(8,128)(2,1)} %bitcast.58, bf16[3,1024,512]{2,1,0:T(8,128)(2,1)} %bitcast.59, ...), custom_call_target="tpu_custom_call" | custom-call | flops 3221225472 | bytes 11534336 | tf_op jit(solution)/shard_map/project/pallas_call | solution.py:395
  15.1 7.3 %all-to-all-start.2 = ((bf16[8,1024,128]{2,1,0:T(8,128)(2,1)}), bf16[8,1024,128]{2,1,0:T(8,128)(2,1)S(1)}, u32[]{:S(2)}, u32[]{:S(2)}) async-start(bf16[8,1024,128]{2,1,0:T(8,128)(2,1)} %get-tuple-element.114), calls=%async_computation.2 | async-start | bytes 4194304 | tf_op jit(solution)/shard_map/all_to_all | solution.py:733
  30.5 43.3 %collective-permute-done.refs_2_ = bf16[1024,1024]{1,0:T(8,128)(2,1)} collective-permute-done((bf16[1024,1024]{1,0:T(8,128)(2,1)S(1)}, bf16[1024,1024]{1,0:T(8,128)(2,1)}, u32[]{:S(2)}, u32[]{:S(2)}) %collective-permute-start) | collective-permute-done | bytes 2097184 | tf_op jit(solution)/shard_map/ppermute | solution.py:729
  75.3 20.4 %all_to_all.50.q_ref.refs_0_ = bf16[8,256,128]{2,1,0:T(8,128)(2,1)S(1)} all-to-all(bf16[8,256,128]{2,1,0:T(8,128)(2,1)S(1)} %copy-done.32), channel_id=1, replica_groups=mesh['z'=4,'y'=2,'core'=2,'head'=2] {'z','y'}, dimensions={0} | all-to-all | bytes 1048576 | tf_op jit(solution)/shard_map/all_to_all | solution.py:733
  99.9 28.8 %attend.2 = (bf16[8,256,128]{2,1,0:T(8,128)(2,1)S(1)}, f32[8,64,512]{2,1,0:T(8,128)S(1)}, f32[8,1,512]{2,1,0:T(1,128)S(1)}) custom-call(s32[32]{0:T(128)S(1)} %copy-done.15, s32[8]{0:T(128)S(1)} %copy-done.16, s32[2]{0:T(128)S(1)} %pad_add_fusion.1.place_ref, bf16[8,256,128]{2,1,0:T(8,128)(2,1)S(1)} %all_to_all.50.q_ref.refs_0_, ...), custom_call_target="tpu_custom_call" | custom-call | flops 671088640 | bytes 4194304 | tf_op jit(solution)/shard_map/attend/pallas_call | solution.py:556
  130.5 5.1 collective-permute-start.3
  135.6 32.4 %attend.3 = (bf16[8,256,128]{2,1,0:T(8,128)(2,1)S(1)}, f32[8,64,512]{2,1,0:T(8,128)S(1)}, f32[8,1,512]{2,1,0:T(1,128)S(1)}) custom-call(s32[32]{0:T(128)S(1)} %copy-done.15, s32[8]{0:T(128)S(1)} %copy-done.16, s32[2]{0:T(128)S(1)} %pad_add_fusion.place_ref, bf16[8,256,128]{2,1,0:T(8,128)(2,1)S(1)} %all-to-all-done.q_ref.refs_0_, ...), custom_call_target="tpu_custom_call" | custom-call | flops 671088640 | bytes 4194304 | tf_op jit(solution)/shard_map/attend/pallas_call | solution.py:556
  170.6 6.3 all-to-all-start.3
  179.7 23.3 %all-to-all-done.3.pack_ref = bf16[8,512,128]{2,1,0:T(8,128)(2,1)} async-done(((bf16[8,512,128]{2,1,0:T(8,128)(2,1)}), bf16[8,512,128]{2,1,0:T(8,128)(2,1)}, u32[]{:S(2)}, u32[]{:S(2)}) %all-to-all-start.3) | async-done | bytes 1048608 | tf_op jit(solution)/shard_map/all_to_all | solution.py:733
  203.0 27.9 %forward_rows.1 = (bf16[512,1024]{1,0:T(8,128)(2,1)}, bf16[512,1024]{1,0:T(8,128)(2,1)}, bf16[512,1024]{1,0:T(8,128)(2,1)}, bf16[512,4096]{1,0:T(8,128)(2,1)}, b...) custom-call(s32[1]{0:T(128)} %bitcast.side_ref, ...), custom_call_target="tpu_custom_call" | custom-call | flops 4294967296 | bytes 8388608 | tf_op jit(solution)/shard_map/forward_rows/pallas_call | solution.py:922
  230.9 6.3 convolution_convert_fusion
  237.8 6.9 collective-permute-done.9
  244.6 5.5 add_convert_fusion
  252.8 21.6 %backward_rows.1 = (bf16[512,4096]{1,0:T(8,128)(2,1)}, f32[512,1024]{1,0:T(8,128)}, bf16[512,1024]{1,0:T(8,128)(2,1)}, bf16[8,256,128]{2,1,0:T(8,128)(2,1)}, bf1...) custom-call(s32[1]{0:T(128)} %bitcast.side_ref, ...), custom_call_target="tpu_custom_call" | custom-call | flops 4294967296 | bytes 8388608 | tf_op jit(solution)/shard_map/backward_rows/pallas_call | solution.py:922
  281.7 4.4 collective-permute-start.10
  290.3 4.3 convolution_convert_fusion.1
  297.2 4.4 collective-permute-done.14
  306.2 4.6 add_convert_fusion.4
  323.2 4.8 add_convert_fusion.3
  328.1 53.4 %attend_back.2 = (bf16[8,256,128]{2,1,0:T(8,128)(2,1)S(1)}, f32[32,512,128]{2,1,0:T(8,128)S(1)}) custom-call(s32[32]{0:T(128)S(1)} %copy-done.15, s32[8]{0:T(128)S(1)} %copy-done.16, s32[2]{0:T(128)S(1)} %pad_add_fusion.place_ref, bf16[8,256,128]{2,1,0:T(8,128)(2,1)S(1)} %all-to-all-done.q_ref.refs_0_, bf16[8,256,128]{2,1,0:T(8,128)(2,1)} %all-to-all-done.4.refs_1_, ...), custom_call_target="tpu_custom_call" | custom-call | flops 671088640 | bytes 6291456 | tf_op jit(solution)/shard_map/attend_back/pallas_call | solution.py:704
  395.9 5.9 all-to-all-start.6
  405.1 49.4 %attend_back.3 = (bf16[8,256,128]{2,1,0:T(8,128)(2,1)S(1)}, bf16[16,512,128]{2,1,0:T(8,128)(2,1)S(1)}, bf16[16,512,128]{2,1,0:T(8,128)(2,1)S(1)}) custom-call(s32[32]{0:T(128)S(1)} %copy-done.15, s32[8]{0:T(128)S(1)} %copy-done.16, s32[2]{0:T(128)S(1)} %pad_add_fusion.1.place_ref, bf16[8,256,128]{2,1,0:T(8,128)(2,1)S(1)} %all_to_all.50.q_ref.refs_0_, ...), custom_call_target="tpu_custom_call" | custom-call | flops 671088640 | bytes 6291456 | tf_op jit(solution)/shard_map/attend_back/pallas_call | solution.py:704
  458.0 4.4 collective-permute-done.23
  466.2 13.4 %reduce-scatter.2.cloned.1.call-done = bf16[160,1024]{1,0:T(8,128)(2,1)} async-done(((bf16[1280,1024]{1,0:T(8,128)(2,1)}), bf16[160,1024]{1,0:T(8,128)(2,1)}) %reduce-scatter.2.cloned.1.call-update) | async-done | bytes 327696 | tf_op jit(solution)/shard_map/reduce_scatter | solution.py:1309
  495.6 58.0 %collective-permute-done.25 = bf16[128,1024]{1,0:T(8,128)(2,1)} collective-permute-done((bf16[128,1024]{1,0:T(8,128)(2,1)S(1)}, bf16[128,1024]{1,0:T(8,128)(2,1)}, u32[]{:S(2)}, u32[]{:S(2)}) %collective-permute-start.25) | collective-permute-done | bytes 262176 | tf_op jit(solution)/shard_map/ppermute | solution.py:1198
  557.9 11.2 %project_back.1 = (bf16[16,3,64,512]{3,2,1,0:T(8,128)(2,1)}, bf16[1024,512]{1,0:T(8,128)(2,1)S(1)}, f32[1024,512]{1,0:T(8,128)S(1)}, f32[2,512]{1,0:T(2,128)S(1)}) custom-call(s32[1]{0:T(128)} %bitcast.side_ref, bf16[8,256,128]{2,1,0:T(8,128)(2,1)S(1)} %copy-done.7, bf16[8,1280,128]{2,1,0:T(8,128)(2,1)S(1)} %all-to-all-done.7.kv_ref, ...), custom_call_target="tpu_custom_call" | custom-call | flops 1073741824 | bytes 8388608 | tf_op jit(solution)/shard_map/project_back/pallas_call | solution.py:1053
  582.8 31.0 %collective-permute-done.28 = bf16[4,3,64,512]{3,2,1,0:T(8,128)(2,1)} collective-permute-done((bf16[4,3,64,512]{3,2,1,0:T(8,128)(2,1)}, bf16[4,3,64,512]{3,2,1,0:T(8,128)(2,1)}, u32[]{:S(2)}, u32[]{:S(2)}) %collective-permute-start.28) | collective-permute-done | bytes 786464 | tf_op jit(solution)/shard_map/ppermute | solution.py:729
  627.4 18.2 %collective-permute-done.32 = bf16[256,1024]{1,0:T(8,128)(2,1)S(1)} collective-permute-done((bf16[256,1024]{1,0:T(8,128)(2,1)}, bf16[256,1024]{1,0:T(8,128)(2,1)S(1)}, u32[]{:S(2)}, u32[]{:S(2)}) %collective-permute-start.32) | collective-permute-done | bytes 524320 | tf_op jit(solution)/shard_map/ppermute | solution.py:1198
  655.5 4.4 maximum_convert_fusion
  662.8 10.7 %all-to-all-done.9 = bf16[4,3,64,512]{3,2,1,0:T(8,128)(2,1)S(1)} async-done(((bf16[4,3,64,512]{3,2,1,0:T(8,128)(2,1)}), bf16[4,3,64,512]{3,2,1,0:T(8,128)(2,1)S(1)}, u32[]{:S(2)}, u32[]{:S(2)}) %all-to-all-start.9) | async-done | bytes 786464 | tf_op jit(solution)/shard_map/all_to_all | solution.py:1352
  684.6 8.7 %collective-permute-done.35 = bf16[4,3,64,512]{3,2,0,1:T(8,128)(2,1)} collective-permute-done((bf16[4,3,64,512]{3,2,0,1:T(8,128)(2,1)}, bf16[4,3,64,512]{3,2,0,1:T(8,128)(2,1)}, u32[]{:S(2)}, u32[]{:S(2)}) %collective-permute-start.35) | collective-permute-done | bytes 786464 | tf_op jit(solution)/shard_map/ppermute | solution.py:729
  704.5 4.5 maximum_convert_fusion.1
  (270 shorter events, 167.3 us)
Async XLA Ops:
  15.1 58.7 %all-to-all-start.2 = ((bf16[8,1024,128]{2,1,0:T(8,128)(2,1)}), bf16[8,1024,128]{2,1,0:T(8,128)(2,1)S(1)}, u32[]{:S(2)}, u32[]{:S(2)}) async-start(bf16[8,1024,128]{2,1,0:T(8,128)(2,1)} %get-tuple-element.114), calls=%async_computation.2 | async-start | bytes 4194304 | tf_op jit(solution)/shard_map/all_to_all | solution.py:733
  26.6 47.2 %collective-permute-start = (bf16[1024,1024]{1,0:T(8,128)(2,1)S(1)}, bf16[1024,1024]{1,0:T(8,128)(2,1)}, u32[]{:S(2)}, u32[]{:S(2)}) collective-permute-start(bf16[1024,1024]{1,0:T(8,128)(2,1)S(1)} %get-tuple-element.133.refs_0_), channel_id=1, source_target_pairs={{0,1},{1,0},{2,3},{3,2},{4,5},{5,4},{6,7},{7,6},{8,9},{9,8},{10,11... | collective-permute-start | bytes 6291464 | tf_op jit(solution)/shard_map/ppermute | solution.py:729
  73.8 56.7 %collective-permute-start.2 = (bf16[1024,1024]{1,0:T(8,128)(2,1)}, bf16[1024,1024]{1,0:T(8,128)(2,1)}, u32[]{:S(2)}, u32[]{:S(2)}) collective-permute-start(bf16[1024,1024]{1,0:T(8,128)(2,1)} %get-tuple-element.121.refs_4_), channel_id=1, source_target_pairs={{0,1},{1,0},{2,3},{3,2},{4,5},{5,4},{6,7},{7,6},{8,9},{9,8},{10,11... | collective-permute-start | bytes 6291464 | tf_op jit(solution)/shard_map/ppermute | solution.py:729
  95.6 34.8 %all-to-all-start = ((bf16[8,256,128]{2,1,0:T(8,128)(2,1)}), bf16[8,256,128]{2,1,0:T(8,128)(2,1)S(1)}, u32[]{:S(2)}, u32[]{:S(2)}) async-start(bf16[8,256,128]{2,1,0:T(8,128)(2,1)} %get-tuple-element.111), calls=%async_computation | async-start | bytes 1048576 | tf_op jit(solution)/shard_map/all_to_all | solution.py:733
  99.3 69.7 %collective-permute-start.4 = (bf16[512,1024]{1,0:T(8,128)(2,1)}, bf16[512,1024]{1,0:T(8,128)(2,1)}, u32[]{:S(2)}, u32[]{:S(2)}) collective-permute-start(bf16[512,1024]{1,0:T(8,128)(2,1)} %refs_8_.1), channel_id=1, source_target_pairs={{0,1},{1,0},{2,3},{3,2},{4,5},{5,4},{6,7},{7,6},{8,9},{9,8},{10,11... | collective-permute-start | bytes 3145736 | tf_op jit(solution)/shard_map/ppermute | solution.py:729
  130.5 38.5 %collective-permute-start.3 = (bf16[8,256,128]{2,1,0:T(8,128)(2,1)}, bf16[8,256,128]{2,1,0:T(8,128)(2,1)S(1)}, u32[]{:S(2)}, u32[]{:S(2)}) collective-permute-start(bf16[8,256,128]{2,1,0:T(8,128)(2,1)} %copy-done.20), channel_id=1, source_target_pairs={{0,1},{1,0},{2,3},{3,2},{4,5},{5,4},{6,7},{7,6},{8,9},{9,8},{10,11... | collective-permute-start | bytes 1572872 | tf_op jit(solution)/shard_map/ppermute | solution.py:729
  135.6 33.4 %collective-permute-start.5 = (bf16[1024]{0:T(1024)(128)(2,1)S(1)}, bf16[1024]{0:T(1024)(128)(2,1)S(1)}, u32[]{:S(2)}, u32[]{:S(2)}) collective-permute-start(bf16[1024]{0:T(1024)(128)(2,1)S(1)} %get-tuple-element.128), channel_id=1, source_target_pairs={{0,1},{1,0},{2,3},{3,2},{4,5},{5,4},{6,7},{7,6},{8,9},{9,8},{10,11... | collective-permute-start | bytes 6152 | tf_op jit(solution)/shard_map/ppermute | solution.py:729
  169.0 33.9 %collective-permute-start.7 = (bf16[1024,1024]{1,0:T(8,128)(2,1)}, bf16[1024,1024]{1,0:T(8,128)(2,1)}, u32[]{:S(2)}, u32[]{:S(2)}) collective-permute-start(bf16[1024,1024]{1,0:T(8,128)(2,1)} %collective-permute-done.refs_2_), channel_id=1, source_target_pairs={{0,2},{2,0},{1,3},{3,1},{4,6},{6,4},{5,7},{7,5},{8,10},{10,8},{9,1... | collective-permute-start | bytes 6291464 | tf_op jit(solution)/shard_map/ppermute | solution.py:729
  169.1 33.9 %collective-permute-start.8 = (bf16[1024,1024]{1,0:T(8,128)(2,1)}, bf16[1024,1024]{1,0:T(8,128)(2,1)}, u32[]{:S(2)}, u32[]{:S(2)}) collective-permute-start(bf16[1024,1024]{1,0:T(8,128)(2,1)} %collective-permute-done.2.refs_6_), channel_id=1, source_target_pairs={{0,2},{2,0},{1,3},{3,1},{4,6},{6,4},{5,7},{7,5},{8,10},{10,8},{9,1... | collective-permute-start | bytes 6291464 | tf_op jit(solution)/shard_map/ppermute | solution.py:729
  170.6 32.3 %all-to-all-start.3 = ((bf16[8,512,128]{2,1,0:T(8,128)(2,1)}), bf16[8,512,128]{2,1,0:T(8,128)(2,1)}, u32[]{:S(2)}, u32[]{:S(2)}) async-start(bf16[8,512,128]{2,1,0:T(8,128)(2,1)} %pad_maximum_fusion.6), calls=%async_computation.3 | async-start | bytes 2097152 | tf_op jit(solution)/shard_map/all_to_all | solution.py:733
  252.8 48.8 %collective-permute-start.14 = (bf16[1024,1024]{1,0:T(8,128)(2,1)}, bf16[1024,1024]{1,0:T(8,128)(2,1)}, u32[]{:S(2)}, u32[]{:S(2)}) collective-permute-start(bf16[1024,1024]{1,0:T(8,128)(2,1)} %dynamic-slice_bitcast_fusion), channel_id=1, source_target_pairs={{0,1},{1,0},{2,3},{3,2},{4,5},{5,4},{6,7},{7,6},{8,9},{9,8},{10,11... | collective-permute-start | bytes 6291464 | tf_op jit(solution)/shard_map/ppermute | solution.py:729
  281.7 30.3 %collective-permute-start.10 = (bf16[8,256,128]{2,1,0:T(8,128)(2,1)}, bf16[8,256,128]{2,1,0:T(8,128)(2,1)}, u32[]{:S(2)}, u32[]{:S(2)}) collective-permute-start(bf16[8,256,128]{2,1,0:T(8,128)(2,1)} %get-tuple-element.148), channel_id=1, source_target_pairs={{0,1},{1,0},{2,3},{3,2},{4,5},{5,4},{6,7},{7,6},{8,9},{9,8},{10,11... | collective-permute-start | bytes 1572872 | tf_op jit(solution)/shard_map/ppermute | solution.py:729
  312.1 73.7 %collective-permute-start.16 = (bf16[1024,1024]{1,0:T(8,128)(2,1)}, bf16[1024,1024]{1,0:T(8,128)(2,1)}, u32[]{:S(2)}, u32[]{:S(2)}) collective-permute-start(bf16[1024,1024]{1,0:T(8,128)(2,1)} %add_convert_fusion.4), channel_id=1, source_target_pairs={{0,1},{1,0},{2,3},{3,2},{4,5},{5,4},{6,7},{7,6},{8,9},{9,8},{10,11... | collective-permute-start | bytes 6291464 | tf_op jit(solution)/shard_map/ppermute | solution.py:729
  312.3 73.4 %collective-permute-start.15 = (bf16[512,1024]{1,0:T(8,128)(2,1)}, bf16[512,1024]{1,0:T(8,128)(2,1)}, u32[]{:S(2)}, u32[]{:S(2)}) collective-permute-start(bf16[512,1024]{1,0:T(8,128)(2,1)} %constant_dynamic-slice_fusion.4), channel_id=1, source_target_pairs={{0,4},{4,0},{1,5},{5,1},{2,6},{6,2},{3,7},{7,3},{8,12},{12,8},{9,1... | collective-permute-start | bytes 3145736 | tf_op jit(solution)/shard_map/ppermute | solution.py:729
  313.8 72.0 %all-to-all-start.5 = ((bf16[8,256,128]{2,1,0:T(8,128)(2,1)}), bf16[8,256,128]{2,1,0:T(8,128)(2,1)}, u32[]{:S(2)}, u32[]{:S(2)}) async-start(bf16[8,256,128]{2,1,0:T(8,128)(2,1)} %collective-permute-done.10), calls=%async_computation.5 | async-start | bytes 1048576 | tf_op jit(solution)/shard_map/all_to_all | solution.py:733
  317.9 161.7 %reduce-scatter.2.cloned.1.call-start = ((), (), s32[]{:S(2)}) async-start(), calls=%async_computation.11 | async-start | bytes 2949120 | tf_op jit(solution)/shard_map/reduce_scatter | solution.py:1309
  318.5 67.3 %collective-permute-start.17 = (bf16[256,1024]{1,0:T(8,128)(2,1)}, bf16[256,1024]{1,0:T(8,128)(2,1)}, u32[]{:S(2)}, u32[]{:S(2)}) collective-permute-start(bf16[256,1024]{1,0:T(8,128)(2,1)} %fusion.3), channel_id=1, source_target_pairs={{0,1},{1,0},{2,3},{3,2},{4,5},{5,4},{6,7},{7,6},{8,9},{9,8},{10,11... | collective-permute-start | bytes 1572872 | tf_op jit(solution)/shard_map/ppermute | solution.py:729
  322.9 69.4 %collective-permute-start.20 = (bf16[256,1024]{1,0:T(8,128)(2,1)}, bf16[256,1024]{1,0:T(8,128)(2,1)}, u32[]{:S(2)}, u32[]{:S(2)}) collective-permute-start(bf16[256,1024]{1,0:T(8,128)(2,1)} %convolution_convert_fusion.3), channel_id=1, source_target_pairs={{0,2},{2,0},{1,3},{3,1},{4,6},{6,4},{5,7},{7,5},{8,10},{10,8},{9,1... | collective-permute-start | bytes 1572872 | tf_op jit(solution)/shard_map/ppermute | solution.py:729
  322.9 62.8 %collective-permute-start.18 = (f32[80,128]{1,0:T(8,128)S(1)}, f32[80,128]{1,0:T(8,128)S(1)}, u32[]{:S(2)}, u32[]{:S(2)}) collective-permute-start(f32[80,128]{1,0:T(8,128)S(1)} %bitcast_add_fusion), channel_id=1, source_target_pairs={{0,1},{1,0},{2,3},{3,2},{4,5},{5,4},{6,7},{7,6},{8,9},{9,8},{10,11... | collective-permute-start | bytes 122888 | tf_op jit(solution)/shard_map/ppermute | solution.py:729
  395.9 62.0 %all-to-all-start.6 = ((bf16[8,256,128]{2,1,0:T(8,128)(2,1)}), bf16[8,256,128]{2,1,0:T(8,128)(2,1)S(1)}, u32[]{:S(2)}, u32[]{:S(2)}) async-start(bf16[8,256,128]{2,1,0:T(8,128)(2,1)} %copy-done.14), calls=%async_computation.6 | async-start | bytes 1048576 | tf_op jit(solution)/shard_map/all_to_all | solution.py:733
  401.8 56.1 %collective-permute-start.22 = (bf16[256,1024]{1,0:T(8,128)(2,1)}, bf16[256,1024]{1,0:T(8,128)(2,1)}, u32[]{:S(2)}, u32[]{:S(2)}) collective-permute-start(bf16[256,1024]{1,0:T(8,128)(2,1)} %constant_dynamic-slice_fusion.3), channel_id=1, source_target_pairs={{0,8},{8,0},{16,24},{24,16},{1,9},{9,1},{17,25},{25,17},{2,10},{10... | collective-permute-start | bytes 1572872 | tf_op jit(solution)/shard_map/ppermute | solution.py:1198
  403.8 54.1 %collective-permute-start.21 = (f32[80,128]{1,0:T(8,128)S(1)}, f32[80,128]{1,0:T(8,128)S(1)}, u32[]{:S(2)}, u32[]{:S(2)}) collective-permute-start(f32[80,128]{1,0:T(8,128)S(1)} %add.190), channel_id=1, source_target_pairs={{0,8},{8,0},{16,24},{24,16},{1,9},{9,1},{17,25},{25,17},{2,10},{10... | collective-permute-start | bytes 122888 | tf_op jit(solution)/shard_map/ppermute | solution.py:1198
  479.6 75.0 %all-to-all-start.7 = ((bf16[8,1280,128]{2,1,0:T(8,128)(2,1)}), bf16[8,1280,128]{2,1,0:T(8,128)(2,1)S(1)}, u32[]{:S(2)}, u32[]{:S(2)}) async-start(bf16[8,1280,128]{2,1,0:T(8,128)(2,1)} %pad_maximum_fusion.1), calls=%async_computation.8 | async-start | bytes 5242880 | tf_op jit(solution)/shard_map/all_to_all | solution.py:733
  483.3 162.7 %all-gather.2.cloned.1.call-start = ((), (), s32[]{:S(2)}) async-start(), calls=%async_computation.12 | async-start | bytes 2949120 | tf_op jit(solution)/shard_map/all_gather | solution.py:1217
  483.5 71.2 %collective-permute-start.26 = (bf16[512,1024]{1,0:T(8,128)(2,1)}, bf16[512,1024]{1,0:T(8,128)(2,1)}, u32[]{:S(2)}, u32[]{:S(2)}) collective-permute-start(bf16[512,1024]{1,0:T(8,128)(2,1)} %get-tuple-element.139), channel_id=1, source_target_pairs={{0,1},{1,0},{2,3},{3,2},{4,5},{5,4},{6,7},{7,6},{8,9},{9,8},{10,11... | collective-permute-start | bytes 3145736 | tf_op jit(solution)/shard_map/ppermute | solution.py:729
  487.2 66.4 %collective-permute-start.25 = (bf16[128,1024]{1,0:T(8,128)(2,1)S(1)}, bf16[128,1024]{1,0:T(8,128)(2,1)}, u32[]{:S(2)}, u32[]{:S(2)}) collective-permute-start(bf16[128,1024]{1,0:T(8,128)(2,1)S(1)} %constant_dynamic-slice_fusion.2), channel_id=1, source_target_pairs={{0,16},{8,24},{16,0},{24,8},{1,17},{9,25},{17,1},{25,9},{2,18},{10... | collective-permute-start | bytes 786440 | tf_op jit(solution)/shard_map/ppermute | solution.py:1198
  494.1 60.6 %collective-permute-start.24 = (f32[80,128]{1,0:T(8,128)S(1)}, f32[80,128]{1,0:T(8,128)S(1)}, u32[]{:S(2)}, u32[]{:S(2)}) collective-permute-start(f32[80,128]{1,0:T(8,128)S(1)} %add.196), channel_id=1, source_target_pairs={{0,4},{4,0},{1,5},{5,1},{2,6},{6,2},{3,7},{7,3},{8,12},{12,8},{9,1... | collective-permute-start | bytes 122888 | tf_op jit(solution)/shard_map/ppermute | solution.py:729
  579.9 33.9 %collective-permute-start.28 = (bf16[4,3,64,512]{3,2,1,0:T(8,128)(2,1)}, bf16[4,3,64,512]{3,2,1,0:T(8,128)(2,1)}, u32[]{:S(2)}, u32[]{:S(2)}) collective-permute-start(bf16[4,3,64,512]{3,2,1,0:T(8,128)(2,1)} %constant_dynamic-slice_fusion), channel_id=1, source_target_pairs={{0,4},{4,0},{1,5},{5,1},{2,6},{6,2},{3,7},{7,3},{8,12},{12,8},{9,1... | collective-permute-start | bytes 2359304 | tf_op jit(solution)/shard_map/ppermute | solution.py:729
  581.4 38.3 %collective-permute-start.31 = (bf16[128,1024]{1,0:T(8,128)(2,1)S(1)}, bf16[128,1024]{1,0:T(8,128)(2,1)S(1)}, u32[]{:S(2)}, u32[]{:S(2)}) collective-permute-start(bf16[128,1024]{1,0:T(8,128)(2,1)S(1)} %add_convert_fusion.9), channel_id=1, source_target_pairs={{0,16},{8,24},{16,0},{24,8},{1,17},{9,25},{17,1},{25,9},{2,18},{10... | collective-permute-start | bytes 786440 | tf_op jit(solution)/shard_map/ppermute | solution.py:1198
  581.4 64.5 %collective-permute-start.33 = (bf16[1024,512]{1,0:T(8,128)(2,1)S(1)}, bf16[1024,512]{1,0:T(8,128)(2,1)}, u32[]{:S(2)}, u32[]{:S(2)}) collective-permute-start(bf16[1024,512]{1,0:T(8,128)(2,1)S(1)} %copy-done.19), channel_id=1, source_target_pairs={{0,1},{1,0},{2,3},{3,2},{4,5},{5,4},{6,7},{7,6},{8,9},{9,8},{10,11... | collective-permute-start | bytes 3145736 | tf_op jit(solution)/shard_map/ppermute | solution.py:729
  616.1 29.8 %all-to-all-start.8 = ((bf16[4,3,64,512]{3,2,1,0:T(8,128)(2,1)}), bf16[4,3,64,512]{3,2,1,0:T(8,128)(2,1)S(1)}, u32[]{:S(2)}, u32[]{:S(2)}) async-start(bf16[4,3,64,512]{3,2,1,0:T(8,128)(2,1)} %add_convert_fusion.7), calls=%async_computation.9 | async-start | bytes 1572864 | tf_op jit(solution)/shard_map/all_to_all | solution.py:1342
  646.0 38.6 %collective-permute-start.40 = (bf16[512,1024]{1,0:T(8,128)(2,1)S(1)}, bf16[512,1024]{1,0:T(8,128)(2,1)}, u32[]{:S(2)}, u32[]{:S(2)}) collective-permute-start(bf16[512,1024]{1,0:T(8,128)(2,1)S(1)} %pad_maximum_fusion.7), channel_id=1, source_target_pairs={{0,4},{4,0},{1,5},{5,1},{2,6},{6,2},{3,7},{7,3},{8,12},{12,8},{9,1... | collective-permute-start | bytes 3145736 | tf_op jit(solution)/shard_map/ppermute | solution.py:729
  (67 other events, 752.3 us)
Sparse Core Ops, SparseCore 0:
  396.1 83.5 reduce-scatter.1
  554.8 66.9 all-gather.1

commit v4 on v3

--- a/solution.py
+++ b/solution.py
@@ -849,14 +849,17 @@
         sums_ref[n : n + 1, :] = sums[n]
 
 
-def backward_kernel(side_ref, slope_ref, second_low, grad_second, normed_one, inv_one, gain_ref, *refs):
+def backward_kernel(
+    place_ref, slope_ref, second_low, grad_second, normed_one, inv_one, gain_ref, second_sums, *refs
+):
     up_hbm, down_hbm, out_hbm = refs[0:4], refs[4:8], refs[8:10]
-    grad_pre_ref, hidden_ref, hidden_low, gc_own, gc_far, sums_ref, bias_grad_ref = refs[10:17]
-    ups, downs, outs, acc, sem = refs[17:]
+    grad_pre_ref, hidden_ref, hidden_low, gc_own, gc_far, sums_ref = refs[10:16]
+    ups, downs, outs, acc, sem = refs[16:]
+    side, core = place_ref[0], place_ref[1]
     low = jnp.bfloat16
     width = acc.shape[1]
     for n in range(4):
-        slot = weight_slot(n, side_ref[0])
+        slot = weight_slot(n, side)
         pltpu.make_async_copy(down_hbm[n], downs.at[slot], sem.at[2 * slot]).start()
         pltpu.make_async_copy(up_hbm[n], ups.at[slot], sem.at[2 * slot + 1]).start()
     copies = [pltpu.make_async_copy(out_hbm[n], outs.at[n], sem.at[8 + n]) for n in range(2)]
@@ -869,6 +872,7 @@
     def backward(n, carry):
         pltpu.make_async_copy(down_hbm[0], downs.at[n], sem.at[2 * n]).wait()
         base = pl.multiple_of(n * width, width)
+        row = 2 * (n % 2) + jnp.where(n < 2, core, 1 - core)
         for c in range(0, width, TILE):
             total = None
             for r in range(0, CH, TILE):
@@ -879,7 +883,7 @@
                 grad_pre_ref[rows, pl.ds(base + c, TILE)] = grad_pre
                 part = jnp.sum(grad_pre.astype(jnp.float32), axis=0, keepdims=True)
                 total = part if total is None else total + part
-            bias_grad_ref[n, :, c : c + TILE] = total
+            sums_ref[pl.ds(row, 1), c : c + TILE] = total
         pltpu.make_async_copy(up_hbm[0], ups.at[n], sem.at[2 * n + 1]).wait()
         acc[...] += nt(grad_pre_ref[:, pl.ds(base, width)], ups[n])
         return carry
@@ -904,7 +908,9 @@
 
     sums = lax.fori_loop(0, CH // BLOCK, last_step, (zero, zero, zero))
     for n in range(3):
-        sums_ref[n : n + 1, :] = sums[n]
+        sums_ref[4 + n : 5 + n, :] = sums[n]
+        sums_ref[7 + n : 8 + n, :] = second_sums[n : n + 1, :]
+    sums_ref[10:16, :] = jnp.zeros((6, width), jnp.float32)
     for copy in copies:
         copy.wait()
     for source, pack in enumerate((gc_own, gc_far)):
@@ -972,15 +978,17 @@
     )
 
 
-def backward_rows(side, slopes, second_low, grad_second, normed_one, inv_one, gain, heads, weights):
+def backward_rows(
+    place, slopes, second_low, grad_second, normed_one, inv_one, gain, second_sums, heads, weights
+):
     width = second_low.shape[1]
     units = 4 * width
     low = jnp.bfloat16
     return dense_call(
         backward_kernel,
         "backward_rows",
-        [pl.BlockSpec(memory_space=pltpu.SMEM)] + [pl.BlockSpec(memory_space=pltpu.VMEM)] * 6,
-        (side, slopes, second_low, grad_second, normed_one, inv_one, gain),
+        [pl.BlockSpec(memory_space=pltpu.SMEM)] + [pl.BlockSpec(memory_space=pltpu.VMEM)] * 7,
+        (place, slopes, second_low, grad_second, normed_one, inv_one, gain, second_sums),
         weights,
         [
             ((CH, units), low),
@@ -988,8 +996,7 @@
             ((CH, width), low),
             ((heads, CH // 2, 128), low),
             ((heads, CH // 2, 128), low),
-            ((3, width), jnp.float32),
-            ((4, 1, width), jnp.float32),
+            ((16, width), jnp.float32),
         ],
         [pltpu.VMEM((CH, width), jnp.float32)],
         width,
@@ -1069,6 +1076,53 @@
     )(side, near, kv, layer_t, weight, hidden)
 
 
+def weight_kernel(kept, place_ref, first_low, grad_pres, ctx_ref, hidden_low, *refs):
+    got_ref = refs[0] if kept else None
+    out_ref, first_t = refs[-2:]
+    far = pl.program_id(0)
+    side, core = place_ref[0], place_ref[1]
+    width, cols = first_t.shape[0], ctx_ref.shape[1] // 2
+
+    @pl.when(far == 0)
+    def _():
+        first_t[...] = first_low[...].T
+
+    slot = (0 if kept else 2) + jnp.where(far == 0, side, 1 - side)
+    for c in range(0, width, TILE):
+        at = pl.ds(pl.multiple_of(slot * width + c, TILE), TILE)
+        total = mm(first_t[...], grad_pres[:, at])
+        if kept:
+            total += got_ref[0, :width, c : c + TILE].astype(jnp.float32)
+        out_ref[0, :width, c : c + TILE] = total.astype(jnp.bfloat16)
+    part = cols // 2
+    start = far * cols + (core if kept else 1 - core) * part
+    total = tn(ctx_ref[:, pl.ds(pl.multiple_of(start, part), part)], hidden_low[...])
+    if kept:
+        total += got_ref[0, width:, :].astype(jnp.float32)
+    out_ref[0, width:, :] = total.astype(jnp.bfloat16)
+
+
+def weight_grads(place, first_low, grad_pres, ctx_rows, hidden_low, got=None):
+    kept = got is not None
+    rows, width = first_low.shape
+    height = width + ctx_rows.shape[1] // 4
+    vmem = pl.BlockSpec(memory_space=pltpu.VMEM)
+    block = pl.BlockSpec((1, height, width), lambda n: (n, 0, 0))
+    return pl.pallas_call(
+        functools.partial(weight_kernel, kept),
+        grid=(2,),
+        in_specs=[pl.BlockSpec(memory_space=pltpu.SMEM)] + [vmem] * 4 + ([block] if kept else []),
+        out_specs=block,
+        out_shape=jax.ShapeDtypeStruct((2, height, width), jnp.bfloat16),
+        scratch_shapes=[pltpu.VMEM((width, rows), jnp.bfloat16)],
+        compiler_params=pltpu.CompilerParams(vmem_limit_bytes=40 * 1024 * 1024),
+        cost_estimate=pl.CostEstimate(
+            flops=4 * rows * width * height, bytes_accessed=12 << 20, transcendentals=0
+        ),
+        name="weight_grads",
+    )(place, first_low, grad_pres, ctx_rows, hidden_low, *((got,) if kept else ()))
+
+
 def fast_local(
     layer_in,
     slot_stretch,
@@ -1249,65 +1303,49 @@
     down_far = lax.dynamic_index_in_dim(down_sum, 1 - side, 0, keepdims=False)
     down_far, grad_second = lax.optimization_barrier((down_far, grad_second))
     down_got = swap_across(down_far, "head")
-    grad_pres, grad_hidden, hidden_low, gc_own, gc_far, first_sums, bias_grads = backward_rows(
-        side_vec, slopes, second_low, grad_second, normed_one, inv_one, vectors[1:2], heads, weights
+    side_core = jnp.stack([side, core]).astype(jnp.int32)
+    grad_pres, grad_hidden, hidden_low, gc_own, gc_far, small = backward_rows(
+        side_core,
+        slopes,
+        second_low,
+        grad_second,
+        normed_one,
+        inv_one,
+        vectors[1:2],
+        second_sums,
+        heads,
+        weights,
     )
     gc_in = swap_across(gc_far, "head")
     g_near = spread(gc_own)
-    def take(block, start, size):
-        return lax.dynamic_slice_in_dim(block, start, size, 1)
-
-    up_own, up_far = (
-        on_chip([tn(first_low, take(grad_pres, (n + place) * width, width)) for n in (0, 2)])
-        for place in (side, 1 - side)
-    )
-    out_own, out_far = (
-        on_chip(
-            [
-                tn(take(ctx_rows, base + which * half_rows, half_rows), hidden_low)
-                for which in (core, 1 - core)
-            ]
-        )
-        for base in (0, cols)
-    )
-
-    def ordered(first, second):
-        return jnp.concatenate(
-            [jnp.where(is_first, first, second), jnp.where(is_first, second, first)]
-        )
-
-    small = jnp.concatenate(
-        [
-            ordered(bias_grads[0, 0], bias_grads[2, 0]),
-            ordered(bias_grads[1, 0], bias_grads[3, 0]),
-            first_sums.reshape(-1),
-            second_sums.reshape(-1),
-        ]
-    )
-    small = small.reshape(-1, 128)
-    small = sum_over(small.reshape(-1, 128), ("core",))
+    operands = (side_core, first_low, grad_pres, ctx_rows, hidden_low)
+    both_sent, down_got = lax.optimization_barrier((weight_grads(*operands), down_got))
+    both_got = swap_across(both_sent, "core")
+    both_sum = weight_grads(*operands, both_got)
+    both_own, both_far = both_sum[0], both_sum[1]
+
     down_kept, down_sent = halves(add_low(down_own, down_got), bits["y"])
-    g_near, gc_in, up_far, out_far, small, down_sent = lax.optimization_barrier(
-        (g_near, gc_in, up_far, out_far, small, down_sent)
-    )
-    up_got, out_got = swap_across(up_far, "head"), swap_across(out_far, "head")
-    small_got = swap_across(small, "head")
+    g_near, gc_in, both_far, down_sent = lax.optimization_barrier(
+        (g_near, gc_in, both_far, down_sent)
+    )
+    both_got = swap_across(both_far, "head")
+    small_got = swap_across(small, "core")
     down_got = partner(down_sent, "y")
     g_far = spread(gc_in)
     dq_near, part_grad = attend_back(
         tables, near_place, q_near, g_near, ctx_t_near, lse_near, own_keys, other_keys
     )
-    part_grad, g_far, down_got, up_got, out_got, small_got = lax.optimization_barrier(
-        (part_grad, g_far, down_got, up_got, out_got, small_got)
-    )
-    both_sum = jnp.concatenate([add_low(up_own, up_got), add_low(out_own, out_got)])
+    part_grad, g_far, down_got, both_got, small_got = lax.optimization_barrier(
+        (part_grad, g_far, down_got, both_got, small_got)
+    )
+    both_sum = add_low(both_own, both_got)
     down_kept, down_sent = halves(add_low(down_kept, down_got), bits["z_near"])
     small = small + small_got
     part_grad, both_sum, small, down_sent = lax.optimization_barrier(
         (part_grad, both_sum, small, down_sent)
     )
     both_sum = lax.psum_scatter(both_sum, ("z", "y"), scatter_dimension=0, tiled=True)
-    small_got = partner(small, "z_near")
+    small_got = swap_across(small, "head")
     down_got = partner(down_sent, "z_near")
     dq_far, own_grad, other_grad = attend_back(
         tables, far_place, q_far, g_far, ctx_t_far, lse_far, own_keys, other_keys, part_grad
@@ -1321,7 +1359,7 @@
     kv_grad, both_sum = lax.optimization_barrier((kv_grad, both_sum))
     kv_grad = spread(kv_grad)
     small = small + small_got
-    small_got = partner(small, "y")
+    small_got = partner(small, "z_near")
     down_sum = reduce_step(add_low(down_kept, down_got), "z_far")
     out_other = swap_across(out_rows, "head")
     kv_grad, small_got, both_sum, down_sum, out_other = lax.optimization_barrier(
@@ -1329,7 +1367,7 @@
     )
     both_sum = collect(both_sum)
     small = small + small_got
-    small_got = partner(small, "z_far")
+    small_got = partner(small, "y")
     down_sum = gather_step(down_sum, "z_far")
     deep = lax.axis_size("z")
     grad_w, far_part, own_part, grad_qv = project_back(
@@ -1345,9 +1383,11 @@
     small = small + small_got
     down_sum = gather_step(down_sum, "z_near")
     grad_qv = sum_over(grad_qv.reshape(-1, 128), ("core", "y"))
-    pieces, grad_qv, both_sum, down_sum, arrived = lax.optimization_barrier(
-        (pieces, grad_qv, both_sum, down_sum, arrived)
-    )
+    small_got = partner(small, "z_far")
+    pieces, grad_qv, both_sum, down_sum, arrived, small_got = lax.optimization_barrier(
+        (pieces, grad_qv, both_sum, down_sum, arrived, small_got)
+    )
+    small = small + small_got
     mine = jnp.sum(pieces.astype(jnp.float32), axis=0).astype(low)
     every = lax.all_to_all(jnp.broadcast_to(mine[None], pieces.shape), "z", 0, 0, tiled=True)
     bit = bits["y"] == 0

time: 724 us -> 713 us (0.985)
  matrix products: 38.7 us -> 11.8 us
    dot_general x10 -> x2, matrix products: 38.7 us -> 11.8 us  [tn(): lax.dot_general(left, right, (((0,), (0,)), ((), ())), preferred_element_...]
    ppermute x35 -> x31, waiting for transfers between devices: 108 us -> 119 us  [swap_across(): return lax.ppermute(block, axis_name, SWAP)]
    pallas_call x0 -> x2, Pallas kernels: none -> 10.7 us  [weight_grads(): pl.pallas_call(functools.partial(weight_kernel, kept), grid=(2,), in_spec...]
    ppermute x8, waiting for transfers between devices: 79.6 us -> 72.1 us  [partner(): lax.ppermute(block, 'z', [(n, n ^ hop) for n in range(lax.axis_size('z'))])]
    unnamed x98 -> x96, local copies, waits for them, and re-layouts: 25.7 us -> 32.2 us
    ppermute x35 -> x31, starting transfers between devices: 28 us -> 30.2 us  [swap_across(): return lax.ppermute(block, axis_name, SWAP)]
  transfers between devices with their start and end apart: 54 -> 50, of which waited for: 18 -> 17; matrix products, arithmetic and copies ran while one was open for 13% -> 9% of each run, Pallas kernels for 27% -> 28%
where the time goes in v4:
time: 713 us; the launch traced here: 707 us
  waiting for transfers between devices  234 us (33%)
  Pallas kernels  232 us (33%)
  starting transfers between devices  86.8 us (12%)
  other arithmetic  57.1 us (8%)
  local copies, waits for them, and re-layouts  50.2 us (7%)
  blocking collectives  20.4 us (3%)
  between operations  15.1 us (2%)
  matrix products  11.8 us (2%)
    ppermute x31, waiting for transfers between devices, swap_across(): return lax.ppermute(block, axis_name, SWAP)  119 us
    pallas_call x2, Pallas kernels, attend_back(): pl.pallas_call(functools.partial(attend_back_kernel, first), grid_spec=pl...  96.8 us
    ppermute x8, waiting for transfers between devices, partner(): lax.ppermute(block, 'z', [(n, n ^ hop) for n in range(lax.axis_size('z'))])  72.1 us
    pallas_call x2, Pallas kernels, attend(): pl.pallas_call(attend_kernel, grid_spec=pltpu.PrefetchScalarGridSpec(num_...  57.6 us
    pallas_call x2, Pallas kernels, dense_call(): pl.pallas_call(kernel, in_specs=in_specs + [anywhere] * 10, out_specs=[vm...  49.6 us
    all_to_all x7, starting transfers between devices, spread(): return lax.all_to_all(block, ('z', 'y'), 0, 0, tiled=True)  35.2 us
    unnamed x96, local copies, waits for them, and re-layouts  32.2 us
    ppermute x31, starting transfers between devices, swap_across(): return lax.ppermute(block, axis_name, SWAP)  30.2 us
  transfers between devices with their start and end apart: 50, of which 17 were waited for; matrix products, arithmetic and copies ran while one was open for 9% of the time, Pallas kernels for 28%

profile of v4, /device:TPU:0, one launch (start us, length us, event | category | flops | bytes accessed | tf_op | source)
XLA Modules:
  0.0 707.5 jit_solution(8526212326743986775)
XLA Ops:
  7.2 7.9 %project.1 = (bf16[8,1024,128]{2,1,0:T(8,128)(2,1)}, bf16[8,256,128]{2,1,0:T(8,128)(2,1)}, bf16[8,256,128]{2,1,0:T(8,128)(2,1)}) custom-call(s32[1]{0:T(128)} %bitcast.side_ref, bf16[1024,1024]{1,0:T(8,128)(2,1)} %layer_in.1, bf16[3,1024,512]{2,1,0:T(8,128)(2,1)} %bitcast.46, bf16[3,1024,512]{2,1,0:T(8,128)(2,1)} %bitcast.47, ...), custom_call_target="tpu_custom_call" | custom-call | flops 3221225472 | bytes 11534336 | tf_op jit(solution)/shard_map/project/pallas_call | solution.py:395
  15.1 7.3 %all-to-all-start.2 = ((bf16[8,1024,128]{2,1,0:T(8,128)(2,1)}), bf16[8,1024,128]{2,1,0:T(8,128)(2,1)S(1)}, u32[]{:S(2)}, u32[]{:S(2)}) async-start(bf16[8,1024,128]{2,1,0:T(8,128)(2,1)} %get-tuple-element.113), calls=%async_computation.2 | async-start | bytes 4194304 | tf_op jit(solution)/shard_map/all_to_all | solution.py:733
  30.5 43.3 %collective-permute-done.refs_2_ = bf16[1024,1024]{1,0:T(8,128)(2,1)} collective-permute-done((bf16[1024,1024]{1,0:T(8,128)(2,1)S(1)}, bf16[1024,1024]{1,0:T(8,128)(2,1)}, u32[]{:S(2)}, u32[]{:S(2)}) %collective-permute-start) | collective-permute-done | bytes 2097184 | tf_op jit(solution)/shard_map/ppermute | solution.py:729
  75.3 20.4 %all_to_all.50.q_ref.refs_0_ = bf16[8,256,128]{2,1,0:T(8,128)(2,1)S(1)} all-to-all(bf16[8,256,128]{2,1,0:T(8,128)(2,1)S(1)} %copy-done.37), channel_id=1, replica_groups=mesh['z'=4,'y'=2,'core'=2,'head'=2] {'z','y'}, dimensions={0} | all-to-all | bytes 1048576 | tf_op jit(solution)/shard_map/all_to_all | solution.py:733
  99.9 27.0 %attend.2 = (bf16[8,256,128]{2,1,0:T(8,128)(2,1)S(1)}, f32[8,64,512]{2,1,0:T(8,128)S(1)}, f32[8,1,512]{2,1,0:T(1,128)S(1)}) custom-call(s32[32]{0:T(128)S(1)} %copy-done.23, s32[8]{0:T(128)S(1)} %copy-done.24, s32[2]{0:T(128)S(1)} %pad_add_fusion.1.place_ref, bf16[8,256,128]{2,1,0:T(8,128)(2,1)S(1)} %all_to_all.50.q_ref.refs_0_, ...), custom_call_target="tpu_custom_call" | custom-call | flops 671088640 | bytes 4194304 | tf_op jit(solution)/shard_map/attend/pallas_call | solution.py:556
  128.7 5.0 collective-permute-start.3
  133.9 30.6 %attend.3 = (bf16[8,256,128]{2,1,0:T(8,128)(2,1)S(1)}, f32[8,64,512]{2,1,0:T(8,128)S(1)}, f32[8,1,512]{2,1,0:T(1,128)S(1)}) custom-call(s32[32]{0:T(128)S(1)} %copy-done.23, s32[8]{0:T(128)S(1)} %copy-done.24, s32[2]{0:T(128)S(1)} %pad_add_fusion.place_ref, bf16[8,256,128]{2,1,0:T(8,128)(2,1)S(1)} %all-to-all-done.q_ref.refs_0_, ...), custom_call_target="tpu_custom_call" | custom-call | flops 671088640 | bytes 4194304 | tf_op jit(solution)/shard_map/attend/pallas_call | solution.py:556
  167.1 6.2 all-to-all-start.3
  176.1 23.3 %all-to-all-done.3.pack_ref = bf16[8,512,128]{2,1,0:T(8,128)(2,1)} async-done(((bf16[8,512,128]{2,1,0:T(8,128)(2,1)}), bf16[8,512,128]{2,1,0:T(8,128)(2,1)}, u32[]{:S(2)}, u32[]{:S(2)}) %all-to-all-start.3) | async-done | bytes 1048608 | tf_op jit(solution)/shard_map/all_to_all | solution.py:733
  199.4 27.9 %forward_rows.1 = (bf16[512,1024]{1,0:T(8,128)(2,1)}, bf16[512,1024]{1,0:T(8,128)(2,1)}, bf16[512,1024]{1,0:T(8,128)(2,1)}, bf16[512,4096]{1,0:T(8,128)(2,1)}, b...) custom-call(s32[1]{0:T(128)} %bitcast.side_ref, ...), custom_call_target="tpu_custom_call" | custom-call | flops 4294967296 | bytes 8388608 | tf_op jit(solution)/shard_map/forward_rows/pallas_call | solution.py:928
  227.3 6.3 convolution_convert_fusion
  233.6 7.5 %collective-permute-done.9 = bf16[2048,1024]{1,0:T(8,128)(2,1)} collective-permute-done((bf16[2048,1024]{1,0:T(8,128)(2,1)}, bf16[2048,1024]{1,0:T(8,128)(2,1)}, u32[]{:S(2)}, u32[]{:S(2)}) %collective-permute-start.9) | collective-permute-done | bytes 4194336 | tf_op jit(solution)/shard_map/ppermute | solution.py:729
  241.1 5.5 add_convert_fusion
  250.8 21.7 %backward_rows.1 = (bf16[512,4096]{1,0:T(8,128)(2,1)}, f32[512,1024]{1,0:T(8,128)}, bf16[512,1024]{1,0:T(8,128)(2,1)}, bf16[8,256,128]{2,1,0:T(8,128)(2,1)}, bf1...) custom-call(s32[2]{0:T(128)} %pad_add_fusion.2.place_ref, bf16[512,4096]{1,0:T(8,128)(2,1)} %get-tuple-element.139.slope_ref, ...), custom_call_target="tpu_custom_call" | custom-call | flops 4294967296 | bytes 8388608 | tf_op jit(solution)/shard_map/backward_rows/pallas_call | solution.py:928
  275.9 5.5 weight_grads.2
  281.4 15.9 %collective-permute-done.11 = bf16[1024,1024]{1,0:T(8,128)(2,1)} collective-permute-done((bf16[1024,1024]{1,0:T(8,128)(2,1)}, bf16[1024,1024]{1,0:T(8,128)(2,1)}, u32[]{:S(2)}, u32[]{:S(2)}) %collective-permute-start.11) | collective-permute-done | bytes 2097184 | tf_op jit(solution)/shard_map/ppermute | solution.py:729
  307.9 5.2 weight_grads.3
  325.8 50.6 %attend_back.2 = (bf16[8,256,128]{2,1,0:T(8,128)(2,1)S(1)}, f32[32,512,128]{2,1,0:T(8,128)S(1)}) custom-call(s32[32]{0:T(128)S(1)} %copy-done.23, s32[8]{0:T(128)S(1)} %copy-done.24, s32[2]{0:T(128)S(1)} %pad_add_fusion.place_ref, bf16[8,256,128]{2,1,0:T(8,128)(2,1)S(1)} %all-to-all-done.q_ref.refs_0_, bf16[8,256,128]{2,1,0:T(8,128)(2,1)} %all-to-all-done.4.refs_1_, ...), custom_call_target="tpu_custom_call" | custom-call | flops 671088640 | bytes 6291456 | tf_op jit(solution)/shard_map/attend_back/pallas_call | solution.py:704
  380.6 5.3 fusion
  389.7 6.0 all-to-all-start.6
  399.0 46.2 %attend_back.3 = (bf16[8,256,128]{2,1,0:T(8,128)(2,1)S(1)}, bf16[16,512,128]{2,1,0:T(8,128)(2,1)S(1)}, bf16[16,512,128]{2,1,0:T(8,128)(2,1)S(1)}) custom-call(s32[32]{0:T(128)S(1)} %copy-done.23, s32[8]{0:T(128)S(1)} %copy-done.24, s32[2]{0:T(128)S(1)} %pad_add_fusion.1.place_ref, bf16[8,256,128]{2,1,0:T(8,128)(2,1)S(1)} %all_to_all.50.q_ref.refs_0_, ...), custom_call_target="tpu_custom_call" | custom-call | flops 671088640 | bytes 6291456 | tf_op jit(solution)/shard_map/attend_back/pallas_call | solution.py:704
  448.7 8.1 %collective-permute-start.18 = (bf16[16,512,128]{2,1,0:T(8,128)(2,1)}, bf16[16,512,128]{2,1,0:T(8,128)(2,1)S(1)}, u32[]{:S(2)}, u32[]{:S(2)}) collective-permute-start(bf16[16,512,128]{2,1,0:T(8,128)(2,1)} %copy-done.26), channel_id=1, source_target_pairs={{0,2},{2,0},{1,3},{3,1},{4,6},{6,4},{5,7},{7,5},{8,10},{10,8},{9,1... | collective-permute-start | bytes 6291464 | tf_op jit(solution)/shard_map/ppermute | solution.py:729
  464.6 8.4 %reduce-scatter.2.cloned.1.call-done = bf16[160,1024]{1,0:T(8,128)(2,1)} async-done(((bf16[1280,1024]{1,0:T(8,128)(2,1)}), bf16[160,1024]{1,0:T(8,128)(2,1)}) %reduce-scatter.2.cloned.1.call-update) | async-done | bytes 327696 | tf_op jit(solution)/shard_map/reduce_scatter | solution.py:1347
  489.6 57.1 %collective-permute-done.20 = bf16[128,1024]{1,0:T(8,128)(2,1)} collective-permute-done((bf16[128,1024]{1,0:T(8,128)(2,1)}, bf16[128,1024]{1,0:T(8,128)(2,1)}, u32[]{:S(2)}, u32[]{:S(2)}) %collective-permute-start.20) | collective-permute-done | bytes 262176 | tf_op jit(solution)/shard_map/ppermute | solution.py:1252
  551.1 9.5 %project_back.1 = (bf16[16,3,64,512]{3,2,1,0:T(8,128)(2,1)S(1)}, bf16[1024,512]{1,0:T(8,128)(2,1)S(1)}, f32[1024,512]{1,0:T(8,128)S(1)}, f32[2,512]{1,0:T(2,128)S(1)}) custom-call(s32[1]{0:T(128)} %bitcast.side_ref, bf16[8,256,128]{2,1,0:T(8,128)(2,1)S(1)} %all-to-all-done.6.near_ref, bf16[8,1280,128]{2,1,0:T(8,128)(2,1)S(1)} %all-to-all-done.7.kv_ref, ...), custom_call_target="tpu_custom_call" | custom-call | flops 1073741824 | bytes 8388608 | tf_op jit(solution)/shard_map/project_back/pallas_call | solution.py:1060
  573.2 30.6 %collective-permute-done.23 = bf16[4,3,64,512]{3,2,1,0:T(8,128)(2,1)} collective-permute-done((bf16[4,3,64,512]{3,2,1,0:T(8,128)(2,1)}, bf16[4,3,64,512]{3,2,1,0:T(8,128)(2,1)}, u32[]{:S(2)}, u32[]{:S(2)}) %collective-permute-start.23) | collective-permute-done | bytes 786464 | tf_op jit(solution)/shard_map/ppermute | solution.py:729
  622.4 14.8 %collective-permute-done.27 = bf16[256,1024]{1,0:T(8,128)(2,1)S(1)} collective-permute-done((bf16[256,1024]{1,0:T(8,128)(2,1)}, bf16[256,1024]{1,0:T(8,128)(2,1)S(1)}, u32[]{:S(2)}, u32[]{:S(2)}) %collective-permute-start.27) | collective-permute-done | bytes 524320 | tf_op jit(solution)/shard_map/ppermute | solution.py:1252
  639.7 4.8 all-to-all-start.9
  649.9 4.4 maximum_convert_fusion
  654.3 10.6 %all-to-all-done.9 = bf16[4,3,64,512]{3,2,1,0:T(8,128)(2,1)S(1)} async-done(((bf16[4,3,64,512]{3,2,1,0:T(8,128)(2,1)}), bf16[4,3,64,512]{3,2,1,0:T(8,128)(2,1)S(1)}, u32[]{:S(2)}, u32[]{:S(2)}) %all-to-all-start.9) | async-done | bytes 786464 | tf_op jit(solution)/shard_map/all_to_all | solution.py:1392
  675.2 8.4 %collective-permute-done.32 = bf16[4,3,64,512]{3,2,0,1:T(8,128)(2,1)S(1)} collective-permute-done((bf16[4,3,64,512]{3,2,0,1:T(8,128)(2,1)S(1)}, bf16[4,3,64,512]{3,2,0,1:T(8,128)(2,1)S(1)}, u32[]{:S(2)}, u32[]{:S(2)}) %collective-permute-start.32) | collective-permute-done | bytes 786464 | tf_op jit(solution)/shard_map/ppermute | solution.py:729
  691.2 4.5 maximum_convert_fusion.1
  (251 shorter events, 156.7 us)
Async XLA Ops:
  15.1 58.7 %all-to-all-start.2 = ((bf16[8,1024,128]{2,1,0:T(8,128)(2,1)}), bf16[8,1024,128]{2,1,0:T(8,128)(2,1)S(1)}, u32[]{:S(2)}, u32[]{:S(2)}) async-start(bf16[8,1024,128]{2,1,0:T(8,128)(2,1)} %get-tuple-element.113), calls=%async_computation.2 | async-start | bytes 4194304 | tf_op jit(solution)/shard_map/all_to_all | solution.py:733
  26.6 47.2 %collective-permute-start = (bf16[1024,1024]{1,0:T(8,128)(2,1)S(1)}, bf16[1024,1024]{1,0:T(8,128)(2,1)}, u32[]{:S(2)}, u32[]{:S(2)}) collective-permute-start(bf16[1024,1024]{1,0:T(8,128)(2,1)S(1)} %get-tuple-element.132.refs_0_), channel_id=1, source_target_pairs={{0,1},{1,0},{2,3},{3,2},{4,5},{5,4},{6,7},{7,6},{8,9},{9,8},{10,11... | collective-permute-start | bytes 6291464 | tf_op jit(solution)/shard_map/ppermute | solution.py:729
  73.8 26.1 %collective-permute-start.1 = (bf16[8,1024,128]{2,1,0:T(8,128)(2,1)S(1)}, bf16[8,1024,128]{2,1,0:T(8,128)(2,1)}, u32[]{:S(2)}, u32[]{:S(2)}) collective-permute-start(bf16[8,1024,128]{2,1,0:T(8,128)(2,1)S(1)} %all-to-all-done.2), channel_id=1, source_target_pairs={{0,2},{2,0},{1,3},{3,1},{4,6},{6,4},{5,7},{7,5},{8,10},{10,8},{9,1... | collective-permute-start | bytes 6291464 | tf_op jit(solution)/shard_map/ppermute | solution.py:729
  73.8 55.0 %collective-permute-start.2 = (bf16[1024,1024]{1,0:T(8,128)(2,1)}, bf16[1024,1024]{1,0:T(8,128)(2,1)}, u32[]{:S(2)}, u32[]{:S(2)}) collective-permute-start(bf16[1024,1024]{1,0:T(8,128)(2,1)} %get-tuple-element.120.refs_4_), channel_id=1, source_target_pairs={{0,1},{1,0},{2,3},{3,2},{4,5},{5,4},{6,7},{7,6},{8,9},{9,8},{10,11... | collective-permute-start | bytes 6291464 | tf_op jit(solution)/shard_map/ppermute | solution.py:729
  95.6 33.1 %all-to-all-start = ((bf16[8,256,128]{2,1,0:T(8,128)(2,1)}), bf16[8,256,128]{2,1,0:T(8,128)(2,1)S(1)}, u32[]{:S(2)}, u32[]{:S(2)}) async-start(bf16[8,256,128]{2,1,0:T(8,128)(2,1)} %get-tuple-element.110), calls=%async_computation | async-start | bytes 1048576 | tf_op jit(solution)/shard_map/all_to_all | solution.py:733
  99.3 66.2 %collective-permute-start.4 = (bf16[512,1024]{1,0:T(8,128)(2,1)}, bf16[512,1024]{1,0:T(8,128)(2,1)}, u32[]{:S(2)}, u32[]{:S(2)}) collective-permute-start(bf16[512,1024]{1,0:T(8,128)(2,1)} %refs_8_.1), channel_id=1, source_target_pairs={{0,1},{1,0},{2,3},{3,2},{4,5},{5,4},{6,7},{7,6},{8,9},{9,8},{10,11... | collective-permute-start | bytes 3145736 | tf_op jit(solution)/shard_map/ppermute | solution.py:729
  128.7 36.7 %collective-permute-start.3 = (bf16[8,256,128]{2,1,0:T(8,128)(2,1)}, bf16[8,256,128]{2,1,0:T(8,128)(2,1)S(1)}, u32[]{:S(2)}, u32[]{:S(2)}) collective-permute-start(bf16[8,256,128]{2,1,0:T(8,128)(2,1)} %copy-done.29), channel_id=1, source_target_pairs={{0,1},{1,0},{2,3},{3,2},{4,5},{5,4},{6,7},{7,6},{8,9},{9,8},{10,11... | collective-permute-start | bytes 1572872 | tf_op jit(solution)/shard_map/ppermute | solution.py:729
  133.8 31.6 %collective-permute-start.5 = (bf16[1024]{0:T(1024)(128)(2,1)S(1)}, bf16[1024]{0:T(1024)(128)(2,1)S(1)}, u32[]{:S(2)}, u32[]{:S(2)}) collective-permute-start(bf16[1024]{0:T(1024)(128)(2,1)S(1)} %get-tuple-element.127), channel_id=1, source_target_pairs={{0,1},{1,0},{2,3},{3,2},{4,5},{5,4},{6,7},{7,6},{8,9},{9,8},{10,11... | collective-permute-start | bytes 6152 | tf_op jit(solution)/shard_map/ppermute | solution.py:729
  165.5 33.9 %collective-permute-start.7 = (bf16[1024,1024]{1,0:T(8,128)(2,1)}, bf16[1024,1024]{1,0:T(8,128)(2,1)}, u32[]{:S(2)}, u32[]{:S(2)}) collective-permute-start(bf16[1024,1024]{1,0:T(8,128)(2,1)} %collective-permute-done.refs_2_), channel_id=1, source_target_pairs={{0,2},{2,0},{1,3},{3,1},{4,6},{6,4},{5,7},{7,5},{8,10},{10,8},{9,1... | collective-permute-start | bytes 6291464 | tf_op jit(solution)/shard_map/ppermute | solution.py:729
  165.6 33.8 %collective-permute-start.8 = (bf16[1024,1024]{1,0:T(8,128)(2,1)}, bf16[1024,1024]{1,0:T(8,128)(2,1)}, u32[]{:S(2)}, u32[]{:S(2)}) collective-permute-start(bf16[1024,1024]{1,0:T(8,128)(2,1)} %collective-permute-done.2.refs_6_), channel_id=1, source_target_pairs={{0,2},{2,0},{1,3},{3,1},{4,6},{6,4},{5,7},{7,5},{8,10},{10,8},{9,1... | collective-permute-start | bytes 6291464 | tf_op jit(solution)/shard_map/ppermute | solution.py:729
  167.1 32.3 %all-to-all-start.3 = ((bf16[8,512,128]{2,1,0:T(8,128)(2,1)}), bf16[8,512,128]{2,1,0:T(8,128)(2,1)}, u32[]{:S(2)}, u32[]{:S(2)}) async-start(bf16[8,512,128]{2,1,0:T(8,128)(2,1)} %pad_maximum_fusion.5), calls=%async_computation.3 | async-start | bytes 2097152 | tf_op jit(solution)/shard_map/all_to_all | solution.py:733
  249.3 48.0 %collective-permute-start.11 = (bf16[1024,1024]{1,0:T(8,128)(2,1)}, bf16[1024,1024]{1,0:T(8,128)(2,1)}, u32[]{:S(2)}, u32[]{:S(2)}) collective-permute-start(bf16[1024,1024]{1,0:T(8,128)(2,1)} %dynamic-slice_bitcast_fusion), channel_id=1, source_target_pairs={{0,1},{1,0},{2,3},{3,2},{4,5},{5,4},{6,7},{7,6},{8,9},{9,8},{10,11... | collective-permute-start | bytes 6291464 | tf_op jit(solution)/shard_map/ppermute | solution.py:729
  316.9 63.7 %collective-permute-start.14 = (bf16[1280,1024]{1,0:T(8,128)(2,1)}, bf16[1280,1024]{1,0:T(8,128)(2,1)}, u32[]{:S(2)}, u32[]{:S(2)}) collective-permute-start(bf16[1280,1024]{1,0:T(8,128)(2,1)} %slice_bitcast_fusion.1), channel_id=1, source_target_pairs={{0,1},{1,0},{2,3},{3,2},{4,5},{5,4},{6,7},{7,6},{8,9},{9,8},{10,11... | collective-permute-start | bytes 7864328 | tf_op jit(solution)/shard_map/ppermute | solution.py:729
  318.6 62.0 %collective-permute-start.13 = (bf16[512,1024]{1,0:T(8,128)(2,1)}, bf16[512,1024]{1,0:T(8,128)(2,1)}, u32[]{:S(2)}, u32[]{:S(2)}) collective-permute-start(bf16[512,1024]{1,0:T(8,128)(2,1)} %constant_dynamic-slice_fusion.4), channel_id=1, source_target_pairs={{0,4},{4,0},{1,5},{5,1},{2,6},{6,2},{3,7},{7,3},{8,12},{12,8},{9,1... | collective-permute-start | bytes 3145736 | tf_op jit(solution)/shard_map/ppermute | solution.py:729
  320.1 60.5 %all-to-all-start.5 = ((bf16[8,256,128]{2,1,0:T(8,128)(2,1)}), bf16[8,256,128]{2,1,0:T(8,128)(2,1)}, u32[]{:S(2)}, u32[]{:S(2)}) async-start(bf16[8,256,128]{2,1,0:T(8,128)(2,1)} %collective-permute-done.10), calls=%async_computation.5 | async-start | bytes 1048576 | tf_op jit(solution)/shard_map/all_to_all | solution.py:733
  324.4 148.5 %reduce-scatter.2.cloned.1.call-start = ((), (), s32[]{:S(2)}) async-start(), calls=%async_computation.11 | async-start | bytes 2949120 | tf_op jit(solution)/shard_map/reduce_scatter | solution.py:1347
  324.5 56.1 %collective-permute-start.15 = (f32[16,1024]{1,0:T(8,128)S(1)}, f32[16,1024]{1,0:T(8,128)S(1)}, u32[]{:S(2)}, u32[]{:S(2)}) collective-permute-start(f32[16,1024]{1,0:T(8,128)S(1)} %copy-done.38), channel_id=1, source_target_pairs={{0,2},{2,0},{1,3},{3,1},{4,6},{6,4},{5,7},{7,5},{8,10},{10,8},{9,1... | collective-permute-start | bytes 196616 | tf_op jit(solution)/shard_map/ppermute | solution.py:729
  389.7 59.0 %all-to-all-start.6 = ((bf16[8,256,128]{2,1,0:T(8,128)(2,1)}), bf16[8,256,128]{2,1,0:T(8,128)(2,1)S(1)}, u32[]{:S(2)}, u32[]{:S(2)}) async-start(bf16[8,256,128]{2,1,0:T(8,128)(2,1)} %copy-done.22), calls=%async_computation.6 | async-start | bytes 1048576 | tf_op jit(solution)/shard_map/all_to_all | solution.py:733
  395.6 53.0 %collective-permute-start.17 = (bf16[256,1024]{1,0:T(8,128)(2,1)}, bf16[256,1024]{1,0:T(8,128)(2,1)}, u32[]{:S(2)}, u32[]{:S(2)}) collective-permute-start(bf16[256,1024]{1,0:T(8,128)(2,1)} %constant_dynamic-slice_fusion.3), channel_id=1, source_target_pairs={{0,8},{8,0},{16,24},{24,16},{1,9},{9,1},{17,25},{25,17},{2,10},{10... | collective-permute-start | bytes 1572872 | tf_op jit(solution)/shard_map/ppermute | solution.py:1252
  397.6 51.0 %collective-permute-start.16 = (f32[16,1024]{1,0:T(8,128)S(1)}, f32[16,1024]{1,0:T(8,128)S(1)}, u32[]{:S(2)}, u32[]{:S(2)}) collective-permute-start(f32[16,1024]{1,0:T(8,128)S(1)} %add.123), channel_id=1, source_target_pairs={{0,1},{1,0},{2,3},{3,2},{4,5},{5,4},{6,7},{7,6},{8,9},{9,8},{10,11... | collective-permute-start | bytes 196616 | tf_op jit(solution)/shard_map/ppermute | solution.py:729
  472.9 75.0 %all-to-all-start.7 = ((bf16[8,1280,128]{2,1,0:T(8,128)(2,1)}), bf16[8,1280,128]{2,1,0:T(8,128)(2,1)S(1)}, u32[]{:S(2)}, u32[]{:S(2)}) async-start(bf16[8,1280,128]{2,1,0:T(8,128)(2,1)} %pad_maximum_fusion), calls=%async_computation.8 | async-start | bytes 5242880 | tf_op jit(solution)/shard_map/all_to_all | solution.py:733
  476.5 161.0 %all-gather.2.cloned.1.call-start = ((), (), s32[]{:S(2)}) async-start(), calls=%async_computation.12 | async-start | bytes 2949120 | tf_op jit(solution)/shard_map/all_gather | solution.py:1271
  476.6 71.3 %collective-permute-start.21 = (bf16[512,1024]{1,0:T(8,128)(2,1)}, bf16[512,1024]{1,0:T(8,128)(2,1)}, u32[]{:S(2)}, u32[]{:S(2)}) collective-permute-start(bf16[512,1024]{1,0:T(8,128)(2,1)} %get-tuple-element.138), channel_id=1, source_target_pairs={{0,1},{1,0},{2,3},{3,2},{4,5},{5,4},{6,7},{7,6},{8,9},{9,8},{10,11... | collective-permute-start | bytes 3145736 | tf_op jit(solution)/shard_map/ppermute | solution.py:729
  481.0 65.8 %collective-permute-start.20 = (bf16[128,1024]{1,0:T(8,128)(2,1)}, bf16[128,1024]{1,0:T(8,128)(2,1)}, u32[]{:S(2)}, u32[]{:S(2)}) collective-permute-start(bf16[128,1024]{1,0:T(8,128)(2,1)} %constant_dynamic-slice_fusion.2), channel_id=1, source_target_pairs={{0,16},{8,24},{16,0},{24,8},{1,17},{9,25},{17,1},{25,9},{2,18},{10... | collective-permute-start | bytes 786440 | tf_op jit(solution)/shard_map/ppermute | solution.py:1252
  488.1 59.8 %collective-permute-start.19 = (f32[16,1024]{1,0:T(8,128)S(1)}, f32[16,1024]{1,0:T(8,128)}, u32[]{:S(2)}, u32[]{:S(2)}) collective-permute-start(f32[16,1024]{1,0:T(8,128)S(1)} %add.129), channel_id=1, source_target_pairs={{0,8},{8,0},{16,24},{24,16},{1,9},{9,1},{17,25},{25,17},{2,10},{10... | collective-permute-start | bytes 196616 | tf_op jit(solution)/shard_map/ppermute | solution.py:1252
  570.2 33.5 %collective-permute-start.23 = (bf16[4,3,64,512]{3,2,1,0:T(8,128)(2,1)}, bf16[4,3,64,512]{3,2,1,0:T(8,128)(2,1)}, u32[]{:S(2)}, u32[]{:S(2)}) collective-permute-start(bf16[4,3,64,512]{3,2,1,0:T(8,128)(2,1)} %constant_dynamic-slice_fusion), channel_id=1, source_target_pairs={{0,4},{4,0},{1,5},{5,1},{2,6},{6,2},{3,7},{7,3},{8,12},{12,8},{9,1... | collective-permute-start | bytes 2359304 | tf_op jit(solution)/shard_map/ppermute | solution.py:729
  571.7 37.8 %collective-permute-start.26 = (bf16[128,1024]{1,0:T(8,128)(2,1)S(1)}, bf16[128,1024]{1,0:T(8,128)(2,1)S(1)}, u32[]{:S(2)}, u32[]{:S(2)}) collective-permute-start(bf16[128,1024]{1,0:T(8,128)(2,1)S(1)} %add_convert_fusion.6), channel_id=1, source_target_pairs={{0,16},{8,24},{16,0},{24,8},{1,17},{9,25},{17,1},{25,9},{2,18},{10... | collective-permute-start | bytes 786440 | tf_op jit(solution)/shard_map/ppermute | solution.py:1252
  571.7 65.8 %collective-permute-start.28 = (bf16[1024,512]{1,0:T(8,128)(2,1)S(1)}, bf16[1024,512]{1,0:T(8,128)(2,1)}, u32[]{:S(2)}, u32[]{:S(2)}) collective-permute-start(bf16[1024,512]{1,0:T(8,128)(2,1)S(1)} %copy-done.28), channel_id=1, source_target_pairs={{0,1},{1,0},{2,3},{3,2},{4,5},{5,4},{6,7},{7,6},{8,9},{9,8},{10,11... | collective-permute-start | bytes 3145736 | tf_op jit(solution)/shard_map/ppermute | solution.py:729
  606.0 31.5 %all-to-all-start.8 = ((bf16[4,3,64,512]{3,2,1,0:T(8,128)(2,1)}), bf16[4,3,64,512]{3,2,1,0:T(8,128)(2,1)S(1)}, u32[]{:S(2)}, u32[]{:S(2)}) async-start(bf16[4,3,64,512]{3,2,1,0:T(8,128)(2,1)} %add_convert_fusion.4), calls=%async_computation.9 | async-start | bytes 1572864 | tf_op jit(solution)/shard_map/all_to_all | solution.py:1380
  610.4 26.8 %collective-permute-start.27 = (bf16[256,1024]{1,0:T(8,128)(2,1)}, bf16[256,1024]{1,0:T(8,128)(2,1)S(1)}, u32[]{:S(2)}, u32[]{:S(2)}) collective-permute-start(bf16[256,1024]{1,0:T(8,128)(2,1)} %pad_maximum_fusion.7), channel_id=1, source_target_pairs={{0,8},{8,0},{16,24},{24,16},{1,9},{9,1},{17,25},{25,17},{2,10},{10... | collective-permute-start | bytes 1572872 | tf_op jit(solution)/shard_map/ppermute | solution.py:1252
  637.7 31.7 %collective-permute-start.36 = (bf16[512,1024]{1,0:T(8,128)(2,1)S(1)}, bf16[512,1024]{1,0:T(8,128)(2,1)}, u32[]{:S(2)}, u32[]{:S(2)}) collective-permute-start(bf16[512,1024]{1,0:T(8,128)(2,1)S(1)} %pad_maximum_fusion.6), channel_id=1, source_target_pairs={{0,4},{4,0},{1,5},{5,1},{2,6},{6,2},{3,7},{7,3},{8,12},{12,8},{9,1... | collective-permute-start | bytes 3145736 | tf_op jit(solution)/shard_map/ppermute | solution.py:729
  639.7 25.3 %all-to-all-start.9 = ((bf16[4,3,64,512]{3,2,1,0:T(8,128)(2,1)}), bf16[4,3,64,512]{3,2,1,0:T(8,128)(2,1)S(1)}, u32[]{:S(2)}, u32[]{:S(2)}) async-start(bf16[4,3,64,512]{3,2,1,0:T(8,128)(2,1)} %broadcast_in_dim.2), calls=%async_computation.10 | async-start | bytes 1572864 | tf_op jit(solution)/shard_map/all_to_all | solution.py:1392
  (64 other events, 604.9 us)
Sparse Core Ops, SparseCore 0:
  389.8 83.0 reduce-scatter.1
  548.0 67.6 all-gather.1

commit v5 on v4

--- a/solution.py
+++ b/solution.py
@@ -495,7 +495,7 @@
             values_t[index] = keys[index].T[HD:128, :]
             return carry
 
-        lax.fori_loop(0, 2 * half, turn, 0)
+        lax.fori_loop(0, 2 * half, turn, 0, unroll=4)
 
     core = place_ref[0]
     stretch = slot_ref[my_slot(place_ref, chip)]

time: 713 us -> 719 us (level)
  Pallas kernels: 232 us -> 242 us
    pallas_call x2, Pallas kernels: 96.8 us -> 105 us  [attend_back(): pl.pallas_call(functools.partial(attend_back_kernel, first), grid_spec=pl...]
  transfers between devices with their start and end apart: 50 -> 50, of which waited for: 17 -> 17; matrix products, arithmetic and copies ran while one was open for 9% -> 9% of each run, Pallas kernels for 28% -> 29%
where the time goes in v5:
time: 719 us; the launch traced here: 713 us
  Pallas kernels  242 us (34%)
  waiting for transfers between devices  235 us (33%)
  starting transfers between devices  81.2 us (11%)
  other arithmetic  57.1 us (8%)
  local copies, waits for them, and re-layouts  50.1 us (7%)
  blocking collectives  20.4 us (3%)
  between operations  15.2 us (2%)
  matrix products  11.8 us (2%)
    ppermute x31, waiting for transfers between devices, swap_across(): return lax.ppermute(block, axis_name, SWAP)  119 us
    pallas_call x2, Pallas kernels, attend_back(): pl.pallas_call(functools.partial(attend_back_kernel, first), grid_spec=pl...  105 us
    ppermute x8, waiting for transfers between devices, partner(): lax.ppermute(block, 'z', [(n, n ^ hop) for n in range(lax.axis_size('z'))])  72.1 us
    pallas_call x2, Pallas kernels, attend(): pl.pallas_call(attend_kernel, grid_spec=pltpu.PrefetchScalarGridSpec(num_...  59.6 us
    pallas_call x2, Pallas kernels, dense_call(): pl.pallas_call(kernel, in_specs=in_specs + [anywhere] * 10, out_specs=[vm...  49.6 us
    all_to_all x7, starting transfers between devices, spread(): return lax.all_to_all(block, ('z', 'y'), 0, 0, tiled=True)  35.2 us
    unnamed x96, local copies, waits for them, and re-layouts  32.1 us
    ppermute x31, starting transfers between devices, swap_across(): return lax.ppermute(block, axis_name, SWAP)  24.6 us
  transfers between devices with their start and end apart: 50, of which 17 were waited for; matrix products, arithmetic and copies ran while one was open for 9% of the time, Pallas kernels for 29%

profile of v5, /device:TPU:0, one launch (start us, length us, event | category | flops | bytes accessed | tf_op | source)
XLA Modules:
  0.0 713.4 jit_solution(3975228656132303798)
XLA Ops:
  7.2 7.9 %project.1 = (bf16[8,1024,128]{2,1,0:T(8,128)(2,1)}, bf16[8,256,128]{2,1,0:T(8,128)(2,1)}, bf16[8,256,128]{2,1,0:T(8,128)(2,1)}) custom-call(s32[1]{0:T(128)} %bitcast.side_ref, bf16[1024,1024]{1,0:T(8,128)(2,1)} %layer_in.1, bf16[3,1024,512]{2,1,0:T(8,128)(2,1)} %bitcast.46, bf16[3,1024,512]{2,1,0:T(8,128)(2,1)} %bitcast.47, ...), custom_call_target="tpu_custom_call" | custom-call | flops 3221225472 | bytes 11534336 | tf_op jit(solution)/shard_map/project/pallas_call | solution.py:395
  15.1 7.3 %all-to-all-start.2 = ((bf16[8,1024,128]{2,1,0:T(8,128)(2,1)}), bf16[8,1024,128]{2,1,0:T(8,128)(2,1)S(1)}, u32[]{:S(2)}, u32[]{:S(2)}) async-start(bf16[8,1024,128]{2,1,0:T(8,128)(2,1)} %get-tuple-element.113), calls=%async_computation.2 | async-start | bytes 4194304 | tf_op jit(solution)/shard_map/all_to_all | solution.py:733
  30.5 43.3 %collective-permute-done.refs_2_ = bf16[1024,1024]{1,0:T(8,128)(2,1)} collective-permute-done((bf16[1024,1024]{1,0:T(8,128)(2,1)S(1)}, bf16[1024,1024]{1,0:T(8,128)(2,1)}, u32[]{:S(2)}, u32[]{:S(2)}) %collective-permute-start) | collective-permute-done | bytes 2097184 | tf_op jit(solution)/shard_map/ppermute | solution.py:729
  75.3 20.4 %all_to_all.50.q_ref.refs_0_ = bf16[8,256,128]{2,1,0:T(8,128)(2,1)S(1)} all-to-all(bf16[8,256,128]{2,1,0:T(8,128)(2,1)S(1)} %copy-done.37), channel_id=1, replica_groups=mesh['z'=4,'y'=2,'core'=2,'head'=2] {'z','y'}, dimensions={0} | all-to-all | bytes 1048576 | tf_op jit(solution)/shard_map/all_to_all | solution.py:733
  99.9 27.4 %attend.2 = (bf16[8,256,128]{2,1,0:T(8,128)(2,1)S(1)}, f32[8,64,512]{2,1,0:T(8,128)S(1)}, f32[8,1,512]{2,1,0:T(1,128)S(1)}) custom-call(s32[32]{0:T(128)S(1)} %copy-done.23, s32[8]{0:T(128)S(1)} %copy-done.24, s32[2]{0:T(128)S(1)} %pad_add_fusion.1.place_ref, bf16[8,256,128]{2,1,0:T(8,128)(2,1)S(1)} %all_to_all.50.q_ref.refs_0_, ...), custom_call_target="tpu_custom_call" | custom-call | flops 671088640 | bytes 4194304 | tf_op jit(solution)/shard_map/attend/pallas_call | solution.py:556
  129.1 6.2 collective-permute-start.3
  135.5 32.2 %attend.3 = (bf16[8,256,128]{2,1,0:T(8,128)(2,1)S(1)}, f32[8,64,512]{2,1,0:T(8,128)S(1)}, f32[8,1,512]{2,1,0:T(1,128)S(1)}) custom-call(s32[32]{0:T(128)S(1)} %copy-done.23, s32[8]{0:T(128)S(1)} %copy-done.24, s32[2]{0:T(128)S(1)} %pad_add_fusion.place_ref, bf16[8,256,128]{2,1,0:T(8,128)(2,1)S(1)} %all-to-all-done.q_ref.refs_0_, ...), custom_call_target="tpu_custom_call" | custom-call | flops 671088640 | bytes 4194304 | tf_op jit(solution)/shard_map/attend/pallas_call | solution.py:556
  170.4 6.2 all-to-all-start.3
  179.3 23.3 %all-to-all-done.3.pack_ref = bf16[8,512,128]{2,1,0:T(8,128)(2,1)} async-done(((bf16[8,512,128]{2,1,0:T(8,128)(2,1)}), bf16[8,512,128]{2,1,0:T(8,128)(2,1)}, u32[]{:S(2)}, u32[]{:S(2)}) %all-to-all-start.3) | async-done | bytes 1048608 | tf_op jit(solution)/shard_map/all_to_all | solution.py:733
  202.6 27.9 %forward_rows.1 = (bf16[512,1024]{1,0:T(8,128)(2,1)}, bf16[512,1024]{1,0:T(8,128)(2,1)}, bf16[512,1024]{1,0:T(8,128)(2,1)}, bf16[512,4096]{1,0:T(8,128)(2,1)}, b...) custom-call(s32[1]{0:T(128)} %bitcast.side_ref, ...), custom_call_target="tpu_custom_call" | custom-call | flops 4294967296 | bytes 8388608 | tf_op jit(solution)/shard_map/forward_rows/pallas_call | solution.py:928
  230.6 6.3 convolution_convert_fusion
  236.8 7.5 %collective-permute-done.9 = bf16[2048,1024]{1,0:T(8,128)(2,1)} collective-permute-done((bf16[2048,1024]{1,0:T(8,128)(2,1)}, bf16[2048,1024]{1,0:T(8,128)(2,1)}, u32[]{:S(2)}, u32[]{:S(2)}) %collective-permute-start.9) | collective-permute-done | bytes 4194336 | tf_op jit(solution)/shard_map/ppermute | solution.py:729
  244.3 5.5 add_convert_fusion
  253.7 21.6 %backward_rows.1 = (bf16[512,4096]{1,0:T(8,128)(2,1)}, f32[512,1024]{1,0:T(8,128)}, bf16[512,1024]{1,0:T(8,128)(2,1)}, bf16[8,256,128]{2,1,0:T(8,128)(2,1)}, bf1...) custom-call(s32[2]{0:T(128)} %pad_add_fusion.2.place_ref, bf16[512,4096]{1,0:T(8,128)(2,1)} %get-tuple-element.139.slope_ref, ...), custom_call_target="tpu_custom_call" | custom-call | flops 4294967296 | bytes 8388608 | tf_op jit(solution)/shard_map/backward_rows/pallas_call | solution.py:928
  278.8 5.5 weight_grads.2
  284.3 16.2 %collective-permute-done.11 = bf16[1024,1024]{1,0:T(8,128)(2,1)} collective-permute-done((bf16[1024,1024]{1,0:T(8,128)(2,1)}, bf16[1024,1024]{1,0:T(8,128)(2,1)}, u32[]{:S(2)}, u32[]{:S(2)}) %collective-permute-start.11) | collective-permute-done | bytes 2097184 | tf_op jit(solution)/shard_map/ppermute | solution.py:729
  311.1 5.2 weight_grads.3
  329.0 55.8 %attend_back.2 = (bf16[8,256,128]{2,1,0:T(8,128)(2,1)S(1)}, f32[32,512,128]{2,1,0:T(8,128)S(1)}) custom-call(s32[32]{0:T(128)S(1)} %copy-done.23, s32[8]{0:T(128)S(1)} %copy-done.24, s32[2]{0:T(128)S(1)} %pad_add_fusion.place_ref, bf16[8,256,128]{2,1,0:T(8,128)(2,1)S(1)} %all-to-all-done.q_ref.refs_0_, bf16[8,256,128]{2,1,0:T(8,128)(2,1)} %all-to-all-done.4.refs_1_, ...), custom_call_target="tpu_custom_call" | custom-call | flops 671088640 | bytes 6291456 | tf_op jit(solution)/shard_map/attend_back/pallas_call | solution.py:704
  389.1 5.3 fusion
  398.1 6.0 all-to-all-start.6
  407.4 49.4 %attend_back.3 = (bf16[8,256,128]{2,1,0:T(8,128)(2,1)S(1)}, bf16[16,512,128]{2,1,0:T(8,128)(2,1)S(1)}, bf16[16,512,128]{2,1,0:T(8,128)(2,1)S(1)}) custom-call(s32[32]{0:T(128)S(1)} %copy-done.23, s32[8]{0:T(128)S(1)} %copy-done.24, s32[2]{0:T(128)S(1)} %pad_add_fusion.1.place_ref, bf16[8,256,128]{2,1,0:T(8,128)(2,1)S(1)} %all_to_all.50.q_ref.refs_0_, ...), custom_call_target="tpu_custom_call" | custom-call | flops 671088640 | bytes 6291456 | tf_op jit(solution)/shard_map/attend_back/pallas_call | solution.py:704
  468.5 9.8 %reduce-scatter.2.cloned.1.call-done = bf16[160,1024]{1,0:T(8,128)(2,1)} async-done(((bf16[1280,1024]{1,0:T(8,128)(2,1)}), bf16[160,1024]{1,0:T(8,128)(2,1)}) %reduce-scatter.2.cloned.1.call-update) | async-done | bytes 327696 | tf_op jit(solution)/shard_map/reduce_scatter | solution.py:1347
  489.3 4.4 copy.32
  495.3 57.0 %collective-permute-done.20 = bf16[128,1024]{1,0:T(8,128)(2,1)} collective-permute-done((bf16[128,1024]{1,0:T(8,128)(2,1)}, bf16[128,1024]{1,0:T(8,128)(2,1)}, u32[]{:S(2)}, u32[]{:S(2)}) %collective-permute-start.20) | collective-permute-done | bytes 262176 | tf_op jit(solution)/shard_map/ppermute | solution.py:1252
  556.6 9.5 %project_back.1 = (bf16[16,3,64,512]{3,2,1,0:T(8,128)(2,1)S(1)}, bf16[1024,512]{1,0:T(8,128)(2,1)S(1)}, f32[1024,512]{1,0:T(8,128)S(1)}, f32[2,512]{1,0:T(2,128)S(1)}) custom-call(s32[1]{0:T(128)} %bitcast.side_ref, bf16[8,256,128]{2,1,0:T(8,128)(2,1)S(1)} %all-to-all-done.6.near_ref, bf16[8,1280,128]{2,1,0:T(8,128)(2,1)S(1)} %all-to-all-done.7.kv_ref, ...), custom_call_target="tpu_custom_call" | custom-call | flops 1073741824 | bytes 8388608 | tf_op jit(solution)/shard_map/project_back/pallas_call | solution.py:1060
  579.5 29.0 %collective-permute-done.23 = bf16[4,3,64,512]{3,2,1,0:T(8,128)(2,1)} collective-permute-done((bf16[4,3,64,512]{3,2,1,0:T(8,128)(2,1)}, bf16[4,3,64,512]{3,2,1,0:T(8,128)(2,1)}, u32[]{:S(2)}, u32[]{:S(2)}) %collective-permute-start.23) | collective-permute-done | bytes 786464 | tf_op jit(solution)/shard_map/ppermute | solution.py:729
  627.8 14.9 %collective-permute-done.27 = bf16[256,1024]{1,0:T(8,128)(2,1)S(1)} collective-permute-done((bf16[256,1024]{1,0:T(8,128)(2,1)}, bf16[256,1024]{1,0:T(8,128)(2,1)S(1)}, u32[]{:S(2)}, u32[]{:S(2)}) %collective-permute-start.27) | collective-permute-done | bytes 524320 | tf_op jit(solution)/shard_map/ppermute | solution.py:1252
  645.5 4.8 all-to-all-start.9
  655.7 4.4 maximum_convert_fusion
  660.2 10.6 %all-to-all-done.9 = bf16[4,3,64,512]{3,2,1,0:T(8,128)(2,1)S(1)} async-done(((bf16[4,3,64,512]{3,2,1,0:T(8,128)(2,1)}), bf16[4,3,64,512]{3,2,1,0:T(8,128)(2,1)S(1)}, u32[]{:S(2)}, u32[]{:S(2)}) %all-to-all-start.9) | async-done | bytes 786464 | tf_op jit(solution)/shard_map/all_to_all | solution.py:1392
  680.7 8.8 %collective-permute-done.32 = bf16[4,3,64,512]{3,2,0,1:T(8,128)(2,1)S(1)} collective-permute-done((bf16[4,3,64,512]{3,2,0,1:T(8,128)(2,1)S(1)}, bf16[4,3,64,512]{3,2,0,1:T(8,128)(2,1)S(1)}, u32[]{:S(2)}, u32[]{:S(2)}) %collective-permute-start.32) | collective-permute-done | bytes 786464 | tf_op jit(solution)/shard_map/ppermute | solution.py:729
  697.1 4.5 maximum_convert_fusion.1
  (251 shorter events, 154.0 us)
Async XLA Ops:
  15.1 58.7 %all-to-all-start.2 = ((bf16[8,1024,128]{2,1,0:T(8,128)(2,1)}), bf16[8,1024,128]{2,1,0:T(8,128)(2,1)S(1)}, u32[]{:S(2)}, u32[]{:S(2)}) async-start(bf16[8,1024,128]{2,1,0:T(8,128)(2,1)} %get-tuple-element.113), calls=%async_computation.2 | async-start | bytes 4194304 | tf_op jit(solution)/shard_map/all_to_all | solution.py:733
  26.6 47.2 %collective-permute-start = (bf16[1024,1024]{1,0:T(8,128)(2,1)S(1)}, bf16[1024,1024]{1,0:T(8,128)(2,1)}, u32[]{:S(2)}, u32[]{:S(2)}) collective-permute-start(bf16[1024,1024]{1,0:T(8,128)(2,1)S(1)} %get-tuple-element.132.refs_0_), channel_id=1, source_target_pairs={{0,1},{1,0},{2,3},{3,2},{4,5},{5,4},{6,7},{7,6},{8,9},{9,8},{10,11... | collective-permute-start | bytes 6291464 | tf_op jit(solution)/shard_map/ppermute | solution.py:729
  73.8 26.1 %collective-permute-start.1 = (bf16[8,1024,128]{2,1,0:T(8,128)(2,1)S(1)}, bf16[8,1024,128]{2,1,0:T(8,128)(2,1)}, u32[]{:S(2)}, u32[]{:S(2)}) collective-permute-start(bf16[8,1024,128]{2,1,0:T(8,128)(2,1)S(1)} %all-to-all-done.2), channel_id=1, source_target_pairs={{0,2},{2,0},{1,3},{3,1},{4,6},{6,4},{5,7},{7,5},{8,10},{10,8},{9,1... | collective-permute-start | bytes 6291464 | tf_op jit(solution)/shard_map/ppermute | solution.py:729
  73.8 55.4 %collective-permute-start.2 = (bf16[1024,1024]{1,0:T(8,128)(2,1)}, bf16[1024,1024]{1,0:T(8,128)(2,1)}, u32[]{:S(2)}, u32[]{:S(2)}) collective-permute-start(bf16[1024,1024]{1,0:T(8,128)(2,1)} %get-tuple-element.120.refs_4_), channel_id=1, source_target_pairs={{0,1},{1,0},{2,3},{3,2},{4,5},{5,4},{6,7},{7,6},{8,9},{9,8},{10,11... | collective-permute-start | bytes 6291464 | tf_op jit(solution)/shard_map/ppermute | solution.py:729
  95.6 33.5 %all-to-all-start = ((bf16[8,256,128]{2,1,0:T(8,128)(2,1)}), bf16[8,256,128]{2,1,0:T(8,128)(2,1)S(1)}, u32[]{:S(2)}, u32[]{:S(2)}) async-start(bf16[8,256,128]{2,1,0:T(8,128)(2,1)} %get-tuple-element.110), calls=%async_computation | async-start | bytes 1048576 | tf_op jit(solution)/shard_map/all_to_all | solution.py:733
  99.3 69.4 %collective-permute-start.4 = (bf16[512,1024]{1,0:T(8,128)(2,1)}, bf16[512,1024]{1,0:T(8,128)(2,1)}, u32[]{:S(2)}, u32[]{:S(2)}) collective-permute-start(bf16[512,1024]{1,0:T(8,128)(2,1)} %refs_8_.1), channel_id=1, source_target_pairs={{0,1},{1,0},{2,3},{3,2},{4,5},{5,4},{6,7},{7,6},{8,9},{9,8},{10,11... | collective-permute-start | bytes 3145736 | tf_op jit(solution)/shard_map/ppermute | solution.py:729
  129.1 39.5 %collective-permute-start.3 = (bf16[8,256,128]{2,1,0:T(8,128)(2,1)}, bf16[8,256,128]{2,1,0:T(8,128)(2,1)S(1)}, u32[]{:S(2)}, u32[]{:S(2)}) collective-permute-start(bf16[8,256,128]{2,1,0:T(8,128)(2,1)} %copy-done.29), channel_id=1, source_target_pairs={{0,1},{1,0},{2,3},{3,2},{4,5},{5,4},{6,7},{7,6},{8,9},{9,8},{10,11... | collective-permute-start | bytes 1572872 | tf_op jit(solution)/shard_map/ppermute | solution.py:729
  135.5 33.2 %collective-permute-start.5 = (bf16[1024]{0:T(1024)(128)(2,1)S(1)}, bf16[1024]{0:T(1024)(128)(2,1)S(1)}, u32[]{:S(2)}, u32[]{:S(2)}) collective-permute-start(bf16[1024]{0:T(1024)(128)(2,1)S(1)} %get-tuple-element.127), channel_id=1, source_target_pairs={{0,1},{1,0},{2,3},{3,2},{4,5},{5,4},{6,7},{7,6},{8,9},{9,8},{10,11... | collective-permute-start | bytes 6152 | tf_op jit(solution)/shard_map/ppermute | solution.py:729
  168.7 33.9 %collective-permute-start.7 = (bf16[1024,1024]{1,0:T(8,128)(2,1)}, bf16[1024,1024]{1,0:T(8,128)(2,1)}, u32[]{:S(2)}, u32[]{:S(2)}) collective-permute-start(bf16[1024,1024]{1,0:T(8,128)(2,1)} %collective-permute-done.refs_2_), channel_id=1, source_target_pairs={{0,2},{2,0},{1,3},{3,1},{4,6},{6,4},{5,7},{7,5},{8,10},{10,8},{9,1... | collective-permute-start | bytes 6291464 | tf_op jit(solution)/shard_map/ppermute | solution.py:729
  168.8 33.8 %collective-permute-start.8 = (bf16[1024,1024]{1,0:T(8,128)(2,1)}, bf16[1024,1024]{1,0:T(8,128)(2,1)}, u32[]{:S(2)}, u32[]{:S(2)}) collective-permute-start(bf16[1024,1024]{1,0:T(8,128)(2,1)} %collective-permute-done.2.refs_6_), channel_id=1, source_target_pairs={{0,2},{2,0},{1,3},{3,1},{4,6},{6,4},{5,7},{7,5},{8,10},{10,8},{9,1... | collective-permute-start | bytes 6291464 | tf_op jit(solution)/shard_map/ppermute | solution.py:729
  170.4 32.3 %all-to-all-start.3 = ((bf16[8,512,128]{2,1,0:T(8,128)(2,1)}), bf16[8,512,128]{2,1,0:T(8,128)(2,1)}, u32[]{:S(2)}, u32[]{:S(2)}) async-start(bf16[8,512,128]{2,1,0:T(8,128)(2,1)} %pad_maximum_fusion.5), calls=%async_computation.3 | async-start | bytes 2097152 | tf_op jit(solution)/shard_map/all_to_all | solution.py:733
  252.5 48.0 %collective-permute-start.11 = (bf16[1024,1024]{1,0:T(8,128)(2,1)}, bf16[1024,1024]{1,0:T(8,128)(2,1)}, u32[]{:S(2)}, u32[]{:S(2)}) collective-permute-start(bf16[1024,1024]{1,0:T(8,128)(2,1)} %dynamic-slice_bitcast_fusion), channel_id=1, source_target_pairs={{0,1},{1,0},{2,3},{3,2},{4,5},{5,4},{6,7},{7,6},{8,9},{9,8},{10,11... | collective-permute-start | bytes 6291464 | tf_op jit(solution)/shard_map/ppermute | solution.py:729
  320.1 69.0 %collective-permute-start.14 = (bf16[1280,1024]{1,0:T(8,128)(2,1)}, bf16[1280,1024]{1,0:T(8,128)(2,1)}, u32[]{:S(2)}, u32[]{:S(2)}) collective-permute-start(bf16[1280,1024]{1,0:T(8,128)(2,1)} %slice_bitcast_fusion.1), channel_id=1, source_target_pairs={{0,1},{1,0},{2,3},{3,2},{4,5},{5,4},{6,7},{7,6},{8,9},{9,8},{10,11... | collective-permute-start | bytes 7864328 | tf_op jit(solution)/shard_map/ppermute | solution.py:729
  321.8 67.2 %collective-permute-start.13 = (bf16[512,1024]{1,0:T(8,128)(2,1)}, bf16[512,1024]{1,0:T(8,128)(2,1)}, u32[]{:S(2)}, u32[]{:S(2)}) collective-permute-start(bf16[512,1024]{1,0:T(8,128)(2,1)} %constant_dynamic-slice_fusion.4), channel_id=1, source_target_pairs={{0,4},{4,0},{1,5},{5,1},{2,6},{6,2},{3,7},{7,3},{8,12},{12,8},{9,1... | collective-permute-start | bytes 3145736 | tf_op jit(solution)/shard_map/ppermute | solution.py:729
  323.3 65.8 %all-to-all-start.5 = ((bf16[8,256,128]{2,1,0:T(8,128)(2,1)}), bf16[8,256,128]{2,1,0:T(8,128)(2,1)}, u32[]{:S(2)}, u32[]{:S(2)}) async-start(bf16[8,256,128]{2,1,0:T(8,128)(2,1)} %collective-permute-done.10), calls=%async_computation.5 | async-start | bytes 1048576 | tf_op jit(solution)/shard_map/all_to_all | solution.py:733
  327.7 150.6 %reduce-scatter.2.cloned.1.call-start = ((), (), s32[]{:S(2)}) async-start(), calls=%async_computation.11 | async-start | bytes 2949120 | tf_op jit(solution)/shard_map/reduce_scatter | solution.py:1347
  327.7 61.4 %collective-permute-start.15 = (f32[16,1024]{1,0:T(8,128)S(1)}, f32[16,1024]{1,0:T(8,128)S(1)}, u32[]{:S(2)}, u32[]{:S(2)}) collective-permute-start(f32[16,1024]{1,0:T(8,128)S(1)} %copy-done.38), channel_id=1, source_target_pairs={{0,2},{2,0},{1,3},{3,1},{4,6},{6,4},{5,7},{7,5},{8,10},{10,8},{9,1... | collective-permute-start | bytes 196616 | tf_op jit(solution)/shard_map/ppermute | solution.py:729
  398.1 62.1 %all-to-all-start.6 = ((bf16[8,256,128]{2,1,0:T(8,128)(2,1)}), bf16[8,256,128]{2,1,0:T(8,128)(2,1)S(1)}, u32[]{:S(2)}, u32[]{:S(2)}) async-start(bf16[8,256,128]{2,1,0:T(8,128)(2,1)} %copy-done.22), calls=%async_computation.6 | async-start | bytes 1048576 | tf_op jit(solution)/shard_map/all_to_all | solution.py:733
  404.1 56.1 %collective-permute-start.17 = (bf16[256,1024]{1,0:T(8,128)(2,1)}, bf16[256,1024]{1,0:T(8,128)(2,1)}, u32[]{:S(2)}, u32[]{:S(2)}) collective-permute-start(bf16[256,1024]{1,0:T(8,128)(2,1)} %constant_dynamic-slice_fusion.3), channel_id=1, source_target_pairs={{0,8},{8,0},{16,24},{24,16},{1,9},{9,1},{17,25},{25,17},{2,10},{10... | collective-permute-start | bytes 1572872 | tf_op jit(solution)/shard_map/ppermute | solution.py:1252
  406.1 54.1 %collective-permute-start.16 = (f32[16,1024]{1,0:T(8,128)S(1)}, f32[16,1024]{1,0:T(8,128)S(1)}, u32[]{:S(2)}, u32[]{:S(2)}) collective-permute-start(f32[16,1024]{1,0:T(8,128)S(1)} %add.123), channel_id=1, source_target_pairs={{0,1},{1,0},{2,3},{3,2},{4,5},{5,4},{6,7},{7,6},{8,9},{9,8},{10,11... | collective-permute-start | bytes 196616 | tf_op jit(solution)/shard_map/ppermute | solution.py:729
  478.3 75.1 %all-to-all-start.7 = ((bf16[8,1280,128]{2,1,0:T(8,128)(2,1)}), bf16[8,1280,128]{2,1,0:T(8,128)(2,1)S(1)}, u32[]{:S(2)}, u32[]{:S(2)}) async-start(bf16[8,1280,128]{2,1,0:T(8,128)(2,1)} %pad_maximum_fusion), calls=%async_computation.8 | async-start | bytes 5242880 | tf_op jit(solution)/shard_map/all_to_all | solution.py:733
  481.9 161.1 %all-gather.2.cloned.1.call-start = ((), (), s32[]{:S(2)}) async-start(), calls=%async_computation.12 | async-start | bytes 2949120 | tf_op jit(solution)/shard_map/all_gather | solution.py:1271
  482.0 71.4 %collective-permute-start.21 = (bf16[512,1024]{1,0:T(8,128)(2,1)}, bf16[512,1024]{1,0:T(8,128)(2,1)}, u32[]{:S(2)}, u32[]{:S(2)}) collective-permute-start(bf16[512,1024]{1,0:T(8,128)(2,1)} %get-tuple-element.138), channel_id=1, source_target_pairs={{0,1},{1,0},{2,3},{3,2},{4,5},{5,4},{6,7},{7,6},{8,9},{9,8},{10,11... | collective-permute-start | bytes 3145736 | tf_op jit(solution)/shard_map/ppermute | solution.py:729
  486.5 65.7 %collective-permute-start.20 = (bf16[128,1024]{1,0:T(8,128)(2,1)}, bf16[128,1024]{1,0:T(8,128)(2,1)}, u32[]{:S(2)}, u32[]{:S(2)}) collective-permute-start(bf16[128,1024]{1,0:T(8,128)(2,1)} %constant_dynamic-slice_fusion.2), channel_id=1, source_target_pairs={{0,16},{8,24},{16,0},{24,8},{1,17},{9,25},{17,1},{25,9},{2,18},{10... | collective-permute-start | bytes 786440 | tf_op jit(solution)/shard_map/ppermute | solution.py:1252
  493.7 59.6 %collective-permute-start.19 = (f32[16,1024]{1,0:T(8,128)S(1)}, f32[16,1024]{1,0:T(8,128)}, u32[]{:S(2)}, u32[]{:S(2)}) collective-permute-start(f32[16,1024]{1,0:T(8,128)S(1)} %add.129), channel_id=1, source_target_pairs={{0,8},{8,0},{16,24},{24,16},{1,9},{9,1},{17,25},{25,17},{2,10},{10... | collective-permute-start | bytes 196616 | tf_op jit(solution)/shard_map/ppermute | solution.py:1252
  575.7 32.8 %collective-permute-start.23 = (bf16[4,3,64,512]{3,2,1,0:T(8,128)(2,1)}, bf16[4,3,64,512]{3,2,1,0:T(8,128)(2,1)}, u32[]{:S(2)}, u32[]{:S(2)}) collective-permute-start(bf16[4,3,64,512]{3,2,1,0:T(8,128)(2,1)} %constant_dynamic-slice_fusion), channel_id=1, source_target_pairs={{0,4},{4,0},{1,5},{5,1},{2,6},{6,2},{3,7},{7,3},{8,12},{12,8},{9,1... | collective-permute-start | bytes 2359304 | tf_op jit(solution)/shard_map/ppermute | solution.py:729
  577.2 37.1 %collective-permute-start.26 = (bf16[128,1024]{1,0:T(8,128)(2,1)S(1)}, bf16[128,1024]{1,0:T(8,128)(2,1)S(1)}, u32[]{:S(2)}, u32[]{:S(2)}) collective-permute-start(bf16[128,1024]{1,0:T(8,128)(2,1)S(1)} %add_convert_fusion.6), channel_id=1, source_target_pairs={{0,16},{8,24},{16,0},{24,8},{1,17},{9,25},{17,1},{25,9},{2,18},{10... | collective-permute-start | bytes 786440 | tf_op jit(solution)/shard_map/ppermute | solution.py:1252
  577.2 65.8 %collective-permute-start.28 = (bf16[1024,512]{1,0:T(8,128)(2,1)S(1)}, bf16[1024,512]{1,0:T(8,128)(2,1)}, u32[]{:S(2)}, u32[]{:S(2)}) collective-permute-start(bf16[1024,512]{1,0:T(8,128)(2,1)S(1)} %copy-done.28), channel_id=1, source_target_pairs={{0,1},{1,0},{2,3},{3,2},{4,5},{5,4},{6,7},{7,6},{8,9},{9,8},{10,11... | collective-permute-start | bytes 3145736 | tf_op jit(solution)/shard_map/ppermute | solution.py:729
  610.8 32.3 %all-to-all-start.8 = ((bf16[4,3,64,512]{3,2,1,0:T(8,128)(2,1)}), bf16[4,3,64,512]{3,2,1,0:T(8,128)(2,1)S(1)}, u32[]{:S(2)}, u32[]{:S(2)}) async-start(bf16[4,3,64,512]{3,2,1,0:T(8,128)(2,1)} %add_convert_fusion.4), calls=%async_computation.9 | async-start | bytes 1572864 | tf_op jit(solution)/shard_map/all_to_all | solution.py:1380
  615.2 27.5 %collective-permute-start.27 = (bf16[256,1024]{1,0:T(8,128)(2,1)}, bf16[256,1024]{1,0:T(8,128)(2,1)S(1)}, u32[]{:S(2)}, u32[]{:S(2)}) collective-permute-start(bf16[256,1024]{1,0:T(8,128)(2,1)} %pad_maximum_fusion.7), channel_id=1, source_target_pairs={{0,8},{8,0},{16,24},{24,16},{1,9},{9,1},{17,25},{25,17},{2,10},{10... | collective-permute-start | bytes 1572872 | tf_op jit(solution)/shard_map/ppermute | solution.py:1252
  643.2 31.6 %collective-permute-start.36 = (bf16[512,1024]{1,0:T(8,128)(2,1)S(1)}, bf16[512,1024]{1,0:T(8,128)(2,1)}, u32[]{:S(2)}, u32[]{:S(2)}) collective-permute-start(bf16[512,1024]{1,0:T(8,128)(2,1)S(1)} %pad_maximum_fusion.6), channel_id=1, source_target_pairs={{0,4},{4,0},{1,5},{5,1},{2,6},{6,2},{3,7},{7,3},{8,12},{12,8},{9,1... | collective-permute-start | bytes 3145736 | tf_op jit(solution)/shard_map/ppermute | solution.py:729
  645.5 25.3 %all-to-all-start.9 = ((bf16[4,3,64,512]{3,2,1,0:T(8,128)(2,1)}), bf16[4,3,64,512]{3,2,1,0:T(8,128)(2,1)S(1)}, u32[]{:S(2)}, u32[]{:S(2)}) async-start(bf16[4,3,64,512]{3,2,1,0:T(8,128)(2,1)} %broadcast_in_dim.2), calls=%async_computation.10 | async-start | bytes 1572864 | tf_op jit(solution)/shard_map/all_to_all | solution.py:1392
  (64 other events, 591.4 us)
Sparse Core Ops, SparseCore 0:
  398.3 80.0 reduce-scatter.1
  553.5 68.4 all-gather.1
